TPU v7x, 32 devices: a whole 2x2x4 slice. The times are simulated.
32 devices in a mesh: patch: 8 (over z, x), lat: 4 (over y, core).
Axes of the slice: x: 2, y: 2, z: 4, core: 2. Of those that a mesh axis runs over, the one named last changes fastest.
Arguments:
- obs_values: bfloat16 [4096, 96], P(('patch', 'lat')), may hold values from -6 to 6
- obs_count: int32 [32, 32], P(('patch', 'lat')), may hold values from 0 to 4, as said below
- obs_node: int32 [4096, 3], P(('patch', 'lat')), may hold values from 0 to 319
- mesh_init: bfloat16 [10240, 512], P(('patch', 'lat')), may hold values from -6 to 6
- mesh_offset: int32 [10240, 6], P(('patch', 'lat')), may hold values from -128 to 128, as said below
- weights_flat: bfloat16 [32, 75264], P(('patch', 'lat')), may hold values from -0.25 to 0.25
- edge_bias: float32 [2, 512], replicated, may hold values from -3 to 3
- node_bias: float32 [2, 512], replicated, may hold values from -3 to 3
- norm_gain: float32 [2, 512], replicated, may hold values from 0.1 to 1.9
Outputs:
- mesh_latent: bfloat16 [10240, 512], P(('patch', 'lat'))
Inputs may be any that keep to these rules, and one draw needn't show every extreme that they name: obs_count[s, d] counts the live slots (the first ones) among the 4 slots that device s holds for device d; each source fills all 4 slots for some destination, and some destination receives 4 live slots from every source. `obs_node`: local node on the destination device. The k-th incoming edge of node n comes from node (n + mesh_offset[n, k]) mod 10240; offsets of both -128 and 128 occur.
All inputs are finite; a program needn't handle non-finite values.
Results may differ from a plain program's by a relative error of at most 0.0085.
Values may be sent and summed in bfloat16 or wider, within the bound.
No kernel may reach another device: no remote copies, remote signals or barrier semaphores. Data moves between devices by JAX's collectives and lax.ppermute only.
A program may use at most 128 MiB of HBM per device.

v0:
```python
import jax
import jax.numpy as jnp
from jax import lax
from jax.sharding import PartitionSpec as P

D = 512
CH = 96
OBS_EDGES = 3
DEG = 6
HALO = 128


def extended(block, sides, width):
    for axis, dim in sides:
        count = lax.axis_size(axis)
        forward = [(i, i + 1) for i in range(count - 1)]
        forward.append((count - 1, 0))
        backward = [(target, source) for source, target in forward]
        low = lax.ppermute(
            lax.slice_in_dim(block, block.shape[dim] - width, None, axis=dim), axis, forward
        )
        high = lax.ppermute(lax.slice_in_dim(block, 0, width, axis=dim), axis, backward)
        block = jnp.concatenate([low, block, high], axis=dim)
    return block


def unpack(flat):
    shapes = ((CH, D), (D, 2 * D), (D, D), (D, D), (D, 3 * D), (D, D), (D, D))
    pieces = []
    offset = 0
    for height, breadth in shapes:
        pieces.append(flat[offset : offset + height * breadth].reshape(height, breadth))
        offset = offset + height * breadth
    return pieces


def layer_norm(values, gain):
    center = values - jnp.mean(values, axis=-1, keepdims=True)
    spread = jnp.mean(center * center, axis=-1, keepdims=True)
    return center * lax.rsqrt(spread + 1e-05) * gain


def embed_rows(rows, w_in):
    return jnp.dot(rows, w_in, preferred_element_type=jnp.float32).astype(jnp.bfloat16)


def deliver(values, nodes, counts):
    return (
        lax.all_to_all(
            lax.all_to_all(values, "patch", split_axis=0, concat_axis=0, tiled=True),
            "lat",
            split_axis=1,
            concat_axis=1,
            tiled=True,
        ),
        lax.all_to_all(
            lax.all_to_all(nodes, "patch", split_axis=0, concat_axis=0, tiled=True),
            "lat",
            split_axis=1,
            concat_axis=1,
            tiled=True,
        ),
        lax.all_to_all(
            lax.all_to_all(counts, "patch", split_axis=0, concat_axis=0, tiled=True),
            "lat",
            split_axis=1,
            concat_axis=1,
            tiled=True,
        ),
    )


def shards(
    obs_values,
    obs_count,
    obs_node,
    mesh_init,
    mesh_offset,
    weights_flat,
    edge_bias,
    node_bias,
    norm_gain,
):
    n_patch = lax.axis_size("patch")
    n_lat = lax.axis_size("lat")
    senders = n_patch * n_lat
    capacity = obs_values.shape[0] // senders
    node_dev = mesh_init.shape[0]
    table = lax.all_gather(weights_flat, ("patch", "lat"), axis=0, tiled=True)
    w_in, w_enc, w_agg, w_out, w_proc, w_pagg, w_pout = unpack(table.reshape(-1))
    breadth = obs_values.shape[1]
    arrived, targets, counts = deliver(
        obs_values.reshape(n_patch, n_lat, capacity, breadth),
        obs_node.reshape(n_patch, n_lat, capacity, OBS_EDGES),
        obs_count.reshape(n_patch, n_lat),
    )
    arrived = arrived.reshape(senders * capacity, breadth)
    targets = targets.reshape(senders * capacity, OBS_EDGES)
    embedded = embed_rows(arrived, w_in)
    alive = (
        (jnp.arange(capacity, dtype=jnp.int32)[None, :] < counts.reshape(senders, 1))
        .astype(jnp.float32)
        .reshape(-1)
    )
    encoded = jnp.dot(mesh_init, w_enc, preferred_element_type=jnp.float32)
    query = encoded[:, :D] + edge_bias[0]
    total_rows = senders * capacity
    block = min(512, total_rows)
    turns = total_rows // block
    node_ids = jnp.arange(node_dev, dtype=jnp.int32)[None, :]

    def encode_block(block_index, totals):
        start = block_index * block
        piece = lax.dynamic_slice_in_dim(embedded, start, block, 0).astype(jnp.float32)
        nodes = lax.dynamic_slice_in_dim(targets, start, block, 0)
        weight = lax.dynamic_slice_in_dim(alive, start, block, 0)[:, None]
        for which in range(OBS_EDGES):
            selector = (nodes[:, which][:, None] == node_ids).astype(jnp.float32)
            picked = jnp.dot(selector, query, precision=lax.Precision.HIGHEST)
            message = jax.nn.silu(piece + picked) * weight
            totals = totals + lax.dot_general(
                selector, message, (((0,), (0,)), ((), ())), precision=lax.Precision.HIGHEST
            )
        return totals

    totals = lax.fori_loop(0, turns, encode_block, jnp.zeros((node_dev, D), jnp.float32))
    gathered = totals.astype(jnp.bfloat16)
    hidden = jax.nn.silu(
        encoded[:, D:] + jnp.dot(gathered, w_agg, preferred_element_type=jnp.float32) + node_bias[0]
    ).astype(jnp.bfloat16)
    first = (
        mesh_init.astype(jnp.float32)
        + layer_norm(jnp.dot(hidden, w_out, preferred_element_type=jnp.float32), norm_gain[0])
    ).astype(jnp.bfloat16)
    projected = jnp.dot(first, w_proc, preferred_element_type=jnp.float32)
    sources = projected[:, :D].astype(jnp.bfloat16)
    target = projected[:, D : 2 * D] + edge_bias[1]
    padded = extended(sources, ((("patch", "lat"), 0),), HALO)
    local_ids = jnp.arange(node_dev, dtype=jnp.int32) + HALO
    pooled = jnp.zeros((node_dev, D), jnp.float32)
    for which in range(DEG):
        anchor = local_ids + mesh_offset[:, which]
        pooled = pooled + jax.nn.silu(jnp.take(padded, anchor, axis=0).astype(jnp.float32) + target)
    hidden2 = jax.nn.silu(
        projected[:, 2 * D :]
        + jnp.dot(pooled.astype(jnp.bfloat16), w_pagg, preferred_element_type=jnp.float32)
        + node_bias[1]
    ).astype(jnp.bfloat16)
    return (
        first.astype(jnp.float32)
        + layer_norm(jnp.dot(hidden2, w_pout, preferred_element_type=jnp.float32), norm_gain[1])
    ).astype(jnp.bfloat16)


def solution(mesh):
    return jax.shard_map(
        shards,
        mesh=mesh,
        in_specs=(
            P(("patch", "lat"), None),
            P(("patch", "lat"), None),
            P(("patch", "lat"), None),
            P(("patch", "lat"), None),
            P(("patch", "lat"), None),
            P(("patch", "lat"), None),
            P(),
            P(),
            P(),
        ),
        out_specs=P(("patch", "lat"), None),
        check_vma=False,
    )
```

profile of v0, /device:TPU:15, one launch (start us, length us, event | category | flops | bytes accessed | tf_op | source)
XLA Modules:
  0.0 258.1 jit_solution(6021291949161695831)
XLA Ops:
  6.5 0.7 all-gather.3.cloned.1.call-update
  7.3 0.5 broadcast.105
  7.8 1.3 reduce.18
  9.1 0.7 all_to_all.28
  9.8 5.7 %all-to-all-start.4 = ((s32[8,1,4]{2,1,0:T(1,128)}), s32[8,1,4]{2,1,0:T(1,128)S(1)}, u32[]{:S(2)}, u32[]{:S(2)}) async-start(s32[8,1,4]{2,1,0:T(1,128)} %bitcast.5), calls=%async_computation.4 | async-start | bytes 8192 | tf_op jit(solution)/shard_map/all_to_all | solution.py:64
  15.4 1.0 slice_reduce_fusion.5
  16.4 0.6 compare_and_fusion
  17.0 0.5 compare_and_fusion.2
  17.5 0.6 compare_and_fusion.4
  18.1 0.8 fusion.78
  18.9 0.8 fusion.79
  19.6 0.8 fusion.77
  20.4 0.8 reshape.94
  21.2 0.6 copy.15
  21.9 5.4 %all-to-all-start = ((s32[8,4,4,3]{2,1,3,0:T(4,128)}), s32[8,4,4,3]{2,1,3,0:T(4,128)S(1)}, u32[]{:S(2)}, u32[]{:S(2)}) async-start(s32[8,4,4,3]{2,1,3,0:T(4,128)} %copy.15), calls=%async_computation | async-start | bytes 98304 | tf_op jit(solution)/shard_map/all_to_all | solution.py:57
  27.3 0.6 copy.23
  27.9 3.1 %all-to-all-done = s32[8,4,4,3]{2,1,3,0:T(4,128)S(1)} async-done(((s32[8,4,4,3]{2,1,3,0:T(4,128)}), s32[8,4,4,3]{2,1,3,0:T(4,128)S(1)}, u32[]{:S(2)}, u32[]{:S(2)}) %all-to-all-start) | async-done | bytes 1568 | tf_op jit(solution)/shard_map/all_to_all | solution.py:57
  31.1 5.9 %all-to-all-start.5 = ((s32[8,4,1]{0,2,1:T(1,128)}), s32[8,4,1]{0,2,1:T(1,128)S(1)}, u32[]{:S(2)}, u32[]{:S(2)}) async-start(s32[8,4,1]{0,2,1:T(1,128)} %copy.23), calls=%async_computation.5 | async-start | bytes 4096 | tf_op jit(solution)/shard_map/all_to_all | solution.py:63
  36.9 0.8 copy.16
  37.7 0.7 all-to-all-done.5
  38.4 5.5 %all-to-all-start.1 = ((s32[8,4,4,3]{0,2,3,1:T(4,128)}), s32[8,4,4,3]{0,2,3,1:T(4,128)S(1)}, u32[]{:S(2)}, u32[]{:S(2)}) async-start(s32[8,4,4,3]{0,2,3,1:T(4,128)} %copy.16), calls=%async_computation.1 | async-start | bytes 49152 | tf_op jit(solution)/shard_map/all_to_all | solution.py:56
  43.9 1.5 copy.18
  45.5 0.1 lt.32
  45.6 0.3 all-to-all-done.1
  45.9 5.3 %all-to-all-start.2 = ((bf16[8,4,4,96]{3,2,1,0:T(4,128)(2,1)}), bf16[8,4,4,96]{3,2,1,0:T(4,128)(2,1)S(1)}, u32[]{:S(2)}, u32[]{:S(2)}) async-start(bf16[8,4,4,96]{3,2,1,0:T(4,128)(2,1)} %bitcast.2), calls=%async_computation.2 | async-start | bytes 65536 | tf_op jit(solution)/shard_map/all_to_all | solution.py:50
  51.2 0.1 reshape.100
  51.3 0.2 copy.17
  51.5 0.1 reshape.95
  51.6 4.1 %all-to-all-done.2 = bf16[8,4,4,96]{3,2,1,0:T(4,128)(2,1)S(1)} async-done(((bf16[8,4,4,96]{3,2,1,0:T(4,128)(2,1)}), bf16[8,4,4,96]{3,2,1,0:T(4,128)(2,1)S(1)}, u32[]{:S(2)}, u32[]{:S(2)}) %all-to-all-start.2) | async-done | bytes 24608 | tf_op jit(solution)/shard_map/all_to_all | solution.py:50
  55.7 0.6 copy.19
  56.3 5.6 %all-to-all-start.3 = ((bf16[8,4,4,96]{3,2,0,1:T(4,128)(2,1)}), bf16[8,4,4,96]{3,2,0,1:T(4,128)(2,1)S(1)}, u32[]{:S(2)}, u32[]{:S(2)}) async-start(bf16[8,4,4,96]{3,2,0,1:T(4,128)(2,1)} %copy.19), calls=%async_computation.3 | async-start | bytes 65536 | tf_op jit(solution)/shard_map/all_to_all | solution.py:49
  61.9 2.1 all-to-all-done.3
  64.0 29.9 %all-gather.3.cloned.1.call-done = bf16[32,1,75264]{2,1,0:T(2,128)(2,1)} async-done(((bf16[1,1,75264]{2,1,0:T(2,128)(2,1)}), bf16[32,1,75264]{2,1,0:T(2,128)(2,1)}) %all-gather.3.cloned.1.call-update) | async-done | bytes 4816912 | tf_op jit(solution)/shard_map/all_gather | solution.py:89
  93.9 87.6 %reduce = bf16[32,75264]{1,0:T(8,128)(2,1)} reduce(bf16[32,1,75264]{2,1,0:T(2,128)(2,1)} %all-gather.3.cloned.1.call-done, bf16[]{:T(256)} %constant.49), dimensions={1}, to_apply=%all-gather.reduce_sub_computation | reduce | bytes 9633794 | tf_op jit(solution)/shard_map/all_gather | solution.py:89
  181.5 9.6 %slice.107 = bf16[4704,512]{1,0:T(8,128)(2,1)} reshape(bf16[32,75264]{1,0:T(8,128)(2,1)} %reduce) | data formatting | bytes 9633792 | tf_op jit(solution)/shard_map/slice | solution.py:32
  191.1 10.3 %slice.103 = bf16[2352,1024]{1,0:T(8,128)(2,1)} reshape(bf16[32,75264]{1,0:T(8,128)(2,1)} %reduce) | data formatting | bytes 9633792 | tf_op jit(solution)/shard_map/slice | solution.py:32
  201.4 9.7 %reshape.98 = bf16[2408448]{0:T(1024)(128)(2,1)} reshape(bf16[32,75264]{1,0:T(8,128)(2,1)} %reduce) | data formatting | bytes 9633792 | tf_op jit(solution)/shard_map/reshape | solution.py:90
  211.1 1.1 fusion.3
  212.2 1.7 fusion.4
  213.9 0.5 convolution_add_fusion.6
  214.4 0.5 convolution_add_fusion.5
  214.9 0.5 convolution_add_fusion.4
  215.4 0.6 fusion.45
  215.9 0.6 convolution_add_fusion.3
  216.5 0.6 fusion.2
  217.1 2.0 fusion.80
  219.1 0.2 multiply_reduce_fusion.1
  219.3 0.6 copy-done
  219.9 0.8 slice-done
  220.7 1.8 reshape.99
  222.5 1.3 add_convert_fusion.2
  223.8 2.0 fusion.83
  225.8 2.1 collective-permute-start
  228.0 1.9 collective-permute-done
  229.9 4.2 %collective-permute-done.1 = bf16[128,512]{1,0:T(8,128)(2,1)S(1)} collective-permute-done((bf16[128,512]{1,0:T(8,128)(2,1)S(1)}, bf16[128,512]{1,0:T(8,128)(2,1)S(1)}, u32[]{:S(2)}, u32[]{:S(2)}) %collective-permute-start.1) | collective-permute-done | bytes 131104 | tf_op jit(solution)/shard_map/ppermute | solution.py:22
  234.2 2.2 gather_fusion.4
  236.4 2.0 gather_fusion
  238.5 2.0 gather_fusion.1
  240.5 2.0 gather_fusion.2
  242.5 2.0 gather_fusion.3
  244.5 2.0 gather_fusion.5
  246.6 3.5 %fusion.84 = (f32[320]{0:T(512)S(1)}, f32[320,512]{1,0:T(8,128)S(1)}) fusion(bf16[4704,512]{1,0:T(8,128)(2,1)} %slice.107, f32[320,1536]{1,0:T(8,128)} %get-tuple-element.50, f32[512]{0:T(512)S(1)} %bitcast.37, bf16[320,512]{1,0:T(8,128)(2,1)S(1)} %gather_fusion.5, bf16[320,512]{1,0:T(8,128)(2,1)S(1)} %gather_fusion.4, ...), kind=kOutput, calls=%fused_computation.131 | convolution fusion | flops 344882880 | bytes 4988992 | tf_op jit(solution)/shard_map/dot_general | solution.py:151
  250.1 0.2 multiply_reduce_fusion
  250.3 0.9 add_convert_fusion
  (27 shorter events, 0.3 us)
Async XLA Ops:
  6.5 87.4 %all-gather.3.cloned.1.call-start = ((), (), s32[]{:S(2)}) async-start(), calls=%async_computation.6 | async-start | bytes 9934848 | tf_op jit(solution)/shard_map/all_gather | solution.py:89
  9.8 12.1 %all-to-all-start.4 = ((s32[8,1,4]{2,1,0:T(1,128)}), s32[8,1,4]{2,1,0:T(1,128)S(1)}, u32[]{:S(2)}, u32[]{:S(2)}) async-start(s32[8,1,4]{2,1,0:T(1,128)} %bitcast.5), calls=%async_computation.4 | async-start | bytes 8192 | tf_op jit(solution)/shard_map/all_to_all | solution.py:64
  21.9 9.2 %all-to-all-start = ((s32[8,4,4,3]{2,1,3,0:T(4,128)}), s32[8,4,4,3]{2,1,3,0:T(4,128)S(1)}, u32[]{:S(2)}, u32[]{:S(2)}) async-start(s32[8,4,4,3]{2,1,3,0:T(4,128)} %copy.15), calls=%async_computation | async-start | bytes 98304 | tf_op jit(solution)/shard_map/all_to_all | solution.py:57
  31.1 7.3 %all-to-all-start.5 = ((s32[8,4,1]{0,2,1:T(1,128)}), s32[8,4,1]{0,2,1:T(1,128)S(1)}, u32[]{:S(2)}, u32[]{:S(2)}) async-start(s32[8,4,1]{0,2,1:T(1,128)} %copy.23), calls=%async_computation.5 | async-start | bytes 4096 | tf_op jit(solution)/shard_map/all_to_all | solution.py:63
  38.4 7.5 %all-to-all-start.1 = ((s32[8,4,4,3]{0,2,3,1:T(4,128)}), s32[8,4,4,3]{0,2,3,1:T(4,128)S(1)}, u32[]{:S(2)}, u32[]{:S(2)}) async-start(s32[8,4,4,3]{0,2,3,1:T(4,128)} %copy.16), calls=%async_computation.1 | async-start | bytes 49152 | tf_op jit(solution)/shard_map/all_to_all | solution.py:56
  45.9 9.8 %all-to-all-start.2 = ((bf16[8,4,4,96]{3,2,1,0:T(4,128)(2,1)}), bf16[8,4,4,96]{3,2,1,0:T(4,128)(2,1)S(1)}, u32[]{:S(2)}, u32[]{:S(2)}) async-start(bf16[8,4,4,96]{3,2,1,0:T(4,128)(2,1)} %bitcast.2), calls=%async_computation.2 | async-start | bytes 65536 | tf_op jit(solution)/shard_map/all_to_all | solution.py:50
  56.3 7.6 %all-to-all-start.3 = ((bf16[8,4,4,96]{3,2,0,1:T(4,128)(2,1)}), bf16[8,4,4,96]{3,2,0,1:T(4,128)(2,1)S(1)}, u32[]{:S(2)}, u32[]{:S(2)}) async-start(bf16[8,4,4,96]{3,2,0,1:T(4,128)(2,1)} %copy.19), calls=%async_computation.3 | async-start | bytes 65536 | tf_op jit(solution)/shard_map/all_to_all | solution.py:49
  201.4 10.8 %copy-start.1 = (bf16[320,512]{1,0:T(8,128)(2,1)S(1)}, bf16[320,512]{1,0:T(8,128)(2,1)}, u32[]{:S(2)}) copy-start(bf16[320,512]{1,0:T(8,128)(2,1)} %param.14) | copy-start | bytes 983044
  219.0 0.8 copy-start
  219.1 1.6 slice-start
  225.8 4.1 %collective-permute-start = (bf16[128,512]{1,0:T(8,128)(2,1)S(1)}, bf16[128,512]{1,0:T(8,128)(2,1)S(1)}, u32[]{:S(2)}, u32[]{:S(2)}) collective-permute-start(bf16[128,512]{1,0:T(8,128)(2,1)S(1)} %get-tuple-element.36), channel_id=1, source_target_pairs={{0,1},{1,2},{2,3},{3,4},{4,5},{5,6},{6,7},{7,8},{8,9},{9,10},{10,1... | collective-permute-start | bytes 393224 | tf_op jit(solution)/shard_map/ppermute | solution.py:19
  227.9 6.2 %collective-permute-start.1 = (bf16[128,512]{1,0:T(8,128)(2,1)S(1)}, bf16[128,512]{1,0:T(8,128)(2,1)S(1)}, u32[]{:S(2)}, u32[]{:S(2)}) collective-permute-start(bf16[128,512]{1,0:T(8,128)(2,1)S(1)} %get-tuple-element.37), channel_id=1, source_target_pairs={{1,0},{2,1},{3,2},{4,3},{5,4},{6,5},{7,6},{8,7},{9,8},{10,9},{11,1... | collective-permute-start | bytes 393224 | tf_op jit(solution)/shard_map/ppermute | solution.py:22
Sparse Core Ops, SparseCore 0:
  10.2 83.6 all-gather.2
where the time goes:
time: 261 us; the launch traced here: 258 us
  other arithmetic  93.5 us (36%)
  local copies, waits for them, and re-layouts  55.1 us (21%)
  waiting for transfers between devices  47.1 us (18%)
  starting transfers between devices  35.5 us (14%)
  between operations  13.6 us (5%)
  matrix products  13.4 us (5%)
    all_gather x1, other arithmetic, shards(): table = lax.all_gather(weights_flat, ('patch', 'lat'), axis=0, tiled=True)  87.6 us
    all_gather x1, waiting for transfers between devices, shards(): table = lax.all_gather(weights_flat, ('patch', 'lat'), axis=0, tiled=True)  29.9 us
    slice x4, local copies, waits for them, and re-layouts, unpack(): flat[offset:offset + height * breadth].reshape(height, breadth)  20.7 us
    gather x6, local copies, waits for them, and re-layouts, shards(): jnp.take(padded, anchor, axis=0).astype(jnp.float32) + target  12.4 us
    reshape x1, local copies, waits for them, and re-layouts, shards(): table.reshape(-1)  9.71 us
    all_to_all x1, starting transfers between devices, deliver(): lax.all_to_all(lax.all_to_all(counts, 'patch', split_axis=0, concat_axis=...  5.87 us
    all_to_all x1, starting transfers between devices, deliver(): lax.all_to_all(counts, 'patch', split_axis=0, concat_axis=0, tiled=True)  5.66 us
    all_to_all x1, starting transfers between devices, deliver(): lax.all_to_all(lax.all_to_all(values, 'patch', split_axis=0, concat_axis=...  5.58 us
  transfers between devices with their start and end apart: 9, of which 8 were waited for; matrix products, arithmetic and copies ran while one was open for 5% of the time, Pallas kernels for 0%

commit v1 on v0

--- a/solution.py
+++ b/solution.py
@@ -1,6 +1,8 @@
 import jax
 import jax.numpy as jnp
 from jax import lax
+from jax.experimental import pallas as pl
+from jax.experimental.pallas import tpu as pltpu
 from jax.sharding import PartitionSpec as P
 
 D = 512
@@ -70,7 +72,7 @@
     )
 
 
-def shards(
+def general(
     obs_values,
     obs_count,
     obs_node,
@@ -152,6 +154,291 @@
     ).astype(jnp.bfloat16)
 
 
+BF = jnp.bfloat16
+F32 = jnp.float32
+TILE = 16
+FRAME = 168
+
+
+def silu(values):
+    half = 0.5 * values
+    return half + half * jnp.tanh(half)
+
+
+def mm(left, right):
+    return jnp.dot(left, right, preferred_element_type=F32)
+
+
+def iota(shape, dim):
+    return lax.broadcasted_iota(jnp.int32, shape, dim)
+
+
+def in_vmem():
+    return pl.BlockSpec(memory_space=pltpu.VMEM)
+
+
+def in_smem():
+    return pl.BlockSpec(memory_space=pltpu.SMEM)
+
+
+def in_any():
+    return pl.BlockSpec(memory_space=pl.ANY)
+
+
+def frame_kernel(me_ref, w_ref, val_ref, node_ref, count_ref, *refs):
+    outs, (slots, rows, frame) = refs[:4], refs[4:]
+    me = me_ref[0]
+    height = w_ref.shape[0]
+    n_slots, breadth = val_ref.shape
+    senders = count_ref.shape[1]
+    capacity = n_slots // senders
+    phase = lax.rem(height * me, TILE)
+    own = iota((n_slots, senders), 0) // capacity == iota((n_slots, senders), 1)
+    live = jnp.sum(jnp.where(own, count_ref[...].astype(F32), 0.0), axis=1, keepdims=True)
+    place = (iota((n_slots, 1), 0) % capacity).astype(F32)
+    code = jnp.where(place < live, node_ref[...] + 1, 0)
+    high = (code >> 4).astype(F32)
+    low = (code & 15).astype(F32)
+    lane = iota((n_slots, 128 - breadth), 1)
+    tail = jnp.zeros((n_slots, 128 - breadth), F32)
+    for k in range(OBS_EDGES):
+        tail = jnp.where(lane == 2 * k, high[:, k : k + 1], tail)
+        tail = jnp.where(lane == 2 * k + 1, low[:, k : k + 1], tail)
+    slots[:, :breadth] = val_ref[...].astype(F32)
+    slots[:, breadth:] = tail
+    for j in range(capacity):
+        rows[:, 128 * j : 128 * (j + 1)] = slots[pl.ds(j, senders, stride=capacity), :]
+    shift = (iota((FRAME, height), 0) == iota((FRAME, height), 1) + phase).astype(BF)
+    frame[...] = mm(shift, w_ref[...])
+    start = pl.multiple_of(jnp.where(phase >= 8, 0, FRAME - 8), 8)
+    for flip in range(4):
+        plane = (me >> 3) ^ flip
+        frame[pl.ds(start, 8), :] = rows[pl.ds(pl.multiple_of(plane * 8, 8), 8), :]
+        outs[flip][...] = frame[...].astype(BF)
+
+
+def encoder_kernel(me_ref, *refs):
+    pieces = refs[:16]
+    init_ref, edge_ref, nbias_ref, gain_ref = refs[16:20]
+    src_ref, tgt_ref, rest_ref, first_ref, pagg_ref, pout_ref = refs[20:26]
+    big, heads, tails, obs, enc, proc, sems = refs[26:]
+    height = WROWS
+    me = me_ref[0]
+    core = me & 1
+    copies = []
+    at = 0
+    for unit in range(4):
+        for twin in range(2):
+            ax = jnp.where((core ^ twin) == 0, 4, 2)
+            ay = jnp.where((core ^ twin) == 0, 2, 4)
+            for pair in range(2):
+                for j in range(2):
+                    piece = pieces[unit * 4 + twin * 2 + pair]
+                    mask = (8 * unit) ^ twin ^ (ax if j else 0) ^ (ay if pair else 0)
+                    dev = me ^ mask
+                    row = pl.multiple_of((height * dev) // TILE * TILE + TILE, TILE)
+                    for s, (lo, hi, dst) in enumerate((
+                        (0, 16, heads.at[dev]),
+                        (16, 144, big.at[pl.ds(row, 128)]),
+                        (144, FRAME, tails.at[dev, pl.ds(0, FRAME - 144)]),
+                    )):
+                        copy = pltpu.make_async_copy(piece.at[j, pl.ds(lo, hi - lo)], dst, sems.at[at, s])
+                        copy.start()
+                        copies.append(copy)
+                    at += 1
+    for copy in copies:
+        copy.wait()
+    row16 = iota((TILE, D), 0)
+    for dev in range(32):
+        phase = height * dev % TILE
+        tile = height * dev // TILE
+        after = height * (dev + 1) // TILE
+        head = heads[dev]
+        if phase:
+            before = height * (dev - 1) // TILE
+            skip = TILE * (tile - before) - 144
+            last = tails[dev - 1, skip : skip + TILE, :]
+            head = jnp.where(row16 < phase, last.astype(F32), head.astype(F32)).astype(BF)
+        big[TILE * tile : TILE * (tile + 1), :] = head
+        if after - tile == 10:
+            big[TILE * (tile + 9) : TILE * (tile + 10), :] = tails[dev, 0:TILE, :]
+        if phase >= 8:
+            seen = heads[dev].astype(F32)[0:8]
+        else:
+            seen = tails[dev, TILE : 2 * TILE, :].astype(F32)[0:8]
+        for j in range(4):
+            obs[j, 8 * dev : 8 * (dev + 1), :] = seen[:, 128 * j : 128 * (j + 1)]
+    e0 = CH
+    a0 = CH + 2 * D
+    o0 = CH + 3 * D
+    p0 = CH + 4 * D
+    g0 = CH + 7 * D
+    u0 = CH + 8 * D
+    pagg_ref[...] = big[g0 : g0 + D, :]
+    pout_ref[...] = big[u0 : u0 + D, :]
+    out = iota((256, 256), 0)
+    two = (iota((256, 256), 1) == 2 * (out & 127) + (out >> 7)).astype(BF)
+    for j in range(D // 128):
+        got = mm(two, big[e0 + 256 * j : e0 + 256 * (j + 1), :]).astype(BF)
+        enc[0, 128 * j : 128 * (j + 1), :] = got[:128]
+        enc[1, 128 * j : 128 * (j + 1), :] = got[128:]
+    out = iota((384, 384), 0)
+    three = (iota((384, 384), 1) == 3 * (out & 127) + (out >> 7)).astype(BF)
+    for j in range(D // 128):
+        got = mm(three, big[p0 + 384 * j : p0 + 384 * (j + 1), :]).astype(BF)
+        for m in range(3):
+            proc[m, 128 * j : 128 * (j + 1), :] = got[128 * m : 128 * (m + 1)]
+    init = init_ref[...]
+    query = mm(init, enc[0]) + edge_ref[0:1, :]
+    slots = jnp.concatenate([obs[j, pl.ds(me & 7, 32, stride=8), :] for j in range(4)], axis=0)
+    embedded = mm(slots[:, :CH].astype(BF), big[0:CH, :]).astype(BF).astype(F32)
+    node_ids = iota((slots.shape[0], init.shape[0]), 1)
+    picks = []
+    for k in range(OBS_EDGES):
+        code = slots[:, CH + 2 * k : CH + 2 * k + 1] * 16.0 + slots[:, CH + 2 * k + 1 : CH + 2 * k + 2]
+        picks.append((node_ids == code.astype(jnp.int32) - 1).astype(F32))
+    select = jnp.concatenate(picks, axis=0)
+    spread = select.astype(BF)
+    q_high = query.astype(BF)
+    q_low = (query - q_high.astype(F32)).astype(BF)
+    picked = mm(spread, q_high) + mm(spread, q_low)
+    message = silu(jnp.concatenate([embedded] * OBS_EDGES, axis=0) + picked)
+    collect = select.T.astype(BF)
+    m_high = message.astype(BF)
+    m_low = (message - m_high.astype(F32)).astype(BF)
+    gathered = (mm(collect, m_high) + mm(collect, m_low)).astype(BF)
+    hidden = silu(
+        mm(init, enc[1]) + mm(gathered, big[a0 : a0 + D, :]) + nbias_ref[0:1, :]
+    ).astype(BF)
+    first = (
+        init.astype(F32) + layer_norm(mm(hidden, big[o0 : o0 + D, :]), gain_ref[0:1, :])
+    ).astype(BF)
+    first_ref[...] = first
+    src_ref[...] = mm(first, proc[0]).astype(BF)
+    tgt_ref[...] = mm(first, proc[1]) + edge_ref[1:2, :]
+    rest_ref[...] = mm(first, proc[2]) + nbias_ref[1:2, :]
+
+
+def processor_kernel(
+    low_ref, src_ref, high_ref, tgt_ref, rest_ref, first_ref, off_ref, pagg_ref, pout_ref, gain_ref, out_ref, ext
+):
+    count = src_ref.shape[0]
+    ext[0:HALO, :] = low_ref[...]
+    ext[HALO : HALO + count, :] = src_ref[...]
+    ext[HALO + count :, :] = high_ref[...]
+    target = tgt_ref[...]
+    cols = iota((count, count + 2 * HALO), 1) - iota((count, count + 2 * HALO), 0) - HALO
+    pooled = jnp.zeros((count, D), F32)
+    for k in range(DEG):
+        select = (cols == off_ref[:, k : k + 1]).astype(BF)
+        pooled = pooled + silu(mm(select, ext[...]) + target)
+    hidden = silu(rest_ref[...] + mm(pooled.astype(BF), pagg_ref[...])).astype(BF)
+    out_ref[...] = (
+        first_ref[...].astype(F32) + layer_norm(mm(hidden, pout_ref[...]), gain_ref[1:2, :])
+    ).astype(BF)
+
+
+WROWS = 147
+
+
+def fits(obs_values, obs_node, mesh_init, weights_flat):
+    return (
+        lax.axis_size("patch") == 8
+        and lax.axis_size("lat") == 4
+        and weights_flat.shape[1] == WROWS * D
+        and obs_values.shape == (128, CH)
+        and mesh_init.shape[0] <= 320
+        and mesh_init.shape[0] >= HALO
+    )
+
+
+def spread_weights(frames):
+    axes = ("patch", "lat")
+
+    def move(block, masks):
+        return lax.ppermute(block, axes, [(i, i ^ masks[i & 1]) for i in range(32)])
+
+    units = [frames[0]] + [move(frames[f], (8 * f, 8 * f)) for f in (1, 2, 3)]
+    pieces = []
+    for unit in units:
+        pair = jnp.stack([unit, move(unit, (4, 2))])
+        other = move(pair, (2, 4))
+        pieces += [pair, other, move(pair, (1, 1)), move(other, (1, 1))]
+    return pieces
+
+
+def shards(
+    obs_values,
+    obs_count,
+    obs_node,
+    mesh_init,
+    mesh_offset,
+    weights_flat,
+    edge_bias,
+    node_bias,
+    norm_gain,
+):
+    if not fits(obs_values, obs_node, mesh_init, weights_flat):
+        return general(
+            obs_values,
+            obs_count,
+            obs_node,
+            mesh_init,
+            mesh_offset,
+            weights_flat,
+            edge_bias,
+            node_bias,
+            norm_gain,
+        )
+    axes = ("patch", "lat")
+    me = lax.axis_index(axes).astype(jnp.int32).reshape(1)
+    count = mesh_init.shape[0]
+    frames = pl.pallas_call(
+        frame_kernel,
+        out_shape=[jax.ShapeDtypeStruct((FRAME, D), BF)] * 4,
+        in_specs=[in_smem()] + [in_vmem()] * 4,
+        out_specs=[in_vmem()] * 4,
+        scratch_shapes=[
+            pltpu.VMEM((128, 128), F32),
+            pltpu.VMEM((32, D), F32),
+            pltpu.VMEM((FRAME, D), F32),
+        ],
+        name="frames",
+    )(me, weights_flat.reshape(WROWS, D), obs_values, obs_node, obs_count)
+    pieces = spread_weights(frames)
+    wide = jax.ShapeDtypeStruct((count, D), F32)
+    slim = jax.ShapeDtypeStruct((count, D), BF)
+    square = jax.ShapeDtypeStruct((D, D), BF)
+    sources, target, rest, first, w_pagg, w_pout = pl.pallas_call(
+        encoder_kernel,
+        out_shape=[slim, wide, wide, slim, square, square],
+        in_specs=[in_smem()] + [in_any()] * 16 + [in_vmem()] * 4,
+        out_specs=[in_vmem()] * 6,
+        scratch_shapes=[
+            pltpu.VMEM((32 * WROWS, D), BF),
+            pltpu.VMEM((32, TILE, D), BF),
+            pltpu.VMEM((32, 2 * TILE, D), BF),
+            pltpu.VMEM((4, 256, 128), F32),
+            pltpu.VMEM((2, D, D), BF),
+            pltpu.VMEM((3, D, D), BF),
+            pltpu.SemaphoreType.DMA((32, 3)),
+        ],
+        name="encoder",
+    )(me, *pieces, mesh_init, edge_bias, node_bias, norm_gain)
+    forward = [(i, (i + 1) % 32) for i in range(32)]
+    backward = [(j, i) for i, j in forward]
+    low = lax.ppermute(sources[count - HALO :], axes, forward)
+    high = lax.ppermute(sources[:HALO], axes, backward)
+    return pl.pallas_call(
+        processor_kernel,
+        out_shape=slim,
+        in_specs=[in_vmem()] * 10,
+        out_specs=in_vmem(),
+        scratch_shapes=[pltpu.VMEM((count + 2 * HALO, D), BF)],
+        name="processor",
+    )(low, sources, high, target, rest, first, mesh_offset, w_pagg, w_pout, norm_gain)
+
+
 def solution(mesh):
     return jax.shard_map(
         shards,

time: 261 us -> 76.9 us (0.29)
  other arithmetic: 93.5 us -> 2.85 us
  local copies, waits for them, and re-layouts: 55.1 us -> 6.21 us
  starting transfers between devices: 35.5 us -> 14.7 us
  Pallas kernels: 0 us -> 17.9 us
  between operations: 13.6 us -> 0.17 us
  matrix products: 13.4 us -> 0 us
  waiting for transfers between devices: 47.1 us -> 34.7 us
    all_gather x1 -> x0, other arithmetic: 87.6 us -> none  [shards(): table = lax.all_gather(weights_flat, ('patch', 'lat'), axis=0, tiled=True)]
    all_to_all x6 -> x0, starting transfers between devices: 33.4 us -> none  [the longest x1 5.87 us: deliver(): lax.all_to_all(lax.all_to_all(counts, 'patch', split_axis=0, concat_axis=...]
    all_gather x1 -> x0, waiting for transfers between devices: 29.9 us -> none  [shards(): table = lax.all_gather(weights_flat, ('patch', 'lat'), axis=0, tiled=True)]
    ppermute x2 -> x21, waiting for transfers between devices: 6.13 us -> 34.7 us  [the longest x19 29.3 us: move(): return lax.ppermute(block, axes, [(i, i ^ masks[i & 1]) for i in range(32)])]
    slice x10 -> x1, local copies, waits for them, and re-layouts: 24 us -> 0.99 us  [shards(): high = lax.ppermute(sources[:HALO], axes, backward)]
    pallas_call x0 -> x3, Pallas kernels: none -> 17.9 us  [the longest x1 9.96 us: shards(): pl.pallas_call(encoder_kernel, out_shape=[slim, wide, wide, slim, square,...]
    dot_general x11 -> x0, matrix products: 13.4 us -> none  [the longest x1 3.51 us: shards(): jnp.dot(hidden2, w_pout, preferred_element_type=jnp.float32)]
    ppermute x2 -> x21, starting transfers between devices: 2.14 us -> 14.7 us  [the longest x19 11.4 us: move(): return lax.ppermute(block, axes, [(i, i ^ masks[i & 1]) for i in range(32)])]
  transfers between devices with their start and end apart: 9 -> 21, of which waited for: 8 -> 12; matrix products, arithmetic and copies ran while one was open for 5% -> 2% of each run, Pallas kernels for 0% -> 0%
where the time goes in v1:
time: 76.9 us; the launch traced here: 76.6 us
  waiting for transfers between devices  34.7 us (45%)
  Pallas kernels  17.9 us (23%)
  starting transfers between devices  14.7 us (19%)
  local copies, waits for them, and re-layouts  6.21 us (8%)
  other arithmetic  2.85 us (4%)
    ppermute x19, waiting for transfers between devices, move(): return lax.ppermute(block, axes, [(i, i ^ masks[i & 1]) for i in range(32)])  29.3 us
    ppermute x19, starting transfers between devices, move(): return lax.ppermute(block, axes, [(i, i ^ masks[i & 1]) for i in range(32)])  11.4 us
    pallas_call x1, Pallas kernels, shards(): pl.pallas_call(encoder_kernel, out_shape=[slim, wide, wide, slim, square,...  9.96 us
    pallas_call x1, Pallas kernels, shards(): pl.pallas_call(processor_kernel, out_shape=slim, in_specs=[in_vmem()] * 1...  5.78 us
    unnamed x45, local copies, waits for them, and re-layouts  4.47 us
    ppermute x1, waiting for transfers between devices, shards(): high = lax.ppermute(sources[:HALO], axes, backward)  4.24 us
    ppermute x1, starting transfers between devices, shards(): low = lax.ppermute(sources[count - HALO:], axes, forward)  3.29 us
    pallas_call x1, Pallas kernels, shards(): pl.pallas_call(frame_kernel, out_shape=[jax.ShapeDtypeStruct((FRAME, D),...  2.17 us
  transfers between devices with their start and end apart: 21, of which 12 were waited for; matrix products, arithmetic and copies ran while one was open for 2% of the time, Pallas kernels for 0%

profile of v1, /device:TPU:15, one launch (start us, length us, event | category | flops | bytes accessed | tf_op | source)
XLA Modules:
  0.0 76.6 jit_solution(17690903403663219967)
XLA Ops:
  0.0 1.8 %reduce = bf16[75264]{0:T(1024)(128)(2,1)S(1)} reduce(bf16[1,75264]{1,0:T(2,128)(2,1)} %param.14, bf16[]{:T(256)} %constant.13), dimensions={0}, to_apply=%param.14.reduce_sub_computation | reduce | bytes 301058 | tf_op args[5]
  1.8 0.0 copy-start.20
  1.8 0.8 reshape.7.w_ref
  2.6 0.7 copy.11.node_ref
  3.3 0.0 copy-done.18
  3.3 0.7 copy.10.val_ref
  4.0 2.2 %frames.1 = (bf16[168,512]{1,0:T(8,128)(2,1)}, bf16[168,512]{1,0:T(8,128)(2,1)}, bf16[168,512]{1,0:T(8,128)(2,1)}, bf16[168,512]{1,0:T(8,128)(2,1)}) custom-call(s32[1]{0:T(128)} %bitcast.me_ref, bf16[147,512]{1,0:T(8,128)(2,1)} %reshape.7.w_ref, bf16[128,96]{1,0:T(8,128)(2,1)} %copy.10.val_ref, s32[128,3]{1,0:T(8,128)} %copy.11.node_ref, s32[1,32]{1,0:T(1,128)} %count_ref.1), custom_call_target="tpu_custom_call" | custom-call | tf_op jit(solution)/shard_map/frames/pallas_call | solution.py:396
  6.2 2.3 %collective-permute-start.9 = (bf16[168,512]{1,0:T(8,128)(2,1)}, bf16[168,512]{1,0:T(8,128)(2,1)S(1)}, u32[]{:S(2)}, u32[]{:S(2)}) collective-permute-start(bf16[168,512]{1,0:T(8,128)(2,1)} %get-tuple-element.17), channel_id=1, source_target_pairs={{0,16},{1,17},{2,18},{3,19},{4,20},{5,21},{6,22},{7,23},{8,24},{9,... | collective-permute-start | bytes 516104 | tf_op jit(solution)/shard_map/ppermute | solution.py:359
  8.5 0.0 collective-permute-start.14
  8.5 0.2 collective-permute-start
  8.7 1.2 %collective-permute-start.4 = (bf16[168,512]{1,0:T(8,128)(2,1)}, bf16[168,512]{1,0:T(8,128)(2,1)S(1)}, u32[]{:S(2)}, u32[]{:S(2)}) collective-permute-start(bf16[168,512]{1,0:T(8,128)(2,1)} %get-tuple-element.16), channel_id=1, source_target_pairs={{0,8},{1,9},{2,10},{3,11},{4,12},{5,13},{6,14},{7,15},{8,0},{9,1},... | collective-permute-start | bytes 516104 | tf_op jit(solution)/shard_map/ppermute | solution.py:359
  10.0 10.3 %collective-permute-done.9 = bf16[168,512]{1,0:T(8,128)(2,1)S(1)} collective-permute-done((bf16[168,512]{1,0:T(8,128)(2,1)}, bf16[168,512]{1,0:T(8,128)(2,1)S(1)}, u32[]{:S(2)}, u32[]{:S(2)}) %collective-permute-start.9) | collective-permute-done | bytes 172064 | tf_op jit(solution)/shard_map/ppermute | solution.py:359
  20.2 0.2 collective-permute-start.10
  20.5 3.5 %collective-permute-done.14 = bf16[168,512]{1,0:T(8,128)(2,1)S(1)} collective-permute-done((bf16[168,512]{1,0:T(8,128)(2,1)}, bf16[168,512]{1,0:T(8,128)(2,1)S(1)}, u32[]{:S(2)}, u32[]{:S(2)}) %collective-permute-start.14) | collective-permute-done | bytes 172064 | tf_op jit(solution)/shard_map/ppermute | solution.py:359
  23.9 0.2 collective-permute-start.15
  24.1 0.0 collective-permute-done
  24.1 1.0 %pad_maximum_fusion.refs_0_ = bf16[2,168,512]{2,1,0:T(8,128)(2,1)S(1)} fusion(bf16[1,168,512]{2,1,0:T(8,128)(2,1)S(1)} %bitcast.15, bf16[1,168,512]{2,1,0:T(8,128)(2,1)} %bitcast.12), kind=kLoop, calls=%fused_computation | loop fusion | flops 172032 | bytes 688128 | tf_op jit(solution)/shard_map/stack | solution.py:364
  25.1 0.3 collective-permute-start.1
  25.4 1.1 %collective-permute-start.2 = (bf16[2,168,512]{2,1,0:T(8,128)(2,1)S(1)}, bf16[2,168,512]{2,1,0:T(8,128)(2,1)S(1)}, u32[]{:S(2)}, u32[]{:S(2)}) collective-permute-start(bf16[2,168,512]{2,1,0:T(8,128)(2,1)S(1)} %pad_maximum_fusion.refs_0_), channel_id=1, source_target_pairs={{0,1},{1,0},{2,3},{3,2},{4,5},{5,4},{6,7},{7,6},{8,9},{9,8},{10,11... | collective-permute-start | bytes 1032200 | tf_op jit(solution)/shard_map/ppermute | solution.py:359
  26.5 0.0 collective-permute-done.4
  26.5 1.2 %collective-permute-start.5 = (bf16[168,512]{1,0:T(8,128)(2,1)S(1)}, bf16[168,512]{1,0:T(8,128)(2,1)S(1)}, u32[]{:S(2)}, u32[]{:S(2)}) collective-permute-start(bf16[168,512]{1,0:T(8,128)(2,1)S(1)} %collective-permute-done.4), channel_id=1, source_target_pairs={{0,4},{1,3},{2,6},{3,1},{4,0},{5,7},{6,2},{7,5},{8,12},{9,11},{10,... | collective-permute-start | bytes 516104 | tf_op jit(solution)/shard_map/ppermute | solution.py:359
  27.7 0.0 collective-permute-done.10
  27.8 1.3 %collective-permute-start.11 = (bf16[2,168,512]{2,1,0:T(8,128)(2,1)S(1)}, bf16[2,168,512]{2,1,0:T(8,128)(2,1)S(1)}, u32[]{:S(2)}, u32[]{:S(2)}) collective-permute-start(bf16[2,168,512]{2,1,0:T(8,128)(2,1)S(1)} %pad_maximum_fusion.2.refs_8_), channel_id=1, source_target_pairs={{0,2},{1,5},{2,0},{3,7},{4,6},{5,1},{6,4},{7,3},{8,10},{9,13},{10,... | collective-permute-start | bytes 1032200 | tf_op jit(solution)/shard_map/ppermute | solution.py:359
  29.1 0.0 collective-permute-done.15
  29.1 0.0 copy-start.2
  29.1 0.3 collective-permute-start.16
  29.4 3.4 %collective-permute-done.5 = bf16[168,512]{1,0:T(8,128)(2,1)S(1)} collective-permute-done((bf16[168,512]{1,0:T(8,128)(2,1)S(1)}, bf16[168,512]{1,0:T(8,128)(2,1)S(1)}, u32[]{:S(2)}, u32[]{:S(2)}) %collective-permute-start.5) | collective-permute-done | bytes 172064 | tf_op jit(solution)/shard_map/ppermute | solution.py:359
  32.9 0.0 copy-start.3
  32.9 1.3 %collective-permute-start.6 = (bf16[2,168,512]{2,1,0:T(8,128)(2,1)S(1)}, bf16[2,168,512]{2,1,0:T(8,128)(2,1)S(1)}, u32[]{:S(2)}, u32[]{:S(2)}) collective-permute-start(bf16[2,168,512]{2,1,0:T(8,128)(2,1)S(1)} %pad_maximum_fusion.1.refs_4_), channel_id=1, source_target_pairs={{0,2},{1,5},{2,0},{3,7},{4,6},{5,1},{6,4},{7,3},{8,10},{9,13},{10,... | collective-permute-start | bytes 1032200 | tf_op jit(solution)/shard_map/ppermute | solution.py:359
  34.2 0.7 collective-permute-done.1.refs_1_
  35.0 0.5 collective-permute-start.12
  35.4 0.0 collective-permute-done.2.refs_2_
  35.4 0.1 collective-permute-start.17
  35.5 3.1 %collective-permute-done.11.refs_9_ = bf16[2,168,512]{2,1,0:T(8,128)(2,1)S(1)} collective-permute-done((bf16[2,168,512]{2,1,0:T(8,128)(2,1)S(1)}, bf16[2,168,512]{2,1,0:T(8,128)(2,1)S(1)}, u32[]{:S(2)}, u32[]{:S(2)}) %collective-permute-start.11) | collective-permute-done | bytes 344096 | tf_op jit(solution)/shard_map/ppermute | solution.py:359
  38.6 0.1 collective-permute-start.7
  38.8 3.6 %collective-permute-done.16.refs_13_ = bf16[2,168,512]{2,1,0:T(8,128)(2,1)S(1)} collective-permute-done((bf16[2,168,512]{2,1,0:T(8,128)(2,1)S(1)}, bf16[2,168,512]{2,1,0:T(8,128)(2,1)S(1)}, u32[]{:S(2)}, u32[]{:S(2)}) %collective-permute-start.16) | collective-permute-done | bytes 344096 | tf_op jit(solution)/shard_map/ppermute | solution.py:359
  42.3 0.1 collective-permute-start.3
  42.4 3.3 %collective-permute-done.6.refs_5_ = bf16[2,168,512]{2,1,0:T(8,128)(2,1)S(1)} collective-permute-done((bf16[2,168,512]{2,1,0:T(8,128)(2,1)S(1)}, bf16[2,168,512]{2,1,0:T(8,128)(2,1)S(1)}, u32[]{:S(2)}, u32[]{:S(2)}) %collective-permute-start.6) | collective-permute-done | bytes 344096 | tf_op jit(solution)/shard_map/ppermute | solution.py:359
  45.7 0.4 collective-permute-start.13
  46.1 0.0 collective-permute-done.12.refs_10_
  46.1 0.1 collective-permute-start.18
  46.3 0.0 collective-permute-done.17.refs_14_
  46.3 0.4 collective-permute-start.8
  46.7 0.0 collective-permute-done.7.refs_6_
  46.7 0.0 collective-permute-done.3.refs_3_
  46.7 0.7 collective-permute-done.13.refs_11_
  47.4 0.5 collective-permute-done.18.refs_15_
  47.9 0.0 copy-done.11
  47.9 0.2 copy-done.13
  48.1 0.3 collective-permute-done.8.refs_7_
  48.4 0.0 copy-done.4
  48.4 0.0 copy-done.6
  48.4 0.5 copy-done.14
  48.9 0.8 copy-done.15
  49.7 10.0 %encoder.1 = (bf16[320,512]{1,0:T(8,128)(2,1)}, f32[320,512]{1,0:T(8,128)}, f32[320,512]{1,0:T(8,128)}, bf16[320,512]{1,0:T(8,128)(2,1)}, bf16[512,512]{1,0:T(8,128)(2,1)}, /*index=5*/bf16[512,512]{1,0:T(8,128)(2,1)}) custom-call(s32[1]{0:T(128)} %bitcast.me_ref, bf16[2,168,512]{2,1,0:T(8,128)(2,1)} %copy-done, bf16[2,168,512]{2,1,0:T(8,128)(2,1)} %copy-done.4, ...), custom_call_target="tpu_custom_call" | custom-call | tf_op jit(solution)/shard_map/encoder/pallas_call | solution.py:412
  59.7 0.0 copy-start.19
  59.7 1.0 %fusion = (bf16[128,512]{1,0:T(8,128)(2,1)S(1)}, bf16[128,512]{1,0:T(8,128)(2,1)S(1)}) fusion(bf16[320,512]{1,0:T(8,128)(2,1)} %get-tuple-element.19.src_ref), kind=kLoop, calls=%fused_computation.4 | loop fusion | bytes 524288 | tf_op jit(solution)/shard_map/slice | solution.py:431
  60.7 3.3 %collective-permute-start.19 = (bf16[128,512]{1,0:T(8,128)(2,1)S(1)}, bf16[128,512]{1,0:T(8,128)(2,1)S(1)}, u32[]{:S(2)}, u32[]{:S(2)}) collective-permute-start(bf16[128,512]{1,0:T(8,128)(2,1)S(1)} %get-tuple-element.26), channel_id=1, source_target_pairs={{0,1},{1,2},{2,3},{3,4},{4,5},{5,6},{6,7},{7,8},{8,9},{9,10},{10,1... | collective-permute-start | bytes 393224 | tf_op jit(solution)/shard_map/ppermute | solution.py:430
  64.0 0.0 collective-permute-start.20
  64.0 0.8 %copy.12.off_ref = s32[320,6]{1,0:T(8,128)} copy(s32[320,6]{0,1:T(8,128)S(1)} %copy-done.19) | data formatting | bytes 15360 | tf_op args[4]
  64.8 1.1 %collective-permute-done.19.low_ref = bf16[128,512]{1,0:T(8,128)(2,1)S(1)} collective-permute-done((bf16[128,512]{1,0:T(8,128)(2,1)S(1)}, bf16[128,512]{1,0:T(8,128)(2,1)S(1)}, u32[]{:S(2)}, u32[]{:S(2)}) %collective-permute-start.19) | collective-permute-done | bytes 131104 | tf_op jit(solution)/shard_map/ppermute | solution.py:430
  65.9 4.2 %collective-permute-done.20.high_ref = bf16[128,512]{1,0:T(8,128)(2,1)S(1)} collective-permute-done((bf16[128,512]{1,0:T(8,128)(2,1)S(1)}, bf16[128,512]{1,0:T(8,128)(2,1)S(1)}, u32[]{:S(2)}, u32[]{:S(2)}) %collective-permute-start.20) | collective-permute-done | bytes 131104 | tf_op jit(solution)/shard_map/ppermute | solution.py:431
  70.2 0.6 copy-done.17
  70.8 5.8 %processor.1 = bf16[320,512]{1,0:T(8,128)(2,1)} custom-call(bf16[128,512]{1,0:T(8,128)(2,1)} %copy-done.16, bf16[320,512]{1,0:T(8,128)(2,1)} %get-tuple-element.19.src_ref, bf16[128,512]{1,0:T(8,128)(2,1)} %copy-done.17, f32[320,512]{1,0:T(8,128)} %get-tuple-element.20.tgt_ref, f32[320,512]{1,0:T(8,128)} %get-tuple-element.21.rest_ref, ...), custom_call_target="tpu_custom_call" | custom-call | tf_op jit(solution)/shard_map/processor/pallas_call | solution.py:432
  (33 shorter events, 0.2 us)
Async XLA Ops:
  1.8 0.8 %copy-start.20 = (s32[128,3]{0,1:T(4,128)S(1)}, s32[128,3]{0,1:T(4,128)}, u32[]{:S(2)}) copy-start(s32[128,3]{0,1:T(4,128)} %param.11) | copy-start | bytes 4612
  2.6 0.7 copy-start.18
  6.2 14.0 %collective-permute-start.9 = (bf16[168,512]{1,0:T(8,128)(2,1)}, bf16[168,512]{1,0:T(8,128)(2,1)S(1)}, u32[]{:S(2)}, u32[]{:S(2)}) collective-permute-start(bf16[168,512]{1,0:T(8,128)(2,1)} %get-tuple-element.17), channel_id=1, source_target_pairs={{0,16},{1,17},{2,18},{3,19},{4,20},{5,21},{6,22},{7,23},{8,24},{9,... | collective-permute-start | bytes 516104 | tf_op jit(solution)/shard_map/ppermute | solution.py:359
  8.5 15.4 %collective-permute-start.14 = (bf16[168,512]{1,0:T(8,128)(2,1)}, bf16[168,512]{1,0:T(8,128)(2,1)S(1)}, u32[]{:S(2)}, u32[]{:S(2)}) collective-permute-start(bf16[168,512]{1,0:T(8,128)(2,1)} %get-tuple-element.18), channel_id=1, source_target_pairs={{0,24},{1,25},{2,26},{3,27},{4,28},{5,29},{6,30},{7,31},{8,16},{9,... | collective-permute-start | bytes 516104 | tf_op jit(solution)/shard_map/ppermute | solution.py:359
  8.5 15.6 %collective-permute-start = (bf16[168,512]{1,0:T(8,128)(2,1)}, bf16[168,512]{1,0:T(8,128)(2,1)S(1)}, u32[]{:S(2)}, u32[]{:S(2)}) collective-permute-start(bf16[168,512]{1,0:T(8,128)(2,1)} %get-tuple-element.15), channel_id=1, source_target_pairs={{0,4},{1,3},{2,6},{3,1},{4,0},{5,7},{6,2},{7,5},{8,12},{9,11},{10,... | collective-permute-start | bytes 516104 | tf_op jit(solution)/shard_map/ppermute | solution.py:359
  8.7 17.7 %collective-permute-start.4 = (bf16[168,512]{1,0:T(8,128)(2,1)}, bf16[168,512]{1,0:T(8,128)(2,1)S(1)}, u32[]{:S(2)}, u32[]{:S(2)}) collective-permute-start(bf16[168,512]{1,0:T(8,128)(2,1)} %get-tuple-element.16), channel_id=1, source_target_pairs={{0,8},{1,9},{2,10},{3,11},{4,12},{5,13},{6,14},{7,15},{8,0},{9,1},... | collective-permute-start | bytes 516104 | tf_op jit(solution)/shard_map/ppermute | solution.py:359
  20.2 7.5 %collective-permute-start.10 = (bf16[168,512]{1,0:T(8,128)(2,1)S(1)}, bf16[168,512]{1,0:T(8,128)(2,1)S(1)}, u32[]{:S(2)}, u32[]{:S(2)}) collective-permute-start(bf16[168,512]{1,0:T(8,128)(2,1)S(1)} %collective-permute-done.9), channel_id=1, source_target_pairs={{0,4},{1,3},{2,6},{3,1},{4,0},{5,7},{6,2},{7,5},{8,12},{9,11},{10,... | collective-permute-start | bytes 516104 | tf_op jit(solution)/shard_map/ppermute | solution.py:359
  23.9 5.2 %collective-permute-start.15 = (bf16[168,512]{1,0:T(8,128)(2,1)S(1)}, bf16[168,512]{1,0:T(8,128)(2,1)S(1)}, u32[]{:S(2)}, u32[]{:S(2)}) collective-permute-start(bf16[168,512]{1,0:T(8,128)(2,1)S(1)} %collective-permute-done.14), channel_id=1, source_target_pairs={{0,4},{1,3},{2,6},{3,1},{4,0},{5,7},{6,2},{7,5},{8,12},{9,11},{10,... | collective-permute-start | bytes 516104 | tf_op jit(solution)/shard_map/ppermute | solution.py:359
  25.1 2.7 %copy-start = (bf16[2,168,512]{2,1,0:T(8,128)(2,1)}, bf16[2,168,512]{2,1,0:T(8,128)(2,1)S(1)}, u32[]{:S(2)}) copy-start(bf16[2,168,512]{2,1,0:T(8,128)(2,1)S(1)} %pad_maximum_fusion.refs_0_) | copy-start | bytes 1032196
  25.1 9.8 %collective-permute-start.1 = (bf16[2,168,512]{2,1,0:T(8,128)(2,1)S(1)}, bf16[2,168,512]{2,1,0:T(8,128)(2,1)S(1)}, u32[]{:S(2)}, u32[]{:S(2)}) collective-permute-start(bf16[2,168,512]{2,1,0:T(8,128)(2,1)S(1)} %pad_maximum_fusion.refs_0_), channel_id=1, source_target_pairs={{0,2},{1,5},{2,0},{3,7},{4,6},{5,1},{6,4},{7,3},{8,10},{9,13},{10,... | collective-permute-start | bytes 1032200 | tf_op jit(solution)/shard_map/ppermute | solution.py:359
  25.4 10.0 %collective-permute-start.2 = (bf16[2,168,512]{2,1,0:T(8,128)(2,1)S(1)}, bf16[2,168,512]{2,1,0:T(8,128)(2,1)S(1)}, u32[]{:S(2)}, u32[]{:S(2)}) collective-permute-start(bf16[2,168,512]{2,1,0:T(8,128)(2,1)S(1)} %pad_maximum_fusion.refs_0_), channel_id=1, source_target_pairs={{0,1},{1,0},{2,3},{3,2},{4,5},{5,4},{6,7},{7,6},{8,9},{9,8},{10,11... | collective-permute-start | bytes 1032200 | tf_op jit(solution)/shard_map/ppermute | solution.py:359
  26.5 6.4 %collective-permute-start.5 = (bf16[168,512]{1,0:T(8,128)(2,1)S(1)}, bf16[168,512]{1,0:T(8,128)(2,1)S(1)}, u32[]{:S(2)}, u32[]{:S(2)}) collective-permute-start(bf16[168,512]{1,0:T(8,128)(2,1)S(1)} %collective-permute-done.4), channel_id=1, source_target_pairs={{0,4},{1,3},{2,6},{3,1},{4,0},{5,7},{6,2},{7,5},{8,12},{9,11},{10,... | collective-permute-start | bytes 516104 | tf_op jit(solution)/shard_map/ppermute | solution.py:359
  27.8 7.2 %copy-start.1 = (bf16[2,168,512]{2,1,0:T(8,128)(2,1)}, bf16[2,168,512]{2,1,0:T(8,128)(2,1)S(1)}, u32[]{:S(2)}) copy-start(bf16[2,168,512]{2,1,0:T(8,128)(2,1)S(1)} %pad_maximum_fusion.2.refs_8_) | copy-start | bytes 1032196
  27.8 10.9 %collective-permute-start.11 = (bf16[2,168,512]{2,1,0:T(8,128)(2,1)S(1)}, bf16[2,168,512]{2,1,0:T(8,128)(2,1)S(1)}, u32[]{:S(2)}, u32[]{:S(2)}) collective-permute-start(bf16[2,168,512]{2,1,0:T(8,128)(2,1)S(1)} %pad_maximum_fusion.2.refs_8_), channel_id=1, source_target_pairs={{0,2},{1,5},{2,0},{3,7},{4,6},{5,1},{6,4},{7,3},{8,10},{9,13},{10,... | collective-permute-start | bytes 1032200 | tf_op jit(solution)/shard_map/ppermute | solution.py:359
  29.1 6.3 %copy-start.2 = (bf16[2,168,512]{2,1,0:T(8,128)(2,1)}, bf16[2,168,512]{2,1,0:T(8,128)(2,1)S(1)}, u32[]{:S(2)}) copy-start(bf16[2,168,512]{2,1,0:T(8,128)(2,1)S(1)} %pad_maximum_fusion.3.refs_12_) | copy-start | bytes 1032196
  29.1 13.2 %collective-permute-start.16 = (bf16[2,168,512]{2,1,0:T(8,128)(2,1)S(1)}, bf16[2,168,512]{2,1,0:T(8,128)(2,1)S(1)}, u32[]{:S(2)}, u32[]{:S(2)}) collective-permute-start(bf16[2,168,512]{2,1,0:T(8,128)(2,1)S(1)} %pad_maximum_fusion.3.refs_12_), channel_id=1, source_target_pairs={{0,2},{1,5},{2,0},{3,7},{4,6},{5,1},{6,4},{7,3},{8,10},{9,13},{10,... | collective-permute-start | bytes 1032200 | tf_op jit(solution)/shard_map/ppermute | solution.py:359
  32.9 15.5 %copy-start.3 = (bf16[2,168,512]{2,1,0:T(8,128)(2,1)}, bf16[2,168,512]{2,1,0:T(8,128)(2,1)S(1)}, u32[]{:S(2)}) copy-start(bf16[2,168,512]{2,1,0:T(8,128)(2,1)S(1)} %pad_maximum_fusion.1.refs_4_) | copy-start | bytes 1032196
  32.9 12.8 %collective-permute-start.6 = (bf16[2,168,512]{2,1,0:T(8,128)(2,1)S(1)}, bf16[2,168,512]{2,1,0:T(8,128)(2,1)S(1)}, u32[]{:S(2)}, u32[]{:S(2)}) collective-permute-start(bf16[2,168,512]{2,1,0:T(8,128)(2,1)S(1)} %pad_maximum_fusion.1.refs_4_), channel_id=1, source_target_pairs={{0,2},{1,5},{2,0},{3,7},{4,6},{5,1},{6,4},{7,3},{8,10},{9,13},{10,... | collective-permute-start | bytes 1032200 | tf_op jit(solution)/shard_map/ppermute | solution.py:359
  35.0 13.4 %copy-start.4 = (bf16[2,168,512]{2,1,0:T(8,128)(2,1)}, bf16[2,168,512]{2,1,0:T(8,128)(2,1)S(1)}, u32[]{:S(2)}) copy-start(bf16[2,168,512]{2,1,0:T(8,128)(2,1)S(1)} %collective-permute-done.1.refs_1_) | copy-start | bytes 1032196
  35.0 11.2 %collective-permute-start.12 = (bf16[2,168,512]{2,1,0:T(8,128)(2,1)S(1)}, bf16[2,168,512]{2,1,0:T(8,128)(2,1)S(1)}, u32[]{:S(2)}, u32[]{:S(2)}) collective-permute-start(bf16[2,168,512]{2,1,0:T(8,128)(2,1)S(1)} %pad_maximum_fusion.2.refs_8_), channel_id=1, source_target_pairs={{0,1},{1,0},{2,3},{3,2},{4,5},{5,4},{6,7},{7,6},{8,9},{9,8},{10,11... | collective-permute-start | bytes 1032200 | tf_op jit(solution)/shard_map/ppermute | solution.py:359
  35.4 13.0 %copy-start.5 = (bf16[2,168,512]{2,1,0:T(8,128)(2,1)}, bf16[2,168,512]{2,1,0:T(8,128)(2,1)S(1)}, u32[]{:S(2)}) copy-start(bf16[2,168,512]{2,1,0:T(8,128)(2,1)S(1)} %collective-permute-done.2.refs_2_) | copy-start | bytes 1032196
  35.4 10.8 %collective-permute-start.17 = (bf16[2,168,512]{2,1,0:T(8,128)(2,1)S(1)}, bf16[2,168,512]{2,1,0:T(8,128)(2,1)S(1)}, u32[]{:S(2)}, u32[]{:S(2)}) collective-permute-start(bf16[2,168,512]{2,1,0:T(8,128)(2,1)S(1)} %pad_maximum_fusion.3.refs_12_), channel_id=1, source_target_pairs={{0,1},{1,0},{2,3},{3,2},{4,5},{5,4},{6,7},{7,6},{8,9},{9,8},{10,11... | collective-permute-start | bytes 1032200 | tf_op jit(solution)/shard_map/ppermute | solution.py:359
  38.6 9.8 %copy-start.6 = (bf16[2,168,512]{2,1,0:T(8,128)(2,1)}, bf16[2,168,512]{2,1,0:T(8,128)(2,1)S(1)}, u32[]{:S(2)}) copy-start(bf16[2,168,512]{2,1,0:T(8,128)(2,1)S(1)} %collective-permute-done.11.refs_9_) | copy-start | bytes 1032196
  38.6 8.0 %collective-permute-start.7 = (bf16[2,168,512]{2,1,0:T(8,128)(2,1)S(1)}, bf16[2,168,512]{2,1,0:T(8,128)(2,1)S(1)}, u32[]{:S(2)}, u32[]{:S(2)}) collective-permute-start(bf16[2,168,512]{2,1,0:T(8,128)(2,1)S(1)} %pad_maximum_fusion.1.refs_4_), channel_id=1, source_target_pairs={{0,1},{1,0},{2,3},{3,2},{4,5},{5,4},{6,7},{7,6},{8,9},{9,8},{10,11... | collective-permute-start | bytes 1032200 | tf_op jit(solution)/shard_map/ppermute | solution.py:359
  42.3 6.1 %copy-start.7 = (bf16[2,168,512]{2,1,0:T(8,128)(2,1)}, bf16[2,168,512]{2,1,0:T(8,128)(2,1)S(1)}, u32[]{:S(2)}) copy-start(bf16[2,168,512]{2,1,0:T(8,128)(2,1)S(1)} %collective-permute-done.16.refs_13_) | copy-start | bytes 1032196
  42.3 4.3 %collective-permute-start.3 = (bf16[2,168,512]{2,1,0:T(8,128)(2,1)S(1)}, bf16[2,168,512]{2,1,0:T(8,128)(2,1)S(1)}, u32[]{:S(2)}, u32[]{:S(2)}) collective-permute-start(bf16[2,168,512]{2,1,0:T(8,128)(2,1)S(1)} %collective-permute-done.1.refs_1_), channel_id=1, source_target_pairs={{0,1},{1,0},{2,3},{3,2},{4,5},{5,4},{6,7},{7,6},{8,9},{9,8},{10,11... | collective-permute-start | bytes 1032200 | tf_op jit(solution)/shard_map/ppermute | solution.py:359
  45.7 2.7 %copy-start.8 = (bf16[2,168,512]{2,1,0:T(8,128)(2,1)}, bf16[2,168,512]{2,1,0:T(8,128)(2,1)S(1)}, u32[]{:S(2)}) copy-start(bf16[2,168,512]{2,1,0:T(8,128)(2,1)S(1)} %collective-permute-done.6.refs_5_) | copy-start | bytes 1032196
  45.7 1.7 %collective-permute-start.13 = (bf16[2,168,512]{2,1,0:T(8,128)(2,1)S(1)}, bf16[2,168,512]{2,1,0:T(8,128)(2,1)S(1)}, u32[]{:S(2)}, u32[]{:S(2)}) collective-permute-start(bf16[2,168,512]{2,1,0:T(8,128)(2,1)S(1)} %collective-permute-done.11.refs_9_), channel_id=1, source_target_pairs={{0,1},{1,0},{2,3},{3,2},{4,5},{5,4},{6,7},{7,6},{8,9},{9,8},{10,11... | collective-permute-start | bytes 1032200 | tf_op jit(solution)/shard_map/ppermute | solution.py:359
  46.1 2.3 %copy-start.9 = (bf16[2,168,512]{2,1,0:T(8,128)(2,1)}, bf16[2,168,512]{2,1,0:T(8,128)(2,1)S(1)}, u32[]{:S(2)}) copy-start(bf16[2,168,512]{2,1,0:T(8,128)(2,1)S(1)} %collective-permute-done.12.refs_10_) | copy-start | bytes 1032196
  46.1 1.8 %collective-permute-start.18 = (bf16[2,168,512]{2,1,0:T(8,128)(2,1)S(1)}, bf16[2,168,512]{2,1,0:T(8,128)(2,1)S(1)}, u32[]{:S(2)}, u32[]{:S(2)}) collective-permute-start(bf16[2,168,512]{2,1,0:T(8,128)(2,1)S(1)} %collective-permute-done.16.refs_13_), channel_id=1, source_target_pairs={{0,1},{1,0},{2,3},{3,2},{4,5},{5,4},{6,7},{7,6},{8,9},{9,8},{10,11... | collective-permute-start | bytes 1032200 | tf_op jit(solution)/shard_map/ppermute | solution.py:359
  46.3 2.2 %copy-start.10 = (bf16[2,168,512]{2,1,0:T(8,128)(2,1)}, bf16[2,168,512]{2,1,0:T(8,128)(2,1)S(1)}, u32[]{:S(2)}) copy-start(bf16[2,168,512]{2,1,0:T(8,128)(2,1)S(1)} %collective-permute-done.17.refs_14_) | copy-start | bytes 1032196
  46.3 2.1 %collective-permute-start.8 = (bf16[2,168,512]{2,1,0:T(8,128)(2,1)S(1)}, bf16[2,168,512]{2,1,0:T(8,128)(2,1)S(1)}, u32[]{:S(2)}, u32[]{:S(2)}) collective-permute-start(bf16[2,168,512]{2,1,0:T(8,128)(2,1)S(1)} %collective-permute-done.6.refs_5_), channel_id=1, source_target_pairs={{0,1},{1,0},{2,3},{3,2},{4,5},{5,4},{6,7},{7,6},{8,9},{9,8},{10,11... | collective-permute-start | bytes 1032200 | tf_op jit(solution)/shard_map/ppermute | solution.py:359
  46.7 1.2 %copy-start.11 = (bf16[2,168,512]{2,1,0:T(8,128)(2,1)}, bf16[2,168,512]{2,1,0:T(8,128)(2,1)S(1)}, u32[]{:S(2)}) copy-start(bf16[2,168,512]{2,1,0:T(8,128)(2,1)S(1)} %collective-permute-done.7.refs_6_) | copy-start | bytes 1032196
  46.7 1.2 %copy-start.12 = (bf16[2,168,512]{2,1,0:T(8,128)(2,1)}, bf16[2,168,512]{2,1,0:T(8,128)(2,1)S(1)}, u32[]{:S(2)}) copy-start(bf16[2,168,512]{2,1,0:T(8,128)(2,1)S(1)} %collective-permute-done.3.refs_3_) | copy-start | bytes 1032196
  47.4 0.7 copy-start.13
  48.1 0.8 %copy-start.14 = (bf16[2,168,512]{2,1,0:T(8,128)(2,1)}, bf16[2,168,512]{2,1,0:T(8,128)(2,1)S(1)}, u32[]{:S(2)}) copy-start(bf16[2,168,512]{2,1,0:T(8,128)(2,1)S(1)} %collective-permute-done.18.refs_15_) | copy-start | bytes 1032196
  48.9 0.8 %copy-start.15 = (bf16[2,168,512]{2,1,0:T(8,128)(2,1)}, bf16[2,168,512]{2,1,0:T(8,128)(2,1)S(1)}, u32[]{:S(2)}) copy-start(bf16[2,168,512]{2,1,0:T(8,128)(2,1)S(1)} %collective-permute-done.8.refs_7_) | copy-start | bytes 1032196
  59.7 4.3 %copy-start.19 = (s32[320,6]{0,1:T(8,128)S(1)}, s32[320,6]{0,1:T(8,128)}, u32[]{:S(2)}) copy-start(s32[320,6]{0,1:T(8,128)} %param.13) | copy-start | bytes 23044
  60.7 5.2 %collective-permute-start.19 = (bf16[128,512]{1,0:T(8,128)(2,1)S(1)}, bf16[128,512]{1,0:T(8,128)(2,1)S(1)}, u32[]{:S(2)}, u32[]{:S(2)}) collective-permute-start(bf16[128,512]{1,0:T(8,128)(2,1)S(1)} %get-tuple-element.26), channel_id=1, source_target_pairs={{0,1},{1,2},{2,3},{3,4},{4,5},{5,6},{6,7},{7,8},{8,9},{9,10},{10,1... | collective-permute-start | bytes 393224 | tf_op jit(solution)/shard_map/ppermute | solution.py:430
  64.0 6.2 %collective-permute-start.20 = (bf16[128,512]{1,0:T(8,128)(2,1)S(1)}, bf16[128,512]{1,0:T(8,128)(2,1)S(1)}, u32[]{:S(2)}, u32[]{:S(2)}) collective-permute-start(bf16[128,512]{1,0:T(8,128)(2,1)S(1)} %get-tuple-element.25), channel_id=1, source_target_pairs={{1,0},{2,1},{3,2},{4,3},{5,4},{6,5},{7,6},{8,7},{9,8},{10,9},{11,1... | collective-permute-start | bytes 393224 | tf_op jit(solution)/shard_map/ppermute | solution.py:431
  65.9 4.2 %copy-start.16 = (bf16[128,512]{1,0:T(8,128)(2,1)}, bf16[128,512]{1,0:T(8,128)(2,1)S(1)}, u32[]{:S(2)}) copy-start(bf16[128,512]{1,0:T(8,128)(2,1)S(1)} %collective-permute-done.19.low_ref) | copy-start | bytes 393220
  70.2 0.7 copy-start.17

commit v2 on v1

--- a/solution.py
+++ b/solution.py
@@ -158,6 +158,7 @@
 F32 = jnp.float32
 TILE = 16
 FRAME = 168
+DEAD = 256.0
 
 
 def silu(values):
@@ -186,30 +187,28 @@
 
 
 def frame_kernel(me_ref, w_ref, val_ref, node_ref, count_ref, *refs):
-    outs, (slots, rows, frame) = refs[:4], refs[4:]
+    outs, (turned, slots, rows, frame) = refs[:4], refs[4:]
     me = me_ref[0]
-    height = w_ref.shape[0]
-    n_slots, breadth = val_ref.shape
+    breadth, n_slots = val_ref.shape
     senders = count_ref.shape[1]
     capacity = n_slots // senders
-    phase = lax.rem(height * me, TILE)
-    own = iota((n_slots, senders), 0) // capacity == iota((n_slots, senders), 1)
-    live = jnp.sum(jnp.where(own, count_ref[...].astype(F32), 0.0), axis=1, keepdims=True)
-    place = (iota((n_slots, 1), 0) % capacity).astype(F32)
-    code = jnp.where(place < live, node_ref[...] + 1, 0)
-    high = (code >> 4).astype(F32)
-    low = (code & 15).astype(F32)
-    lane = iota((n_slots, 128 - breadth), 1)
-    tail = jnp.zeros((n_slots, 128 - breadth), F32)
+    phase = lax.rem(WROWS * me, TILE)
+    for r in range(WROWS):
+        frame[pl.ds(phase + r, 1), :] = w_ref[0:1, D * r : D * (r + 1)].astype(F32)
+    own = (iota((senders, n_slots), 0) == iota((senders, n_slots), 1) // capacity).astype(BF)
+    counts = jnp.broadcast_to(count_ref[...], (8, senders)).astype(F32).astype(BF)
+    live = mm(counts, own)[0:1, :]
+    place = (iota((1, n_slots), 1) % capacity).astype(F32)
+    code = jnp.where(place < live, node_ref[...].astype(F32) - DEAD, DEAD)
+    turned[:breadth, :] = val_ref[...].astype(F32)
+    line = iota((n_slots - breadth, n_slots), 0)
+    tail = jnp.zeros((n_slots - breadth, n_slots), F32)
     for k in range(OBS_EDGES):
-        tail = jnp.where(lane == 2 * k, high[:, k : k + 1], tail)
-        tail = jnp.where(lane == 2 * k + 1, low[:, k : k + 1], tail)
-    slots[:, :breadth] = val_ref[...].astype(F32)
-    slots[:, breadth:] = tail
+        tail = jnp.where(line == k, code[k : k + 1, :], tail)
+    turned[breadth:, :] = tail
+    slots[...] = turned[...].T
     for j in range(capacity):
         rows[:, 128 * j : 128 * (j + 1)] = slots[pl.ds(j, senders, stride=capacity), :]
-    shift = (iota((FRAME, height), 0) == iota((FRAME, height), 1) + phase).astype(BF)
-    frame[...] = mm(shift, w_ref[...])
     start = pl.multiple_of(jnp.where(phase >= 8, 0, FRAME - 8), 8)
     for flip in range(4):
         plane = (me >> 3) ^ flip
@@ -221,12 +220,10 @@
     pieces = refs[:16]
     init_ref, edge_ref, nbias_ref, gain_ref = refs[16:20]
     src_ref, tgt_ref, rest_ref, first_ref, pagg_ref, pout_ref = refs[20:26]
-    big, heads, tails, obs, enc, proc, sems = refs[26:]
+    big, heads, tails, obs, enc, proc = refs[26:]
     height = WROWS
     me = me_ref[0]
     core = me & 1
-    copies = []
-    at = 0
     for unit in range(4):
         for twin in range(2):
             ax = jnp.where((core ^ twin) == 0, 4, 2)
@@ -237,17 +234,9 @@
                     mask = (8 * unit) ^ twin ^ (ax if j else 0) ^ (ay if pair else 0)
                     dev = me ^ mask
                     row = pl.multiple_of((height * dev) // TILE * TILE + TILE, TILE)
-                    for s, (lo, hi, dst) in enumerate((
-                        (0, 16, heads.at[dev]),
-                        (16, 144, big.at[pl.ds(row, 128)]),
-                        (144, FRAME, tails.at[dev, pl.ds(0, FRAME - 144)]),
-                    )):
-                        copy = pltpu.make_async_copy(piece.at[j, pl.ds(lo, hi - lo)], dst, sems.at[at, s])
-                        copy.start()
-                        copies.append(copy)
-                    at += 1
-    for copy in copies:
-        copy.wait()
+                    heads[dev] = piece[j, 0:TILE, :]
+                    big[pl.ds(row, 128), :] = piece[j, TILE : TILE + 128, :]
+                    tails[dev, 0 : FRAME - 144, :] = piece[j, 144:FRAME, :]
     row16 = iota((TILE, D), 0)
     for dev in range(32):
         phase = height * dev % TILE
@@ -295,8 +284,8 @@
     node_ids = iota((slots.shape[0], init.shape[0]), 1)
     picks = []
     for k in range(OBS_EDGES):
-        code = slots[:, CH + 2 * k : CH + 2 * k + 1] * 16.0 + slots[:, CH + 2 * k + 1 : CH + 2 * k + 2]
-        picks.append((node_ids == code.astype(jnp.int32) - 1).astype(F32))
+        code = slots[:, CH + k : CH + k + 1] + DEAD
+        picks.append((node_ids == code.astype(jnp.int32)).astype(F32))
     select = jnp.concatenate(picks, axis=0)
     spread = select.astype(BF)
     q_high = query.astype(BF)
@@ -400,11 +389,13 @@
         out_specs=[in_vmem()] * 4,
         scratch_shapes=[
             pltpu.VMEM((128, 128), F32),
+            pltpu.VMEM((128, 128), F32),
             pltpu.VMEM((32, D), F32),
             pltpu.VMEM((FRAME, D), F32),
         ],
+        compiler_params=pltpu.CompilerParams(vmem_limit_bytes=8 << 20),
         name="frames",
-    )(me, weights_flat.reshape(WROWS, D), obs_values, obs_node, obs_count)
+    )(me, weights_flat, obs_values.T, obs_node.T, obs_count)
     pieces = spread_weights(frames)
     wide = jax.ShapeDtypeStruct((count, D), F32)
     slim = jax.ShapeDtypeStruct((count, D), BF)
@@ -412,7 +403,7 @@
     sources, target, rest, first, w_pagg, w_pout = pl.pallas_call(
         encoder_kernel,
         out_shape=[slim, wide, wide, slim, square, square],
-        in_specs=[in_smem()] + [in_any()] * 16 + [in_vmem()] * 4,
+        in_specs=[in_smem()] + [in_vmem()] * 16 + [in_vmem()] * 4,
         out_specs=[in_vmem()] * 6,
         scratch_shapes=[
             pltpu.VMEM((32 * WROWS, D), BF),
@@ -421,8 +412,8 @@
             pltpu.VMEM((4, 256, 128), F32),
             pltpu.VMEM((2, D, D), BF),
             pltpu.VMEM((3, D, D), BF),
-            pltpu.SemaphoreType.DMA((32, 3)),
         ],
+        compiler_params=pltpu.CompilerParams(vmem_limit_bytes=34 << 20),
         name="encoder",
     )(me, *pieces, mesh_init, edge_bias, node_bias, norm_gain)
     forward = [(i, (i + 1) % 32) for i in range(32)]
@@ -435,6 +426,7 @@
         in_specs=[in_vmem()] * 10,
         out_specs=in_vmem(),
         scratch_shapes=[pltpu.VMEM((count + 2 * HALO, D), BF)],
+        compiler_params=pltpu.CompilerParams(vmem_limit_bytes=20 << 20),
         name="processor",
     )(low, sources, high, target, rest, first, mesh_offset, w_pagg, w_pout, norm_gain)
 

time: 76.9 us -> 63 us (0.82)
  Pallas kernels: 17.9 us -> 8.9 us
  local copies, waits for them, and re-layouts: 6.21 us -> 3.25 us
  other arithmetic: 2.85 us -> 0.14 us
    pallas_call x1, Pallas kernels: 9.96 us -> 4.66 us  [shards(): pl.pallas_call(encoder_kernel, out_shape=[slim, wide, wide, slim, square,...]
    unnamed x45 -> x19, local copies, waits for them, and re-layouts: 4.47 us -> 2.54 us
    pallas_call x1, Pallas kernels: 5.78 us -> 3.9 us  [shards(): pl.pallas_call(processor_kernel, out_shape=slim, in_specs=[in_vmem()] * 1...]
    pallas_call x1, Pallas kernels: 2.17 us -> 0.34 us  [shards(): pl.pallas_call(frame_kernel, out_shape=[jax.ShapeDtypeStruct((FRAME, D),...]
    unnamed x1 -> x0, other arithmetic: 1.8 us -> none
    ppermute x1, waiting for transfers between devices: 1.12 us -> 2.11 us  [shards(): low = lax.ppermute(sources[count - HALO:], axes, forward)]
    another operation x4, other arithmetic: 1.05 us -> 0.14 us  [spread_weights(): pair = jnp.stack([unit, move(unit, (4, 2))])]
  transfers between devices with their start and end apart: 21 -> 21, of which waited for: 12 -> 13; matrix products, arithmetic and copies ran while one was open for 2% -> 0% of each run, Pallas kernels for 0% -> 0%
where the time goes in v2:
time: 63 us; the launch traced here: 62.8 us
  waiting for transfers between devices  35.3 us (56%)
  starting transfers between devices  15.1 us (24%)
  Pallas kernels  8.9 us (14%)
  local copies, waits for them, and re-layouts  3.25 us (5%)
    ppermute x19, waiting for transfers between devices, move(): return lax.ppermute(block, axes, [(i, i ^ masks[i & 1]) for i in range(32)])  29.1 us
    ppermute x19, starting transfers between devices, move(): return lax.ppermute(block, axes, [(i, i ^ masks[i & 1]) for i in range(32)])  12 us
    pallas_call x1, Pallas kernels, shards(): pl.pallas_call(encoder_kernel, out_shape=[slim, wide, wide, slim, square,...  4.66 us
    ppermute x1, waiting for transfers between devices, shards(): high = lax.ppermute(sources[:HALO], axes, backward)  4.14 us
    pallas_call x1, Pallas kernels, shards(): pl.pallas_call(processor_kernel, out_shape=slim, in_specs=[in_vmem()] * 1...  3.9 us
    ppermute x1, starting transfers between devices, shards(): low = lax.ppermute(sources[count - HALO:], axes, forward)  3.06 us
    unnamed x19, local copies, waits for them, and re-layouts  2.54 us
    ppermute x1, waiting for transfers between devices, shards(): low = lax.ppermute(sources[count - HALO:], axes, forward)  2.11 us
  transfers between devices with their start and end apart: 21, of which 13 were waited for; matrix products, arithmetic and copies ran while one was open for 0% of the time, Pallas kernels for 0%

profile of v2, /device:TPU:15, one launch (start us, length us, event | category | flops | bytes accessed | tf_op | source)
XLA Modules:
  0.0 62.8 jit_solution(11222862127531378010)
XLA Ops:
  0.0 0.0 copy-start.6
  0.0 0.0 copy-start.7
  0.0 0.7 %copy-done.6 = s32[128,3]{0,1:T(4,128)S(1)} copy-done((s32[128,3]{0,1:T(4,128)S(1)}, s32[128,3]{0,1:T(4,128)}, u32[]{:S(2)}) %copy-start.6) | copy-done | bytes 1560
  0.7 0.0 copy-done.7
  0.7 0.0 copy-start.1
  0.7 1.0 %copy-done.1 = bf16[1,75264]{1,0:T(2,128)(2,1)S(1)} copy-done((bf16[1,75264]{1,0:T(2,128)(2,1)S(1)}, bf16[1,75264]{1,0:T(2,128)(2,1)}, u32[]{:S(2)}) %copy-start.1) | copy-done | bytes 150552
  1.6 0.0 copy-start.2
  1.7 0.7 %copy-done.2 = bf16[128,96]{0,1:T(8,128)(2,1)S(1)} copy-done((bf16[128,96]{0,1:T(8,128)(2,1)S(1)}, bf16[128,96]{0,1:T(8,128)(2,1)}, u32[]{:S(2)}) %copy-start.2) | copy-done | bytes 24600
  2.4 0.3 frames.1
  2.7 2.4 %collective-permute-start.9 = (bf16[168,512]{1,0:T(8,128)(2,1)S(1)}, bf16[168,512]{1,0:T(8,128)(2,1)S(1)}, u32[]{:S(2)}, u32[]{:S(2)}) collective-permute-start(bf16[168,512]{1,0:T(8,128)(2,1)S(1)} %get-tuple-element.17), channel_id=1, source_target_pairs={{0,16},{1,17},{2,18},{3,19},{4,20},{5,21},{6,22},{7,23},{8,24},{9,... | collective-permute-start | bytes 516104 | tf_op jit(solution)/shard_map/ppermute | solution.py:348
  5.1 0.0 collective-permute-start.14
  5.1 0.2 collective-permute-start
  5.3 1.3 %collective-permute-start.4 = (bf16[168,512]{1,0:T(8,128)(2,1)S(1)}, bf16[168,512]{1,0:T(8,128)(2,1)S(1)}, u32[]{:S(2)}, u32[]{:S(2)}) collective-permute-start(bf16[168,512]{1,0:T(8,128)(2,1)S(1)} %get-tuple-element.16), channel_id=1, source_target_pairs={{0,8},{1,9},{2,10},{3,11},{4,12},{5,13},{6,14},{7,15},{8,0},{9,1},... | collective-permute-start | bytes 516104 | tf_op jit(solution)/shard_map/ppermute | solution.py:348
  6.6 9.9 %collective-permute-done.9 = bf16[168,512]{1,0:T(8,128)(2,1)S(1)} collective-permute-done((bf16[168,512]{1,0:T(8,128)(2,1)S(1)}, bf16[168,512]{1,0:T(8,128)(2,1)S(1)}, u32[]{:S(2)}, u32[]{:S(2)}) %collective-permute-start.9) | collective-permute-done | bytes 172064 | tf_op jit(solution)/shard_map/ppermute | solution.py:348
  16.5 0.2 collective-permute-start.10
  16.7 3.5 %collective-permute-done.14 = bf16[168,512]{1,0:T(8,128)(2,1)S(1)} collective-permute-done((bf16[168,512]{1,0:T(8,128)(2,1)S(1)}, bf16[168,512]{1,0:T(8,128)(2,1)S(1)}, u32[]{:S(2)}, u32[]{:S(2)}) %collective-permute-start.14) | collective-permute-done | bytes 172064 | tf_op jit(solution)/shard_map/ppermute | solution.py:348
  20.2 0.2 collective-permute-start.15
  20.4 0.0 collective-permute-done
  20.5 0.3 collective-permute-start.1
  20.8 1.1 %collective-permute-start.2 = (bf16[2,168,512]{2,1,0:T(8,128)(2,1)S(1)}, bf16[2,168,512]{2,1,0:T(8,128)(2,1)S(1)}, u32[]{:S(2)}, u32[]{:S(2)}) collective-permute-start(bf16[2,168,512]{2,1,0:T(8,128)(2,1)S(1)} %pad_maximum_fusion.refs_0_), channel_id=1, source_target_pairs={{0,1},{1,0},{2,3},{3,2},{4,5},{5,4},{6,7},{7,6},{8,9},{9,8},{10,11... | collective-permute-start | bytes 1032200 | tf_op jit(solution)/shard_map/ppermute | solution.py:348
  21.8 0.0 collective-permute-done.4
  21.8 1.2 %collective-permute-start.5 = (bf16[168,512]{1,0:T(8,128)(2,1)S(1)}, bf16[168,512]{1,0:T(8,128)(2,1)S(1)}, u32[]{:S(2)}, u32[]{:S(2)}) collective-permute-start(bf16[168,512]{1,0:T(8,128)(2,1)S(1)} %collective-permute-done.4), channel_id=1, source_target_pairs={{0,4},{1,3},{2,6},{3,1},{4,0},{5,7},{6,2},{7,5},{8,12},{9,11},{10,... | collective-permute-start | bytes 516104 | tf_op jit(solution)/shard_map/ppermute | solution.py:348
  23.1 0.0 collective-permute-done.10
  23.1 1.3 %collective-permute-start.11 = (bf16[2,168,512]{2,1,0:T(8,128)(2,1)S(1)}, bf16[2,168,512]{2,1,0:T(8,128)(2,1)S(1)}, u32[]{:S(2)}, u32[]{:S(2)}) collective-permute-start(bf16[2,168,512]{2,1,0:T(8,128)(2,1)S(1)} %pad_maximum_fusion.2.refs_8_), channel_id=1, source_target_pairs={{0,2},{1,5},{2,0},{3,7},{4,6},{5,1},{6,4},{7,3},{8,10},{9,13},{10,... | collective-permute-start | bytes 1032200 | tf_op jit(solution)/shard_map/ppermute | solution.py:348
  24.4 0.6 collective-permute-done.15
  25.0 0.1 collective-permute-start.16
  25.1 3.6 %collective-permute-done.5 = bf16[168,512]{1,0:T(8,128)(2,1)S(1)} collective-permute-done((bf16[168,512]{1,0:T(8,128)(2,1)S(1)}, bf16[168,512]{1,0:T(8,128)(2,1)S(1)}, u32[]{:S(2)}, u32[]{:S(2)}) %collective-permute-start.5) | collective-permute-done | bytes 172064 | tf_op jit(solution)/shard_map/ppermute | solution.py:348
  28.7 0.0 copy-start
  28.7 0.0 copy-start.3
  28.7 0.0 copy-start.4
  28.7 0.8 %collective-permute-start.6 = (bf16[2,168,512]{2,1,0:T(8,128)(2,1)S(1)}, bf16[2,168,512]{2,1,0:T(8,128)(2,1)S(1)}, u32[]{:S(2)}, u32[]{:S(2)}) collective-permute-start(bf16[2,168,512]{2,1,0:T(8,128)(2,1)S(1)} %pad_maximum_fusion.1.refs_4_), channel_id=1, source_target_pairs={{0,2},{1,5},{2,0},{3,7},{4,6},{5,1},{6,4},{7,3},{8,10},{9,13},{10,... | collective-permute-start | bytes 1032200 | tf_op jit(solution)/shard_map/ppermute | solution.py:348
  29.6 0.4 collective-permute-done.1.refs_1_
  30.0 1.9 %collective-permute-start.12 = (bf16[2,168,512]{2,1,0:T(8,128)(2,1)S(1)}, bf16[2,168,512]{2,1,0:T(8,128)(2,1)S(1)}, u32[]{:S(2)}, u32[]{:S(2)}) collective-permute-start(bf16[2,168,512]{2,1,0:T(8,128)(2,1)S(1)} %pad_maximum_fusion.2.refs_8_), channel_id=1, source_target_pairs={{0,1},{1,0},{2,3},{3,2},{4,5},{5,4},{6,7},{7,6},{8,9},{9,8},{10,11... | collective-permute-start | bytes 1032200 | tf_op jit(solution)/shard_map/ppermute | solution.py:348
  31.9 0.0 collective-permute-done.2.refs_2_
  31.9 0.1 collective-permute-start.17
  31.9 2.4 %collective-permute-done.11.refs_9_ = bf16[2,168,512]{2,1,0:T(8,128)(2,1)S(1)} collective-permute-done((bf16[2,168,512]{2,1,0:T(8,128)(2,1)S(1)}, bf16[2,168,512]{2,1,0:T(8,128)(2,1)S(1)}, u32[]{:S(2)}, u32[]{:S(2)}) %collective-permute-start.11) | collective-permute-done | bytes 344096 | tf_op jit(solution)/shard_map/ppermute | solution.py:348
  34.3 0.1 collective-permute-start.7
  34.4 3.6 %collective-permute-done.16.refs_13_ = bf16[2,168,512]{2,1,0:T(8,128)(2,1)S(1)} collective-permute-done((bf16[2,168,512]{2,1,0:T(8,128)(2,1)S(1)}, bf16[2,168,512]{2,1,0:T(8,128)(2,1)S(1)}, u32[]{:S(2)}, u32[]{:S(2)}) %collective-permute-start.16) | collective-permute-done | bytes 344096 | tf_op jit(solution)/shard_map/ppermute | solution.py:348
  38.0 0.1 collective-permute-start.3
  38.0 3.3 %collective-permute-done.6.refs_5_ = bf16[2,168,512]{2,1,0:T(8,128)(2,1)S(1)} collective-permute-done((bf16[2,168,512]{2,1,0:T(8,128)(2,1)S(1)}, bf16[2,168,512]{2,1,0:T(8,128)(2,1)S(1)}, u32[]{:S(2)}, u32[]{:S(2)}) %collective-permute-start.6) | collective-permute-done | bytes 344096 | tf_op jit(solution)/shard_map/ppermute | solution.py:348
  41.4 0.4 collective-permute-start.13
  41.7 0.0 collective-permute-done.12.refs_10_
  41.7 0.2 collective-permute-start.18
  41.9 0.0 collective-permute-done.17.refs_14_
  41.9 0.4 collective-permute-start.8
  42.3 0.0 collective-permute-done.7.refs_6_
  42.3 0.0 collective-permute-done.3.refs_3_
  42.3 0.8 %collective-permute-done.13.refs_11_ = bf16[2,168,512]{2,1,0:T(8,128)(2,1)S(1)} collective-permute-done((bf16[2,168,512]{2,1,0:T(8,128)(2,1)S(1)}, bf16[2,168,512]{2,1,0:T(8,128)(2,1)S(1)}, u32[]{:S(2)}, u32[]{:S(2)}) %collective-permute-start.13) | collective-permute-done | bytes 344096 | tf_op jit(solution)/shard_map/ppermute | solution.py:348
  43.0 0.5 collective-permute-done.18.refs_15_
  43.5 0.5 collective-permute-done.8.refs_7_
  44.0 0.0 copy-done
  44.0 0.0 copy-done.3
  44.0 0.0 copy-done.4
  44.0 0.0 copy-done.5
  44.0 4.7 %encoder.1 = (bf16[320,512]{1,0:T(8,128)(2,1)S(1)}, f32[320,512]{1,0:T(8,128)S(1)}, f32[320,512]{1,0:T(8,128)S(1)}, bf16[320,512]{1,0:T(8,128)(2,1)S(1)}, bf16[5...) custom-call(s32[1]{0:T(128)} %bitcast.me_ref, bf16[2,168,512]{2,1,0:T(8,128)(2,1)S(1)} %pad_maximum_fusion.refs_0_, ...), custom_call_target="tpu_custom_call" | custom-call | tf_op jit(solution)/shard_map/encoder/pallas_call | solution.py:403
  48.7 0.0 copy-start.8
  48.7 0.7 %fusion = (bf16[128,512]{1,0:T(8,128)(2,1)}, bf16[128,512]{1,0:T(8,128)(2,1)}) fusion(bf16[320,512]{1,0:T(8,128)(2,1)S(1)} %get-tuple-element.19.src_ref), kind=kLoop, calls=%fused_computation.4 | loop fusion | bytes 524288 | tf_op jit(solution)/shard_map/slice | solution.py:422
  49.4 3.1 %collective-permute-start.19 = (bf16[128,512]{1,0:T(8,128)(2,1)}, bf16[128,512]{1,0:T(8,128)(2,1)S(1)}, u32[]{:S(2)}, u32[]{:S(2)}) collective-permute-start(bf16[128,512]{1,0:T(8,128)(2,1)} %get-tuple-element.26), channel_id=1, source_target_pairs={{0,1},{1,2},{2,3},{3,4},{4,5},{5,6},{6,7},{7,8},{8,9},{9,10},{10,1... | collective-permute-start | bytes 393224 | tf_op jit(solution)/shard_map/ppermute | solution.py:421
  52.5 0.0 collective-permute-start.20
  52.5 0.0 copy-done.8
  52.5 0.1 copy.10.off_ref
  52.6 2.1 %collective-permute-done.19.low_ref = bf16[128,512]{1,0:T(8,128)(2,1)S(1)} collective-permute-done((bf16[128,512]{1,0:T(8,128)(2,1)}, bf16[128,512]{1,0:T(8,128)(2,1)S(1)}, u32[]{:S(2)}, u32[]{:S(2)}) %collective-permute-start.19) | collective-permute-done | bytes 131104 | tf_op jit(solution)/shard_map/ppermute | solution.py:421
  54.8 4.1 %collective-permute-done.20.high_ref = bf16[128,512]{1,0:T(8,128)(2,1)S(1)} collective-permute-done((bf16[128,512]{1,0:T(8,128)(2,1)}, bf16[128,512]{1,0:T(8,128)(2,1)S(1)}, u32[]{:S(2)}, u32[]{:S(2)}) %collective-permute-start.20) | collective-permute-done | bytes 131104 | tf_op jit(solution)/shard_map/ppermute | solution.py:422
  58.9 3.9 %processor.1 = bf16[320,512]{1,0:T(8,128)(2,1)} custom-call(bf16[128,512]{1,0:T(8,128)(2,1)S(1)} %collective-permute-done.19.low_ref, bf16[320,512]{1,0:T(8,128)(2,1)S(1)} %get-tuple-element.19.src_ref, bf16[128,512]{1,0:T(8,128)(2,1)S(1)} %collective-permute-done.20.high_ref, f32[320,512]{1,0:T(8,128)S(1)} %get-tuple-element.20.tgt_ref, ...), custom_call_target="tpu_custom_call" | custom-call | tf_op jit(solution)/shard_map/processor/pallas_call | solution.py:423
  (5 shorter events, 0.1 us)
Async XLA Ops:
  0.0 0.7 %copy-start.6 = (s32[128,3]{0,1:T(4,128)S(1)}, s32[128,3]{0,1:T(4,128)}, u32[]{:S(2)}) copy-start(s32[128,3]{0,1:T(4,128)} %param.11) | copy-start | bytes 4612
  0.0 0.7 %copy-start.7 = (s32[1,32]{1,0:T(1,128)S(1)}, s32[1,32]{1,0:T(1,128)}, u32[]{:S(2)}) copy-start(s32[1,32]{1,0:T(1,128)} %count_ref.1) | copy-start | bytes 388
  0.7 1.0 %copy-start.1 = (bf16[1,75264]{1,0:T(2,128)(2,1)S(1)}, bf16[1,75264]{1,0:T(2,128)(2,1)}, u32[]{:S(2)}) copy-start(bf16[1,75264]{1,0:T(2,128)(2,1)} %w_ref.1) | copy-start | bytes 451588
  1.6 0.7 %copy-start.2 = (bf16[128,96]{0,1:T(8,128)(2,1)S(1)}, bf16[128,96]{0,1:T(8,128)(2,1)}, u32[]{:S(2)}) copy-start(bf16[128,96]{0,1:T(8,128)(2,1)} %param.9) | copy-start | bytes 73732
  2.7 13.8 %collective-permute-start.9 = (bf16[168,512]{1,0:T(8,128)(2,1)S(1)}, bf16[168,512]{1,0:T(8,128)(2,1)S(1)}, u32[]{:S(2)}, u32[]{:S(2)}) collective-permute-start(bf16[168,512]{1,0:T(8,128)(2,1)S(1)} %get-tuple-element.17), channel_id=1, source_target_pairs={{0,16},{1,17},{2,18},{3,19},{4,20},{5,21},{6,22},{7,23},{8,24},{9,... | collective-permute-start | bytes 516104 | tf_op jit(solution)/shard_map/ppermute | solution.py:348
  5.1 15.1 %collective-permute-start.14 = (bf16[168,512]{1,0:T(8,128)(2,1)S(1)}, bf16[168,512]{1,0:T(8,128)(2,1)S(1)}, u32[]{:S(2)}, u32[]{:S(2)}) collective-permute-start(bf16[168,512]{1,0:T(8,128)(2,1)S(1)} %get-tuple-element.18), channel_id=1, source_target_pairs={{0,24},{1,25},{2,26},{3,27},{4,28},{5,29},{6,30},{7,31},{8,16},{9,... | collective-permute-start | bytes 516104 | tf_op jit(solution)/shard_map/ppermute | solution.py:348
  5.1 15.3 %collective-permute-start = (bf16[168,512]{1,0:T(8,128)(2,1)S(1)}, bf16[168,512]{1,0:T(8,128)(2,1)S(1)}, u32[]{:S(2)}, u32[]{:S(2)}) collective-permute-start(bf16[168,512]{1,0:T(8,128)(2,1)S(1)} %get-tuple-element.15), channel_id=1, source_target_pairs={{0,4},{1,3},{2,6},{3,1},{4,0},{5,7},{6,2},{7,5},{8,12},{9,11},{10,... | collective-permute-start | bytes 516104 | tf_op jit(solution)/shard_map/ppermute | solution.py:348
  5.3 16.5 %collective-permute-start.4 = (bf16[168,512]{1,0:T(8,128)(2,1)S(1)}, bf16[168,512]{1,0:T(8,128)(2,1)S(1)}, u32[]{:S(2)}, u32[]{:S(2)}) collective-permute-start(bf16[168,512]{1,0:T(8,128)(2,1)S(1)} %get-tuple-element.16), channel_id=1, source_target_pairs={{0,8},{1,9},{2,10},{3,11},{4,12},{5,13},{6,14},{7,15},{8,0},{9,1},... | collective-permute-start | bytes 516104 | tf_op jit(solution)/shard_map/ppermute | solution.py:348
  16.5 6.6 %collective-permute-start.10 = (bf16[168,512]{1,0:T(8,128)(2,1)S(1)}, bf16[168,512]{1,0:T(8,128)(2,1)S(1)}, u32[]{:S(2)}, u32[]{:S(2)}) collective-permute-start(bf16[168,512]{1,0:T(8,128)(2,1)S(1)} %collective-permute-done.9), channel_id=1, source_target_pairs={{0,4},{1,3},{2,6},{3,1},{4,0},{5,7},{6,2},{7,5},{8,12},{9,11},{10,... | collective-permute-start | bytes 516104 | tf_op jit(solution)/shard_map/ppermute | solution.py:348
  20.2 4.8 %collective-permute-start.15 = (bf16[168,512]{1,0:T(8,128)(2,1)S(1)}, bf16[168,512]{1,0:T(8,128)(2,1)S(1)}, u32[]{:S(2)}, u32[]{:S(2)}) collective-permute-start(bf16[168,512]{1,0:T(8,128)(2,1)S(1)} %collective-permute-done.14), channel_id=1, source_target_pairs={{0,4},{1,3},{2,6},{3,1},{4,0},{5,7},{6,2},{7,5},{8,12},{9,11},{10,... | collective-permute-start | bytes 516104 | tf_op jit(solution)/shard_map/ppermute | solution.py:348
  20.5 9.5 %collective-permute-start.1 = (bf16[2,168,512]{2,1,0:T(8,128)(2,1)S(1)}, bf16[2,168,512]{2,1,0:T(8,128)(2,1)S(1)}, u32[]{:S(2)}, u32[]{:S(2)}) collective-permute-start(bf16[2,168,512]{2,1,0:T(8,128)(2,1)S(1)} %pad_maximum_fusion.refs_0_), channel_id=1, source_target_pairs={{0,2},{1,5},{2,0},{3,7},{4,6},{5,1},{6,4},{7,3},{8,10},{9,13},{10,... | collective-permute-start | bytes 1032200 | tf_op jit(solution)/shard_map/ppermute | solution.py:348
  20.8 11.1 %collective-permute-start.2 = (bf16[2,168,512]{2,1,0:T(8,128)(2,1)S(1)}, bf16[2,168,512]{2,1,0:T(8,128)(2,1)S(1)}, u32[]{:S(2)}, u32[]{:S(2)}) collective-permute-start(bf16[2,168,512]{2,1,0:T(8,128)(2,1)S(1)} %pad_maximum_fusion.refs_0_), channel_id=1, source_target_pairs={{0,1},{1,0},{2,3},{3,2},{4,5},{5,4},{6,7},{7,6},{8,9},{9,8},{10,11... | collective-permute-start | bytes 1032200 | tf_op jit(solution)/shard_map/ppermute | solution.py:348
  21.8 6.8 %collective-permute-start.5 = (bf16[168,512]{1,0:T(8,128)(2,1)S(1)}, bf16[168,512]{1,0:T(8,128)(2,1)S(1)}, u32[]{:S(2)}, u32[]{:S(2)}) collective-permute-start(bf16[168,512]{1,0:T(8,128)(2,1)S(1)} %collective-permute-done.4), channel_id=1, source_target_pairs={{0,4},{1,3},{2,6},{3,1},{4,0},{5,7},{6,2},{7,5},{8,12},{9,11},{10,... | collective-permute-start | bytes 516104 | tf_op jit(solution)/shard_map/ppermute | solution.py:348
  23.1 11.2 %collective-permute-start.11 = (bf16[2,168,512]{2,1,0:T(8,128)(2,1)S(1)}, bf16[2,168,512]{2,1,0:T(8,128)(2,1)S(1)}, u32[]{:S(2)}, u32[]{:S(2)}) collective-permute-start(bf16[2,168,512]{2,1,0:T(8,128)(2,1)S(1)} %pad_maximum_fusion.2.refs_8_), channel_id=1, source_target_pairs={{0,2},{1,5},{2,0},{3,7},{4,6},{5,1},{6,4},{7,3},{8,10},{9,13},{10,... | collective-permute-start | bytes 1032200 | tf_op jit(solution)/shard_map/ppermute | solution.py:348
  25.0 12.9 %collective-permute-start.16 = (bf16[2,168,512]{2,1,0:T(8,128)(2,1)S(1)}, bf16[2,168,512]{2,1,0:T(8,128)(2,1)S(1)}, u32[]{:S(2)}, u32[]{:S(2)}) collective-permute-start(bf16[2,168,512]{2,1,0:T(8,128)(2,1)S(1)} %pad_maximum_fusion.3.refs_12_), channel_id=1, source_target_pairs={{0,2},{1,5},{2,0},{3,7},{4,6},{5,1},{6,4},{7,3},{8,10},{9,13},{10,... | collective-permute-start | bytes 1032200 | tf_op jit(solution)/shard_map/ppermute | solution.py:348
  28.7 15.3 %copy-start = (bf16[320,512]{1,0:T(8,128)(2,1)S(1)}, bf16[320,512]{1,0:T(8,128)(2,1)}, u32[]{:S(2)}) copy-start(bf16[320,512]{1,0:T(8,128)(2,1)} %refs_16_.1) | copy-start | bytes 983044
  28.7 15.3 %copy-start.3 = (f32[2,512]{1,0:T(2,128)S(1)}, f32[2,512]{1,0:T(2,128)}, u32[]{:S(2)}) copy-start(f32[2,512]{1,0:T(2,128)} %gain_ref.1) | copy-start | bytes 12292
  28.7 15.3 %copy-start.4 = (f32[2,512]{1,0:T(2,128)S(1)}, f32[2,512]{1,0:T(2,128)}, u32[]{:S(2)}) copy-start(f32[2,512]{1,0:T(2,128)} %refs_17_.1) | copy-start | bytes 12292
  28.7 15.3 %copy-start.5 = (f32[2,512]{1,0:T(2,128)S(1)}, f32[2,512]{1,0:T(2,128)}, u32[]{:S(2)}) copy-start(f32[2,512]{1,0:T(2,128)} %refs_18_.1) | copy-start | bytes 12292
  28.7 12.6 %collective-permute-start.6 = (bf16[2,168,512]{2,1,0:T(8,128)(2,1)S(1)}, bf16[2,168,512]{2,1,0:T(8,128)(2,1)S(1)}, u32[]{:S(2)}, u32[]{:S(2)}) collective-permute-start(bf16[2,168,512]{2,1,0:T(8,128)(2,1)S(1)} %pad_maximum_fusion.1.refs_4_), channel_id=1, source_target_pairs={{0,2},{1,5},{2,0},{3,7},{4,6},{5,1},{6,4},{7,3},{8,10},{9,13},{10,... | collective-permute-start | bytes 1032200 | tf_op jit(solution)/shard_map/ppermute | solution.py:348
  30.0 11.8 %collective-permute-start.12 = (bf16[2,168,512]{2,1,0:T(8,128)(2,1)S(1)}, bf16[2,168,512]{2,1,0:T(8,128)(2,1)S(1)}, u32[]{:S(2)}, u32[]{:S(2)}) collective-permute-start(bf16[2,168,512]{2,1,0:T(8,128)(2,1)S(1)} %pad_maximum_fusion.2.refs_8_), channel_id=1, source_target_pairs={{0,1},{1,0},{2,3},{3,2},{4,5},{5,4},{6,7},{7,6},{8,9},{9,8},{10,11... | collective-permute-start | bytes 1032200 | tf_op jit(solution)/shard_map/ppermute | solution.py:348
  31.9 10.0 %collective-permute-start.17 = (bf16[2,168,512]{2,1,0:T(8,128)(2,1)S(1)}, bf16[2,168,512]{2,1,0:T(8,128)(2,1)S(1)}, u32[]{:S(2)}, u32[]{:S(2)}) collective-permute-start(bf16[2,168,512]{2,1,0:T(8,128)(2,1)S(1)} %pad_maximum_fusion.3.refs_12_), channel_id=1, source_target_pairs={{0,1},{1,0},{2,3},{3,2},{4,5},{5,4},{6,7},{7,6},{8,9},{9,8},{10,11... | collective-permute-start | bytes 1032200 | tf_op jit(solution)/shard_map/ppermute | solution.py:348
  34.3 8.0 %collective-permute-start.7 = (bf16[2,168,512]{2,1,0:T(8,128)(2,1)S(1)}, bf16[2,168,512]{2,1,0:T(8,128)(2,1)S(1)}, u32[]{:S(2)}, u32[]{:S(2)}) collective-permute-start(bf16[2,168,512]{2,1,0:T(8,128)(2,1)S(1)} %pad_maximum_fusion.1.refs_4_), channel_id=1, source_target_pairs={{0,1},{1,0},{2,3},{3,2},{4,5},{5,4},{6,7},{7,6},{8,9},{9,8},{10,11... | collective-permute-start | bytes 1032200 | tf_op jit(solution)/shard_map/ppermute | solution.py:348
  38.0 4.3 %collective-permute-start.3 = (bf16[2,168,512]{2,1,0:T(8,128)(2,1)S(1)}, bf16[2,168,512]{2,1,0:T(8,128)(2,1)S(1)}, u32[]{:S(2)}, u32[]{:S(2)}) collective-permute-start(bf16[2,168,512]{2,1,0:T(8,128)(2,1)S(1)} %collective-permute-done.1.refs_1_), channel_id=1, source_target_pairs={{0,1},{1,0},{2,3},{3,2},{4,5},{5,4},{6,7},{7,6},{8,9},{9,8},{10,11... | collective-permute-start | bytes 1032200 | tf_op jit(solution)/shard_map/ppermute | solution.py:348
  41.4 1.7 %collective-permute-start.13 = (bf16[2,168,512]{2,1,0:T(8,128)(2,1)S(1)}, bf16[2,168,512]{2,1,0:T(8,128)(2,1)S(1)}, u32[]{:S(2)}, u32[]{:S(2)}) collective-permute-start(bf16[2,168,512]{2,1,0:T(8,128)(2,1)S(1)} %collective-permute-done.11.refs_9_), channel_id=1, source_target_pairs={{0,1},{1,0},{2,3},{3,2},{4,5},{5,4},{6,7},{7,6},{8,9},{9,8},{10,11... | collective-permute-start | bytes 1032200 | tf_op jit(solution)/shard_map/ppermute | solution.py:348
  41.7 1.8 %collective-permute-start.18 = (bf16[2,168,512]{2,1,0:T(8,128)(2,1)S(1)}, bf16[2,168,512]{2,1,0:T(8,128)(2,1)S(1)}, u32[]{:S(2)}, u32[]{:S(2)}) collective-permute-start(bf16[2,168,512]{2,1,0:T(8,128)(2,1)S(1)} %collective-permute-done.16.refs_13_), channel_id=1, source_target_pairs={{0,1},{1,0},{2,3},{3,2},{4,5},{5,4},{6,7},{7,6},{8,9},{9,8},{10,11... | collective-permute-start | bytes 1032200 | tf_op jit(solution)/shard_map/ppermute | solution.py:348
  41.9 2.1 %collective-permute-start.8 = (bf16[2,168,512]{2,1,0:T(8,128)(2,1)S(1)}, bf16[2,168,512]{2,1,0:T(8,128)(2,1)S(1)}, u32[]{:S(2)}, u32[]{:S(2)}) collective-permute-start(bf16[2,168,512]{2,1,0:T(8,128)(2,1)S(1)} %collective-permute-done.6.refs_5_), channel_id=1, source_target_pairs={{0,1},{1,0},{2,3},{3,2},{4,5},{5,4},{6,7},{7,6},{8,9},{9,8},{10,11... | collective-permute-start | bytes 1032200 | tf_op jit(solution)/shard_map/ppermute | solution.py:348
  48.7 3.8 %copy-start.8 = (s32[320,6]{0,1:T(8,128)S(1)}, s32[320,6]{0,1:T(8,128)}, u32[]{:S(2)}) copy-start(s32[320,6]{0,1:T(8,128)} %param.13) | copy-start | bytes 23044
  49.4 5.3 %collective-permute-start.19 = (bf16[128,512]{1,0:T(8,128)(2,1)}, bf16[128,512]{1,0:T(8,128)(2,1)S(1)}, u32[]{:S(2)}, u32[]{:S(2)}) collective-permute-start(bf16[128,512]{1,0:T(8,128)(2,1)} %get-tuple-element.26), channel_id=1, source_target_pairs={{0,1},{1,2},{2,3},{3,4},{4,5},{5,6},{6,7},{7,8},{8,9},{9,10},{10,1... | collective-permute-start | bytes 393224 | tf_op jit(solution)/shard_map/ppermute | solution.py:421
  52.5 6.4 %collective-permute-start.20 = (bf16[128,512]{1,0:T(8,128)(2,1)}, bf16[128,512]{1,0:T(8,128)(2,1)S(1)}, u32[]{:S(2)}, u32[]{:S(2)}) collective-permute-start(bf16[128,512]{1,0:T(8,128)(2,1)} %get-tuple-element.25), channel_id=1, source_target_pairs={{1,0},{2,1},{3,2},{4,3},{5,4},{6,5},{7,6},{8,7},{9,8},{10,9},{11,1... | collective-permute-start | bytes 393224 | tf_op jit(solution)/shard_map/ppermute | solution.py:422

commit v3 on v2

--- a/solution.py
+++ b/solution.py
@@ -157,7 +157,7 @@
 BF = jnp.bfloat16
 F32 = jnp.float32
 TILE = 16
-FRAME = 168
+FRAME = 176
 DEAD = 256.0
 
 
@@ -182,12 +182,8 @@
     return pl.BlockSpec(memory_space=pltpu.SMEM)
 
 
-def in_any():
-    return pl.BlockSpec(memory_space=pl.ANY)
-
-
 def frame_kernel(me_ref, w_ref, val_ref, node_ref, count_ref, *refs):
-    outs, (turned, slots, rows, frame) = refs[:4], refs[4:]
+    outs, (turned, slots, rows, frame) = refs[:2], refs[2:]
     me = me_ref[0]
     breadth, n_slots = val_ref.shape
     senders = count_ref.shape[1]
@@ -209,18 +205,21 @@
     slots[...] = turned[...].T
     for j in range(capacity):
         rows[:, 128 * j : 128 * (j + 1)] = slots[pl.ds(j, senders, stride=capacity), :]
-    start = pl.multiple_of(jnp.where(phase >= 8, 0, FRAME - 8), 8)
-    for flip in range(4):
-        plane = (me >> 3) ^ flip
-        frame[pl.ds(start, 8), :] = rows[pl.ds(pl.multiple_of(plane * 8, 8), 8), :]
+    start = pl.multiple_of(jnp.where(phase >= 8, 0, FRAME - 16), 8)
+    for flip in range(2):
+        for ref, spot, plane in (
+            (frame, start, (me >> 3) ^ (2 * flip)),
+            (frame, FRAME - 8, (me >> 3) ^ (2 * flip + 1)),
+        ):
+            ref[pl.ds(spot, 8), :] = rows[pl.ds(pl.multiple_of(plane * 8, 8), 8), :]
         outs[flip][...] = frame[...].astype(BF)
 
 
 def encoder_kernel(me_ref, *refs):
     pieces = refs[:16]
     init_ref, edge_ref, nbias_ref, gain_ref = refs[16:20]
-    src_ref, tgt_ref, rest_ref, first_ref, pagg_ref, pout_ref = refs[20:26]
-    big, heads, tails, obs, enc, proc = refs[26:]
+    src_ref, start_ref, end_ref, tgt_ref, rest_ref, first_ref, pagg_ref, pout_ref = refs[20:28]
+    big, edges, obs, enc, proc = refs[28:]
     height = WROWS
     me = me_ref[0]
     core = me & 1
@@ -234,27 +233,30 @@
                     mask = (8 * unit) ^ twin ^ (ax if j else 0) ^ (ay if pair else 0)
                     dev = me ^ mask
                     row = pl.multiple_of((height * dev) // TILE * TILE + TILE, TILE)
-                    heads[dev] = piece[j, 0:TILE, :]
+                    edges[dev, 0:TILE, :] = piece[j, 0:TILE, :]
                     big[pl.ds(row, 128), :] = piece[j, TILE : TILE + 128, :]
-                    tails[dev, 0 : FRAME - 144, :] = piece[j, 144:FRAME, :]
+                    edges[dev, TILE : 3 * TILE, :] = piece[j, 144:FRAME, :]
+                    if unit % 2:
+                        spot = jnp.where(lax.rem(height * dev, TILE) >= 8, 0, 32)
+                        edges[dev, pl.ds(pl.multiple_of(spot, TILE), 8), :] = piece[j, FRAME - 8 :, :]
     row16 = iota((TILE, D), 0)
     for dev in range(32):
         phase = height * dev % TILE
         tile = height * dev // TILE
         after = height * (dev + 1) // TILE
-        head = heads[dev]
+        head = edges[dev, 0:TILE, :]
         if phase:
             before = height * (dev - 1) // TILE
             skip = TILE * (tile - before) - 144
-            last = tails[dev - 1, skip : skip + TILE, :]
+            last = edges[dev - 1, TILE + skip : 2 * TILE + skip, :]
             head = jnp.where(row16 < phase, last.astype(F32), head.astype(F32)).astype(BF)
         big[TILE * tile : TILE * (tile + 1), :] = head
         if after - tile == 10:
-            big[TILE * (tile + 9) : TILE * (tile + 10), :] = tails[dev, 0:TILE, :]
+            big[TILE * (tile + 9) : TILE * (tile + 10), :] = edges[dev, TILE : 2 * TILE, :]
         if phase >= 8:
-            seen = heads[dev].astype(F32)[0:8]
+            seen = edges[dev, 0:TILE, :].astype(F32)[0:8]
         else:
-            seen = tails[dev, TILE : 2 * TILE, :].astype(F32)[0:8]
+            seen = edges[dev, 2 * TILE : 3 * TILE, :].astype(F32)[0:8]
         for j in range(4):
             obs[j, 8 * dev : 8 * (dev + 1), :] = seen[:, 128 * j : 128 * (j + 1)]
     e0 = CH
@@ -303,7 +305,10 @@
         init.astype(F32) + layer_norm(mm(hidden, big[o0 : o0 + D, :]), gain_ref[0:1, :])
     ).astype(BF)
     first_ref[...] = first
-    src_ref[...] = mm(first, proc[0]).astype(BF)
+    sources = mm(first, proc[0]).astype(BF)
+    src_ref[...] = sources
+    start_ref[...] = sources[:HALO]
+    end_ref[...] = sources[sources.shape[0] - HALO :]
     tgt_ref[...] = mm(first, proc[1]) + edge_ref[1:2, :]
     rest_ref[...] = mm(first, proc[2]) + nbias_ref[1:2, :]
 
@@ -315,12 +320,21 @@
     ext[0:HALO, :] = low_ref[...]
     ext[HALO : HALO + count, :] = src_ref[...]
     ext[HALO + count :, :] = high_ref[...]
-    target = tgt_ref[...]
-    cols = iota((count, count + 2 * HALO), 1) - iota((count, count + 2 * HALO), 0) - HALO
-    pooled = jnp.zeros((count, D), F32)
-    for k in range(DEG):
-        select = (cols == off_ref[:, k : k + 1]).astype(BF)
-        pooled = pooled + silu(mm(select, ext[...]) + target)
+    block = count // 2
+    span = block + 2 * HALO
+    cols = iota((block, span), 1) - iota((block, span), 0) - HALO
+    sums = []
+    for at in range(0, count, block):
+        select = jnp.concatenate(
+            [(cols == off_ref[at : at + block, k : k + 1]).astype(F32) for k in range(DEG)], axis=0
+        ).astype(BF)
+        picked = mm(select, ext[at : at + span, :])
+        target = tgt_ref[at : at + block, :]
+        total = silu(picked[:block] + target)
+        for k in range(1, DEG):
+            total = total + silu(picked[block * k : block * (k + 1)] + target)
+        sums.append(total)
+    pooled = jnp.concatenate(sums, axis=0)
     hidden = silu(rest_ref[...] + mm(pooled.astype(BF), pagg_ref[...])).astype(BF)
     out_ref[...] = (
         first_ref[...].astype(F32) + layer_norm(mm(hidden, pout_ref[...]), gain_ref[1:2, :])
@@ -330,7 +344,7 @@
 WROWS = 147
 
 
-def fits(obs_values, obs_node, mesh_init, weights_flat):
+def fits(obs_values, mesh_init, weights_flat):
     return (
         lax.axis_size("patch") == 8
         and lax.axis_size("lat") == 4
@@ -338,19 +352,27 @@
         and obs_values.shape == (128, CH)
         and mesh_init.shape[0] <= 320
         and mesh_init.shape[0] >= HALO
+        and mesh_init.shape[0] % 32 == 0
     )
 
 
-def spread_weights(frames):
+def spread_weights(near, far):
     axes = ("patch", "lat")
 
     def move(block, masks):
         return lax.ppermute(block, axes, [(i, i ^ masks[i & 1]) for i in range(32)])
 
-    units = [frames[0]] + [move(frames[f], (8 * f, 8 * f)) for f in (1, 2, 3)]
+    beside = move(near, (4, 2))
+    opposite = move(far, (16, 16))
+    aside = move(opposite, (4, 2))
     pieces = []
-    for unit in units:
-        pair = jnp.stack([unit, move(unit, (4, 2))])
+    for unit, twin in (
+        (near, beside),
+        (move(near, (8, 8)), move(beside, (8, 8))),
+        (opposite, aside),
+        (move(opposite, (8, 8)), move(aside, (8, 8))),
+    ):
+        pair = jnp.stack([unit, twin])
         other = move(pair, (2, 4))
         pieces += [pair, other, move(pair, (1, 1)), move(other, (1, 1))]
     return pieces
@@ -367,7 +389,7 @@
     node_bias,
     norm_gain,
 ):
-    if not fits(obs_values, obs_node, mesh_init, weights_flat):
+    if not fits(obs_values, mesh_init, weights_flat):
         return general(
             obs_values,
             obs_count,
@@ -384,9 +406,9 @@
     count = mesh_init.shape[0]
     frames = pl.pallas_call(
         frame_kernel,
-        out_shape=[jax.ShapeDtypeStruct((FRAME, D), BF)] * 4,
+        out_shape=[jax.ShapeDtypeStruct((FRAME, D), BF)] * 2,
         in_specs=[in_smem()] + [in_vmem()] * 4,
-        out_specs=[in_vmem()] * 4,
+        out_specs=[in_vmem()] * 2,
         scratch_shapes=[
             pltpu.VMEM((128, 128), F32),
             pltpu.VMEM((128, 128), F32),
@@ -396,19 +418,19 @@
         compiler_params=pltpu.CompilerParams(vmem_limit_bytes=8 << 20),
         name="frames",
     )(me, weights_flat, obs_values.T, obs_node.T, obs_count)
-    pieces = spread_weights(frames)
+    pieces = spread_weights(*frames)
     wide = jax.ShapeDtypeStruct((count, D), F32)
     slim = jax.ShapeDtypeStruct((count, D), BF)
     square = jax.ShapeDtypeStruct((D, D), BF)
-    sources, target, rest, first, w_pagg, w_pout = pl.pallas_call(
+    side = jax.ShapeDtypeStruct((HALO, D), BF)
+    sources, start, end, target, rest, first, w_pagg, w_pout = pl.pallas_call(
         encoder_kernel,
-        out_shape=[slim, wide, wide, slim, square, square],
+        out_shape=[slim, side, side, wide, wide, slim, square, square],
         in_specs=[in_smem()] + [in_vmem()] * 16 + [in_vmem()] * 4,
-        out_specs=[in_vmem()] * 6,
+        out_specs=[in_vmem()] * 8,
         scratch_shapes=[
             pltpu.VMEM((32 * WROWS, D), BF),
-            pltpu.VMEM((32, TILE, D), BF),
-            pltpu.VMEM((32, 2 * TILE, D), BF),
+            pltpu.VMEM((32, 3 * TILE, D), BF),
             pltpu.VMEM((4, 256, 128), F32),
             pltpu.VMEM((2, D, D), BF),
             pltpu.VMEM((3, D, D), BF),
@@ -418,8 +440,8 @@
     )(me, *pieces, mesh_init, edge_bias, node_bias, norm_gain)
     forward = [(i, (i + 1) % 32) for i in range(32)]
     backward = [(j, i) for i, j in forward]
-    low = lax.ppermute(sources[count - HALO :], axes, forward)
-    high = lax.ppermute(sources[:HALO], axes, backward)
+    low = lax.ppermute(end, axes, forward)
+    high = lax.ppermute(start, axes, backward)
     return pl.pallas_call(
         processor_kernel,
         out_shape=slim,

time: 63 us -> 59.9 us (0.951); the launches traced: 62.8 us -> 58.7 us
  waiting for transfers between devices: 35.3 us -> 26.1 us
  starting transfers between devices: 15.1 us -> 21.2 us
  local copies, waits for them, and re-layouts: 3.25 us -> 2.54 us
    ppermute x19, waiting for transfers between devices: 29.1 us -> 19.8 us  [move(): return lax.ppermute(block, axes, [(i, i ^ masks[i & 1]) for i in range(32)])]
    ppermute x19, starting transfers between devices: 12 us -> 17.9 us  [move(): return lax.ppermute(block, axes, [(i, i ^ masks[i & 1]) for i in range(32)])]
    slice x1 -> x0, local copies, waits for them, and re-layouts: 0.71 us -> none  [shards(): high = lax.ppermute(sources[:HALO], axes, backward)]
  transfers between devices with their start and end apart: 21 -> 21, of which waited for: 13 -> 10; matrix products, arithmetic and copies ran while one was open for 0% -> 0% of each run, Pallas kernels for 0% -> 0%
where the time goes in v3:
time: 59.9 us; the launch traced here: 58.7 us
  waiting for transfers between devices  26.1 us (44%)
  starting transfers between devices  21.2 us (35%)
  Pallas kernels  8.64 us (14%)
  local copies, waits for them, and re-layouts  2.54 us (4%)
    ppermute x19, waiting for transfers between devices, move(): return lax.ppermute(block, axes, [(i, i ^ masks[i & 1]) for i in range(32)])  19.8 us
    ppermute x19, starting transfers between devices, move(): return lax.ppermute(block, axes, [(i, i ^ masks[i & 1]) for i in range(32)])  17.9 us
    pallas_call x1, Pallas kernels, shards(): pl.pallas_call(encoder_kernel, out_shape=[slim, side, side, wide, wide, s...  4.99 us
    ppermute x1, waiting for transfers between devices, shards(): high = lax.ppermute(start, axes, backward)  4.14 us
    pallas_call x1, Pallas kernels, shards(): pl.pallas_call(processor_kernel, out_shape=slim, in_specs=[in_vmem()] * 1...  3.34 us
    ppermute x1, starting transfers between devices, shards(): low = lax.ppermute(end, axes, forward)  3.32 us
    unnamed x19, local copies, waits for them, and re-layouts  2.54 us
    ppermute x1, waiting for transfers between devices, shards(): low = lax.ppermute(end, axes, forward)  2.11 us
  transfers between devices with their start and end apart: 21, of which 10 were waited for; matrix products, arithmetic and copies ran while one was open for 0% of the time, Pallas kernels for 0%

profile of v3, /device:TPU:15, one launch (start us, length us, event | category | flops | bytes accessed | tf_op | source)
XLA Modules:
  0.0 58.7 jit_solution(17796948290760703903)
XLA Ops:
  0.0 0.0 copy-start.6
  0.0 0.0 copy-start.7
  0.0 0.7 %copy-done.6 = s32[128,3]{0,1:T(4,128)S(1)} copy-done((s32[128,3]{0,1:T(4,128)S(1)}, s32[128,3]{0,1:T(4,128)}, u32[]{:S(2)}) %copy-start.6) | copy-done | bytes 1560
  0.7 0.0 copy-done.7
  0.7 0.0 copy-start.1
  0.7 1.0 %copy-done.1 = bf16[1,75264]{1,0:T(2,128)(2,1)S(1)} copy-done((bf16[1,75264]{1,0:T(2,128)(2,1)S(1)}, bf16[1,75264]{1,0:T(2,128)(2,1)}, u32[]{:S(2)}) %copy-start.1) | copy-done | bytes 150552
  1.6 0.0 copy-start.2
  1.7 0.7 %copy-done.2 = bf16[128,96]{0,1:T(8,128)(2,1)S(1)} copy-done((bf16[128,96]{0,1:T(8,128)(2,1)S(1)}, bf16[128,96]{0,1:T(8,128)(2,1)}, u32[]{:S(2)}) %copy-start.2) | copy-done | bytes 24600
  2.4 0.3 frames.1
  2.7 2.4 %collective-permute-start.9 = (bf16[176,512]{1,0:T(8,128)(2,1)S(1)}, bf16[176,512]{1,0:T(8,128)(2,1)S(1)}, u32[]{:S(2)}, u32[]{:S(2)}) collective-permute-start(bf16[176,512]{1,0:T(8,128)(2,1)S(1)} %get-tuple-element.16), channel_id=1, source_target_pairs={{0,16},{1,17},{2,18},{3,19},{4,20},{5,21},{6,22},{7,23},{8,24},{9,... | collective-permute-start | bytes 540680 | tf_op jit(solution)/shard_map/ppermute | solution.py:363
  5.1 0.2 collective-permute-start
  5.3 0.2 collective-permute-start.4
  5.5 7.6 %collective-permute-done.9 = bf16[176,512]{1,0:T(8,128)(2,1)S(1)} collective-permute-done((bf16[176,512]{1,0:T(8,128)(2,1)S(1)}, bf16[176,512]{1,0:T(8,128)(2,1)S(1)}, u32[]{:S(2)}, u32[]{:S(2)}) %collective-permute-start.9) | collective-permute-done | bytes 180256 | tf_op jit(solution)/shard_map/ppermute | solution.py:363
  13.1 0.3 collective-permute-start.10
  13.4 0.0 collective-permute-done
  13.4 0.0 collective-permute-start.5
  13.4 0.5 collective-permute-start.1
  14.0 2.2 %collective-permute-start.2 = (bf16[2,176,512]{2,1,0:T(8,128)(2,1)S(1)}, bf16[2,176,512]{2,1,0:T(8,128)(2,1)S(1)}, u32[]{:S(2)}, u32[]{:S(2)}) collective-permute-start(bf16[2,176,512]{2,1,0:T(8,128)(2,1)S(1)} %pad_maximum_fusion.refs_0_), channel_id=1, source_target_pairs={{0,1},{1,0},{2,3},{3,2},{4,5},{5,4},{6,7},{7,6},{8,9},{9,8},{10,11... | collective-permute-start | bytes 1081352 | tf_op jit(solution)/shard_map/ppermute | solution.py:363
  16.1 0.0 collective-permute-done.4
  16.1 0.4 collective-permute-start.14
  16.5 1.2 %collective-permute-done.10 = bf16[176,512]{1,0:T(8,128)(2,1)S(1)} collective-permute-done((bf16[176,512]{1,0:T(8,128)(2,1)S(1)}, bf16[176,512]{1,0:T(8,128)(2,1)S(1)}, u32[]{:S(2)}, u32[]{:S(2)}) %collective-permute-start.10) | collective-permute-done | bytes 180256 | tf_op jit(solution)/shard_map/ppermute | solution.py:363
  17.7 0.0 collective-permute-start.15
  17.8 0.9 %collective-permute-done.5 = bf16[176,512]{1,0:T(8,128)(2,1)S(1)} collective-permute-done((bf16[176,512]{1,0:T(8,128)(2,1)S(1)}, bf16[176,512]{1,0:T(8,128)(2,1)S(1)}, u32[]{:S(2)}, u32[]{:S(2)}) %collective-permute-start.5) | collective-permute-done | bytes 180256 | tf_op jit(solution)/shard_map/ppermute | solution.py:363
  18.7 0.3 collective-permute-start.11
  19.0 3.7 %collective-permute-done.14 = bf16[176,512]{1,0:T(8,128)(2,1)S(1)} collective-permute-done((bf16[176,512]{1,0:T(8,128)(2,1)S(1)}, bf16[176,512]{1,0:T(8,128)(2,1)S(1)}, u32[]{:S(2)}, u32[]{:S(2)}) %collective-permute-start.14) | collective-permute-done | bytes 180256 | tf_op jit(solution)/shard_map/ppermute | solution.py:363
  22.7 2.6 %collective-permute-start.12 = (bf16[2,176,512]{2,1,0:T(8,128)(2,1)S(1)}, bf16[2,176,512]{2,1,0:T(8,128)(2,1)S(1)}, u32[]{:S(2)}, u32[]{:S(2)}) collective-permute-start(bf16[2,176,512]{2,1,0:T(8,128)(2,1)S(1)} %pad_maximum_fusion.2.refs_8_), channel_id=1, source_target_pairs={{0,1},{1,0},{2,3},{3,2},{4,5},{5,4},{6,7},{7,6},{8,9},{9,8},{10,11... | collective-permute-start | bytes 1081352 | tf_op jit(solution)/shard_map/ppermute | solution.py:363
  25.3 1.3 %collective-permute-done.15 = bf16[176,512]{1,0:T(8,128)(2,1)S(1)} collective-permute-done((bf16[176,512]{1,0:T(8,128)(2,1)S(1)}, bf16[176,512]{1,0:T(8,128)(2,1)S(1)}, u32[]{:S(2)}, u32[]{:S(2)}) %collective-permute-start.15) | collective-permute-done | bytes 180256 | tf_op jit(solution)/shard_map/ppermute | solution.py:363
  26.6 1.3 %collective-permute-start.6 = (bf16[2,176,512]{2,1,0:T(8,128)(2,1)S(1)}, bf16[2,176,512]{2,1,0:T(8,128)(2,1)S(1)}, u32[]{:S(2)}, u32[]{:S(2)}) collective-permute-start(bf16[2,176,512]{2,1,0:T(8,128)(2,1)S(1)} %pad_maximum_fusion.1.refs_4_), channel_id=1, source_target_pairs={{0,2},{1,5},{2,0},{3,7},{4,6},{5,1},{6,4},{7,3},{8,10},{9,13},{10,... | collective-permute-start | bytes 1081352 | tf_op jit(solution)/shard_map/ppermute | solution.py:363
  27.8 0.0 copy-start
  27.8 0.0 copy-start.3
  27.8 0.0 copy-start.4
  27.8 0.0 copy-start.5
  27.9 0.0 collective-permute-done.1.refs_1_
  27.9 1.8 %collective-permute-start.7 = (bf16[2,176,512]{2,1,0:T(8,128)(2,1)S(1)}, bf16[2,176,512]{2,1,0:T(8,128)(2,1)S(1)}, u32[]{:S(2)}, u32[]{:S(2)}) collective-permute-start(bf16[2,176,512]{2,1,0:T(8,128)(2,1)S(1)} %pad_maximum_fusion.1.refs_4_), channel_id=1, source_target_pairs={{0,1},{1,0},{2,3},{3,2},{4,5},{5,4},{6,7},{7,6},{8,9},{9,8},{10,11... | collective-permute-start | bytes 1081352 | tf_op jit(solution)/shard_map/ppermute | solution.py:363
  29.7 0.0 collective-permute-done.2.refs_2_
  29.7 0.3 collective-permute-start.16
  30.0 0.0 collective-permute-done.11.refs_9_
  30.0 0.3 collective-permute-start.17
  30.3 2.8 %collective-permute-done.6.refs_5_ = bf16[2,176,512]{2,1,0:T(8,128)(2,1)S(1)} collective-permute-done((bf16[2,176,512]{2,1,0:T(8,128)(2,1)S(1)}, bf16[2,176,512]{2,1,0:T(8,128)(2,1)S(1)}, u32[]{:S(2)}, u32[]{:S(2)}) %collective-permute-start.6) | collective-permute-done | bytes 360480 | tf_op jit(solution)/shard_map/ppermute | solution.py:363
  33.1 2.3 %collective-permute-start.3 = (bf16[2,176,512]{2,1,0:T(8,128)(2,1)S(1)}, bf16[2,176,512]{2,1,0:T(8,128)(2,1)S(1)}, u32[]{:S(2)}, u32[]{:S(2)}) collective-permute-start(bf16[2,176,512]{2,1,0:T(8,128)(2,1)S(1)} %collective-permute-done.1.refs_1_), channel_id=1, source_target_pairs={{0,1},{1,0},{2,3},{3,2},{4,5},{5,4},{6,7},{7,6},{8,9},{9,8},{10,11... | collective-permute-start | bytes 1081352 | tf_op jit(solution)/shard_map/ppermute | solution.py:363
  35.5 0.0 collective-permute-done.12.refs_10_
  35.5 0.0 collective-permute-start.13
  35.5 0.0 collective-permute-done.7.refs_6_
  35.5 0.5 collective-permute-start.8
  36.0 1.0 %collective-permute-done.16.refs_13_ = bf16[2,176,512]{2,1,0:T(8,128)(2,1)S(1)} collective-permute-done((bf16[2,176,512]{2,1,0:T(8,128)(2,1)S(1)}, bf16[2,176,512]{2,1,0:T(8,128)(2,1)S(1)}, u32[]{:S(2)}, u32[]{:S(2)}) %collective-permute-start.16) | collective-permute-done | bytes 360480 | tf_op jit(solution)/shard_map/ppermute | solution.py:363
  37.0 2.3 %collective-permute-start.18 = (bf16[2,176,512]{2,1,0:T(8,128)(2,1)S(1)}, bf16[2,176,512]{2,1,0:T(8,128)(2,1)S(1)}, u32[]{:S(2)}, u32[]{:S(2)}) collective-permute-start(bf16[2,176,512]{2,1,0:T(8,128)(2,1)S(1)} %collective-permute-done.16.refs_13_), channel_id=1, source_target_pairs={{0,1},{1,0},{2,3},{3,2},{4,5},{5,4},{6,7},{7,6},{8,9},{9,8},{10,11... | collective-permute-start | bytes 1081352 | tf_op jit(solution)/shard_map/ppermute | solution.py:363
  39.3 0.0 collective-permute-done.3.refs_3_
  39.4 0.0 collective-permute-done.17.refs_14_
  39.4 0.0 collective-permute-done.13.refs_11_
  39.4 0.0 collective-permute-done.8.refs_7_
  39.4 1.3 %collective-permute-done.18.refs_15_ = bf16[2,176,512]{2,1,0:T(8,128)(2,1)S(1)} collective-permute-done((bf16[2,176,512]{2,1,0:T(8,128)(2,1)S(1)}, bf16[2,176,512]{2,1,0:T(8,128)(2,1)S(1)}, u32[]{:S(2)}, u32[]{:S(2)}) %collective-permute-start.18) | collective-permute-done | bytes 360480 | tf_op jit(solution)/shard_map/ppermute | solution.py:363
  40.7 0.0 copy-done
  40.7 0.0 copy-done.3
  40.7 0.0 copy-done.4
  40.7 0.0 copy-done.5
  40.7 0.0 copy-start.8
  40.7 5.0 %encoder.1 = (bf16[320,512]{1,0:T(8,128)(2,1)S(1)}, bf16[128,512]{1,0:T(8,128)(2,1)}, bf16[128,512]{1,0:T(8,128)(2,1)}, f32[320,512]{1,0:T(8,128)S(1)}, f32[320,...) custom-call(s32[1]{0:T(128)} %bitcast.me_ref, ...), custom_call_target="tpu_custom_call" | custom-call | tf_op jit(solution)/shard_map/encoder/pallas_call | solution.py:426
  45.7 3.3 %collective-permute-start.19 = (bf16[128,512]{1,0:T(8,128)(2,1)}, bf16[128,512]{1,0:T(8,128)(2,1)S(1)}, u32[]{:S(2)}, u32[]{:S(2)}) collective-permute-start(bf16[128,512]{1,0:T(8,128)(2,1)} %get-tuple-element.17), channel_id=1, source_target_pairs={{0,1},{1,2},{2,3},{3,4},{4,5},{5,6},{6,7},{7,8},{8,9},{9,10},{10,1... | collective-permute-start | bytes 393224 | tf_op jit(solution)/shard_map/ppermute | solution.py:443
  49.0 0.0 collective-permute-start.20
  49.0 0.0 copy-done.8
  49.0 0.1 copy.10.off_ref
  49.1 2.1 %collective-permute-done.19.low_ref = bf16[128,512]{1,0:T(8,128)(2,1)S(1)} collective-permute-done((bf16[128,512]{1,0:T(8,128)(2,1)}, bf16[128,512]{1,0:T(8,128)(2,1)S(1)}, u32[]{:S(2)}, u32[]{:S(2)}) %collective-permute-start.19) | collective-permute-done | bytes 131104 | tf_op jit(solution)/shard_map/ppermute | solution.py:443
  51.3 4.1 %collective-permute-done.20.high_ref = bf16[128,512]{1,0:T(8,128)(2,1)S(1)} collective-permute-done((bf16[128,512]{1,0:T(8,128)(2,1)}, bf16[128,512]{1,0:T(8,128)(2,1)S(1)}, u32[]{:S(2)}, u32[]{:S(2)}) %collective-permute-start.20) | collective-permute-done | bytes 131104 | tf_op jit(solution)/shard_map/ppermute | solution.py:444
  55.4 3.3 %processor.1 = bf16[320,512]{1,0:T(8,128)(2,1)} custom-call(bf16[128,512]{1,0:T(8,128)(2,1)S(1)} %collective-permute-done.19.low_ref, bf16[320,512]{1,0:T(8,128)(2,1)S(1)} %get-tuple-element.18.src_ref, bf16[128,512]{1,0:T(8,128)(2,1)S(1)} %collective-permute-done.20.high_ref, f32[320,512]{1,0:T(8,128)S(1)} %get-tuple-element.20.tgt_ref, ...), custom_call_target="tpu_custom_call" | custom-call | tf_op jit(solution)/shard_map/processor/pallas_call | solution.py:445
  (4 shorter events, 0.1 us)
Async XLA Ops:
  0.0 0.7 %copy-start.6 = (s32[128,3]{0,1:T(4,128)S(1)}, s32[128,3]{0,1:T(4,128)}, u32[]{:S(2)}) copy-start(s32[128,3]{0,1:T(4,128)} %param.11) | copy-start | bytes 4612
  0.0 0.7 %copy-start.7 = (s32[1,32]{1,0:T(1,128)S(1)}, s32[1,32]{1,0:T(1,128)}, u32[]{:S(2)}) copy-start(s32[1,32]{1,0:T(1,128)} %count_ref.1) | copy-start | bytes 388
  0.7 1.0 %copy-start.1 = (bf16[1,75264]{1,0:T(2,128)(2,1)S(1)}, bf16[1,75264]{1,0:T(2,128)(2,1)}, u32[]{:S(2)}) copy-start(bf16[1,75264]{1,0:T(2,128)(2,1)} %w_ref.1) | copy-start | bytes 451588
  1.6 0.7 %copy-start.2 = (bf16[128,96]{0,1:T(8,128)(2,1)S(1)}, bf16[128,96]{0,1:T(8,128)(2,1)}, u32[]{:S(2)}) copy-start(bf16[128,96]{0,1:T(8,128)(2,1)} %param.9) | copy-start | bytes 73732
  2.7 10.4 %collective-permute-start.9 = (bf16[176,512]{1,0:T(8,128)(2,1)S(1)}, bf16[176,512]{1,0:T(8,128)(2,1)S(1)}, u32[]{:S(2)}, u32[]{:S(2)}) collective-permute-start(bf16[176,512]{1,0:T(8,128)(2,1)S(1)} %get-tuple-element.16), channel_id=1, source_target_pairs={{0,16},{1,17},{2,18},{3,19},{4,20},{5,21},{6,22},{7,23},{8,24},{9,... | collective-permute-start | bytes 540680 | tf_op jit(solution)/shard_map/ppermute | solution.py:363
  5.1 8.3 %collective-permute-start = (bf16[176,512]{1,0:T(8,128)(2,1)S(1)}, bf16[176,512]{1,0:T(8,128)(2,1)S(1)}, u32[]{:S(2)}, u32[]{:S(2)}) collective-permute-start(bf16[176,512]{1,0:T(8,128)(2,1)S(1)} %get-tuple-element.15), channel_id=1, source_target_pairs={{0,4},{1,3},{2,6},{3,1},{4,0},{5,7},{6,2},{7,5},{8,12},{9,11},{10,... | collective-permute-start | bytes 540680 | tf_op jit(solution)/shard_map/ppermute | solution.py:363
  5.3 10.8 %collective-permute-start.4 = (bf16[176,512]{1,0:T(8,128)(2,1)S(1)}, bf16[176,512]{1,0:T(8,128)(2,1)S(1)}, u32[]{:S(2)}, u32[]{:S(2)}) collective-permute-start(bf16[176,512]{1,0:T(8,128)(2,1)S(1)} %get-tuple-element.15), channel_id=1, source_target_pairs={{0,8},{1,9},{2,10},{3,11},{4,12},{5,13},{6,14},{7,15},{8,0},{9,1},... | collective-permute-start | bytes 540680 | tf_op jit(solution)/shard_map/ppermute | solution.py:363
  13.1 4.6 %collective-permute-start.10 = (bf16[176,512]{1,0:T(8,128)(2,1)S(1)}, bf16[176,512]{1,0:T(8,128)(2,1)S(1)}, u32[]{:S(2)}, u32[]{:S(2)}) collective-permute-start(bf16[176,512]{1,0:T(8,128)(2,1)S(1)} %collective-permute-done.9), channel_id=1, source_target_pairs={{0,4},{1,3},{2,6},{3,1},{4,0},{5,7},{6,2},{7,5},{8,12},{9,11},{10,... | collective-permute-start | bytes 540680 | tf_op jit(solution)/shard_map/ppermute | solution.py:363
  13.4 5.3 %collective-permute-start.5 = (bf16[176,512]{1,0:T(8,128)(2,1)S(1)}, bf16[176,512]{1,0:T(8,128)(2,1)S(1)}, u32[]{:S(2)}, u32[]{:S(2)}) collective-permute-start(bf16[176,512]{1,0:T(8,128)(2,1)S(1)} %collective-permute-done), channel_id=1, source_target_pairs={{0,8},{1,9},{2,10},{3,11},{4,12},{5,13},{6,14},{7,15},{8,0},{9,1},... | collective-permute-start | bytes 540680 | tf_op jit(solution)/shard_map/ppermute | solution.py:363
  13.4 14.5 %collective-permute-start.1 = (bf16[2,176,512]{2,1,0:T(8,128)(2,1)S(1)}, bf16[2,176,512]{2,1,0:T(8,128)(2,1)S(1)}, u32[]{:S(2)}, u32[]{:S(2)}) collective-permute-start(bf16[2,176,512]{2,1,0:T(8,128)(2,1)S(1)} %pad_maximum_fusion.refs_0_), channel_id=1, source_target_pairs={{0,2},{1,5},{2,0},{3,7},{4,6},{5,1},{6,4},{7,3},{8,10},{9,13},{10,... | collective-permute-start | bytes 1081352 | tf_op jit(solution)/shard_map/ppermute | solution.py:363
  14.0 15.7 %collective-permute-start.2 = (bf16[2,176,512]{2,1,0:T(8,128)(2,1)S(1)}, bf16[2,176,512]{2,1,0:T(8,128)(2,1)S(1)}, u32[]{:S(2)}, u32[]{:S(2)}) collective-permute-start(bf16[2,176,512]{2,1,0:T(8,128)(2,1)S(1)} %pad_maximum_fusion.refs_0_), channel_id=1, source_target_pairs={{0,1},{1,0},{2,3},{3,2},{4,5},{5,4},{6,7},{7,6},{8,9},{9,8},{10,11... | collective-permute-start | bytes 1081352 | tf_op jit(solution)/shard_map/ppermute | solution.py:363
  16.1 6.6 %collective-permute-start.14 = (bf16[176,512]{1,0:T(8,128)(2,1)S(1)}, bf16[176,512]{1,0:T(8,128)(2,1)S(1)}, u32[]{:S(2)}, u32[]{:S(2)}) collective-permute-start(bf16[176,512]{1,0:T(8,128)(2,1)S(1)} %collective-permute-done.9), channel_id=1, source_target_pairs={{0,8},{1,9},{2,10},{3,11},{4,12},{5,13},{6,14},{7,15},{8,0},{9,1},... | collective-permute-start | bytes 540680 | tf_op jit(solution)/shard_map/ppermute | solution.py:363
  17.7 8.8 %collective-permute-start.15 = (bf16[176,512]{1,0:T(8,128)(2,1)S(1)}, bf16[176,512]{1,0:T(8,128)(2,1)S(1)}, u32[]{:S(2)}, u32[]{:S(2)}) collective-permute-start(bf16[176,512]{1,0:T(8,128)(2,1)S(1)} %collective-permute-done.10), channel_id=1, source_target_pairs={{0,8},{1,9},{2,10},{3,11},{4,12},{5,13},{6,14},{7,15},{8,0},{9,1},... | collective-permute-start | bytes 540680 | tf_op jit(solution)/shard_map/ppermute | solution.py:363
  18.7 11.3 %collective-permute-start.11 = (bf16[2,176,512]{2,1,0:T(8,128)(2,1)S(1)}, bf16[2,176,512]{2,1,0:T(8,128)(2,1)S(1)}, u32[]{:S(2)}, u32[]{:S(2)}) collective-permute-start(bf16[2,176,512]{2,1,0:T(8,128)(2,1)S(1)} %pad_maximum_fusion.2.refs_8_), channel_id=1, source_target_pairs={{0,2},{1,5},{2,0},{3,7},{4,6},{5,1},{6,4},{7,3},{8,10},{9,13},{10,... | collective-permute-start | bytes 1081352 | tf_op jit(solution)/shard_map/ppermute | solution.py:363
  22.7 12.8 %collective-permute-start.12 = (bf16[2,176,512]{2,1,0:T(8,128)(2,1)S(1)}, bf16[2,176,512]{2,1,0:T(8,128)(2,1)S(1)}, u32[]{:S(2)}, u32[]{:S(2)}) collective-permute-start(bf16[2,176,512]{2,1,0:T(8,128)(2,1)S(1)} %pad_maximum_fusion.2.refs_8_), channel_id=1, source_target_pairs={{0,1},{1,0},{2,3},{3,2},{4,5},{5,4},{6,7},{7,6},{8,9},{9,8},{10,11... | collective-permute-start | bytes 1081352 | tf_op jit(solution)/shard_map/ppermute | solution.py:363
  26.6 6.6 %collective-permute-start.6 = (bf16[2,176,512]{2,1,0:T(8,128)(2,1)S(1)}, bf16[2,176,512]{2,1,0:T(8,128)(2,1)S(1)}, u32[]{:S(2)}, u32[]{:S(2)}) collective-permute-start(bf16[2,176,512]{2,1,0:T(8,128)(2,1)S(1)} %pad_maximum_fusion.1.refs_4_), channel_id=1, source_target_pairs={{0,2},{1,5},{2,0},{3,7},{4,6},{5,1},{6,4},{7,3},{8,10},{9,13},{10,... | collective-permute-start | bytes 1081352 | tf_op jit(solution)/shard_map/ppermute | solution.py:363
  27.8 12.8 %copy-start = (bf16[320,512]{1,0:T(8,128)(2,1)S(1)}, bf16[320,512]{1,0:T(8,128)(2,1)}, u32[]{:S(2)}) copy-start(bf16[320,512]{1,0:T(8,128)(2,1)} %refs_16_.1) | copy-start | bytes 983044
  27.8 12.8 %copy-start.3 = (f32[2,512]{1,0:T(2,128)S(1)}, f32[2,512]{1,0:T(2,128)}, u32[]{:S(2)}) copy-start(f32[2,512]{1,0:T(2,128)} %gain_ref.1) | copy-start | bytes 12292
  27.8 12.8 %copy-start.4 = (f32[2,512]{1,0:T(2,128)S(1)}, f32[2,512]{1,0:T(2,128)}, u32[]{:S(2)}) copy-start(f32[2,512]{1,0:T(2,128)} %refs_17_.1) | copy-start | bytes 12292
  27.8 12.8 %copy-start.5 = (f32[2,512]{1,0:T(2,128)S(1)}, f32[2,512]{1,0:T(2,128)}, u32[]{:S(2)}) copy-start(f32[2,512]{1,0:T(2,128)} %refs_18_.1) | copy-start | bytes 12292
  27.9 7.6 %collective-permute-start.7 = (bf16[2,176,512]{2,1,0:T(8,128)(2,1)S(1)}, bf16[2,176,512]{2,1,0:T(8,128)(2,1)S(1)}, u32[]{:S(2)}, u32[]{:S(2)}) collective-permute-start(bf16[2,176,512]{2,1,0:T(8,128)(2,1)S(1)} %pad_maximum_fusion.1.refs_4_), channel_id=1, source_target_pairs={{0,1},{1,0},{2,3},{3,2},{4,5},{5,4},{6,7},{7,6},{8,9},{9,8},{10,11... | collective-permute-start | bytes 1081352 | tf_op jit(solution)/shard_map/ppermute | solution.py:363
  29.7 7.3 %collective-permute-start.16 = (bf16[2,176,512]{2,1,0:T(8,128)(2,1)S(1)}, bf16[2,176,512]{2,1,0:T(8,128)(2,1)S(1)}, u32[]{:S(2)}, u32[]{:S(2)}) collective-permute-start(bf16[2,176,512]{2,1,0:T(8,128)(2,1)S(1)} %pad_maximum_fusion.3.refs_12_), channel_id=1, source_target_pairs={{0,2},{1,5},{2,0},{3,7},{4,6},{5,1},{6,4},{7,3},{8,10},{9,13},{10,... | collective-permute-start | bytes 1081352 | tf_op jit(solution)/shard_map/ppermute | solution.py:363
  30.0 9.4 %collective-permute-start.17 = (bf16[2,176,512]{2,1,0:T(8,128)(2,1)S(1)}, bf16[2,176,512]{2,1,0:T(8,128)(2,1)S(1)}, u32[]{:S(2)}, u32[]{:S(2)}) collective-permute-start(bf16[2,176,512]{2,1,0:T(8,128)(2,1)S(1)} %pad_maximum_fusion.3.refs_12_), channel_id=1, source_target_pairs={{0,1},{1,0},{2,3},{3,2},{4,5},{5,4},{6,7},{7,6},{8,9},{9,8},{10,11... | collective-permute-start | bytes 1081352 | tf_op jit(solution)/shard_map/ppermute | solution.py:363
  33.1 6.2 %collective-permute-start.3 = (bf16[2,176,512]{2,1,0:T(8,128)(2,1)S(1)}, bf16[2,176,512]{2,1,0:T(8,128)(2,1)S(1)}, u32[]{:S(2)}, u32[]{:S(2)}) collective-permute-start(bf16[2,176,512]{2,1,0:T(8,128)(2,1)S(1)} %collective-permute-done.1.refs_1_), channel_id=1, source_target_pairs={{0,1},{1,0},{2,3},{3,2},{4,5},{5,4},{6,7},{7,6},{8,9},{9,8},{10,11... | collective-permute-start | bytes 1081352 | tf_op jit(solution)/shard_map/ppermute | solution.py:363
  35.5 3.9 %collective-permute-start.13 = (bf16[2,176,512]{2,1,0:T(8,128)(2,1)S(1)}, bf16[2,176,512]{2,1,0:T(8,128)(2,1)S(1)}, u32[]{:S(2)}, u32[]{:S(2)}) collective-permute-start(bf16[2,176,512]{2,1,0:T(8,128)(2,1)S(1)} %collective-permute-done.11.refs_9_), channel_id=1, source_target_pairs={{0,1},{1,0},{2,3},{3,2},{4,5},{5,4},{6,7},{7,6},{8,9},{9,8},{10,11... | collective-permute-start | bytes 1081352 | tf_op jit(solution)/shard_map/ppermute | solution.py:363
  35.5 3.9 %collective-permute-start.8 = (bf16[2,176,512]{2,1,0:T(8,128)(2,1)S(1)}, bf16[2,176,512]{2,1,0:T(8,128)(2,1)S(1)}, u32[]{:S(2)}, u32[]{:S(2)}) collective-permute-start(bf16[2,176,512]{2,1,0:T(8,128)(2,1)S(1)} %collective-permute-done.6.refs_5_), channel_id=1, source_target_pairs={{0,1},{1,0},{2,3},{3,2},{4,5},{5,4},{6,7},{7,6},{8,9},{9,8},{10,11... | collective-permute-start | bytes 1081352 | tf_op jit(solution)/shard_map/ppermute | solution.py:363
  37.0 3.6 %collective-permute-start.18 = (bf16[2,176,512]{2,1,0:T(8,128)(2,1)S(1)}, bf16[2,176,512]{2,1,0:T(8,128)(2,1)S(1)}, u32[]{:S(2)}, u32[]{:S(2)}) collective-permute-start(bf16[2,176,512]{2,1,0:T(8,128)(2,1)S(1)} %collective-permute-done.16.refs_13_), channel_id=1, source_target_pairs={{0,1},{1,0},{2,3},{3,2},{4,5},{5,4},{6,7},{7,6},{8,9},{9,8},{10,11... | collective-permute-start | bytes 1081352 | tf_op jit(solution)/shard_map/ppermute | solution.py:363
  40.7 8.3 %copy-start.8 = (s32[320,6]{0,1:T(8,128)S(1)}, s32[320,6]{0,1:T(8,128)}, u32[]{:S(2)}) copy-start(s32[320,6]{0,1:T(8,128)} %param.13) | copy-start | bytes 23044
  45.7 5.6 %collective-permute-start.19 = (bf16[128,512]{1,0:T(8,128)(2,1)}, bf16[128,512]{1,0:T(8,128)(2,1)S(1)}, u32[]{:S(2)}, u32[]{:S(2)}) collective-permute-start(bf16[128,512]{1,0:T(8,128)(2,1)} %get-tuple-element.17), channel_id=1, source_target_pairs={{0,1},{1,2},{2,3},{3,4},{4,5},{5,6},{6,7},{7,8},{8,9},{9,10},{10,1... | collective-permute-start | bytes 393224 | tf_op jit(solution)/shard_map/ppermute | solution.py:443
  49.0 6.4 %collective-permute-start.20 = (bf16[128,512]{1,0:T(8,128)(2,1)}, bf16[128,512]{1,0:T(8,128)(2,1)S(1)}, u32[]{:S(2)}, u32[]{:S(2)}) collective-permute-start(bf16[128,512]{1,0:T(8,128)(2,1)} %get-tuple-element.19), channel_id=1, source_target_pairs={{1,0},{2,1},{3,2},{4,3},{5,4},{6,5},{7,6},{8,7},{9,8},{10,9},{11,1... | collective-permute-start | bytes 393224 | tf_op jit(solution)/shard_map/ppermute | solution.py:444

commit v4 on v3

--- a/solution.py
+++ b/solution.py
@@ -182,8 +182,21 @@
     return pl.BlockSpec(memory_space=pltpu.SMEM)
 
 
-def frame_kernel(me_ref, w_ref, val_ref, node_ref, count_ref, *refs):
-    outs, (turned, slots, rows, frame) = refs[:2], refs[2:]
+def in_any():
+    return pl.BlockSpec(memory_space=pltpu.HBM)
+
+
+def frame_kernel(me_ref, *refs):
+    outs = refs[4:6]
+    w_ref, val_ref, node_ref, count_ref, turned, slots, rows, frame, sems = refs[6:]
+    copies = [
+        pltpu.make_async_copy(src, dst, sems.at[i])
+        for i, (src, dst) in enumerate(zip(refs[:4], (w_ref, val_ref, node_ref, count_ref)))
+    ]
+    for copy in copies:
+        copy.start()
+    for copy in copies:
+        copy.wait()
     me = me_ref[0]
     breadth, n_slots = val_ref.shape
     senders = count_ref.shape[1]
@@ -197,29 +210,45 @@
     place = (iota((1, n_slots), 1) % capacity).astype(F32)
     code = jnp.where(place < live, node_ref[...].astype(F32) - DEAD, DEAD)
     turned[:breadth, :] = val_ref[...].astype(F32)
-    line = iota((n_slots - breadth, n_slots), 0)
+    feature = iota((n_slots - breadth, n_slots), 0)
     tail = jnp.zeros((n_slots - breadth, n_slots), F32)
     for k in range(OBS_EDGES):
-        tail = jnp.where(line == k, code[k : k + 1, :], tail)
+        tail = jnp.where(feature == k, code[k : k + 1, :], tail)
     turned[breadth:, :] = tail
     slots[...] = turned[...].T
     for j in range(capacity):
         rows[:, 128 * j : 128 * (j + 1)] = slots[pl.ds(j, senders, stride=capacity), :]
     start = pl.multiple_of(jnp.where(phase >= 8, 0, FRAME - 16), 8)
+    lane = iota((8, 128), 1)
+    line = iota((8, 128), 0)
+    used = breadth + OBS_EDGES
+    quarter = breadth // capacity
+
+    def block(plane):
+        before = slots[pl.ds(pl.multiple_of(lax.rem(32 * plane + 120, 128), 8), 8), :]
+        after = slots[pl.ds(pl.multiple_of(lax.rem(32 * plane + 32, 128), 8), 8), :]
+        extra = pltpu.roll(jnp.where(line < 4, after, before), 4, 0)
+        base = rows[pl.ds(pl.multiple_of(8 * plane, 8), 8), :]
+        parts = []
+        for g in range(capacity):
+            moved = pltpu.roll(extra, (used - quarter * g) % 128, 1)
+            keep = (lane >= used) & (lane < used + quarter)
+            parts.append(jnp.where(keep, moved, base[:, 128 * g : 128 * (g + 1)]))
+        keep = (lane >= used + quarter) & (lane < used + quarter + OBS_EDGES)
+        parts[0] = jnp.where(keep, pltpu.roll(extra, used + quarter - breadth, 1), parts[0])
+        return jnp.concatenate(parts, axis=1)
+
     for flip in range(2):
-        for ref, spot, plane in (
-            (frame, start, (me >> 3) ^ (2 * flip)),
-            (frame, FRAME - 8, (me >> 3) ^ (2 * flip + 1)),
-        ):
-            ref[pl.ds(spot, 8), :] = rows[pl.ds(pl.multiple_of(plane * 8, 8), 8), :]
+        frame[pl.ds(start, 8), :] = block((me >> 3) ^ (2 * flip))
+        frame[FRAME - 8 :, :] = block((me >> 3) ^ (2 * flip + 1))
         outs[flip][...] = frame[...].astype(BF)
 
 
-def encoder_kernel(me_ref, *refs):
+def layer_kernel(me_ref, *refs):
     pieces = refs[:16]
-    init_ref, edge_ref, nbias_ref, gain_ref = refs[16:20]
-    src_ref, start_ref, end_ref, tgt_ref, rest_ref, first_ref, pagg_ref, pout_ref = refs[20:28]
-    big, edges, obs, enc, proc = refs[28:]
+    low_ref, init_ref, high_ref, off_ref, edge_ref, nbias_ref, gain_ref, out_ref = refs[16:24]
+    big, edges, obs, enc, proc, ext, wide = refs[24:]
+    count = init_ref.shape[0]
     height = WROWS
     me = me_ref[0]
     core = me & 1
@@ -265,79 +294,87 @@
     p0 = CH + 4 * D
     g0 = CH + 7 * D
     u0 = CH + 8 * D
-    pagg_ref[...] = big[g0 : g0 + D, :]
-    pout_ref[...] = big[u0 : u0 + D, :]
-    out = iota((256, 256), 0)
-    two = (iota((256, 256), 1) == 2 * (out & 127) + (out >> 7)).astype(BF)
-    for j in range(D // 128):
-        got = mm(two, big[e0 + 256 * j : e0 + 256 * (j + 1), :]).astype(BF)
-        enc[0, 128 * j : 128 * (j + 1), :] = got[:128]
-        enc[1, 128 * j : 128 * (j + 1), :] = got[128:]
-    out = iota((384, 384), 0)
-    three = (iota((384, 384), 1) == 3 * (out & 127) + (out >> 7)).astype(BF)
-    for j in range(D // 128):
-        got = mm(three, big[p0 + 384 * j : p0 + 384 * (j + 1), :]).astype(BF)
-        for m in range(3):
-            proc[m, 128 * j : 128 * (j + 1), :] = got[128 * m : 128 * (m + 1)]
-    init = init_ref[...]
-    query = mm(init, enc[0]) + edge_ref[0:1, :]
-    slots = jnp.concatenate([obs[j, pl.ds(me & 7, 32, stride=8), :] for j in range(4)], axis=0)
-    embedded = mm(slots[:, :CH].astype(BF), big[0:CH, :]).astype(BF).astype(F32)
-    node_ids = iota((slots.shape[0], init.shape[0]), 1)
-    picks = []
-    for k in range(OBS_EDGES):
-        code = slots[:, CH + k : CH + k + 1] + DEAD
-        picks.append((node_ids == code.astype(jnp.int32)).astype(F32))
-    select = jnp.concatenate(picks, axis=0)
-    spread = select.astype(BF)
-    q_high = query.astype(BF)
-    q_low = (query - q_high.astype(F32)).astype(BF)
-    picked = mm(spread, q_high) + mm(spread, q_low)
-    message = silu(jnp.concatenate([embedded] * OBS_EDGES, axis=0) + picked)
-    collect = select.T.astype(BF)
-    m_high = message.astype(BF)
-    m_low = (message - m_high.astype(F32)).astype(BF)
-    gathered = (mm(collect, m_high) + mm(collect, m_low)).astype(BF)
+    for base, fold, dest in ((e0, 2, enc), (p0, 3, proc)):
+        for j in range(4):
+            lanes = slice(128 * j, 128 * (j + 1))
+            wide[j, 0 : fold * D, :] = big[base : base + fold * D, lanes].astype(F32)
+            for m in range(fold):
+                dest[m, :, lanes] = wide[j, pl.ds(m, D, stride=fold), :].astype(BF)
+    init = jnp.concatenate([low_ref[...], init_ref[...], high_ref[...]], axis=0)
+    query = (mm(init, enc[0]) + edge_ref[0:1, :]).astype(BF)
+    spot = me & 7
+    lane = iota((32, 128), 1)
+    used = CH + OBS_EDGES
+    quarter = CH // 4
+
+    def direct(row):
+        return jnp.concatenate([obs[j, pl.ds(row, 32, stride=8), :] for j in range(4)], axis=0)
+
+    def spilled(row):
+        groups = []
+        for j in range(4):
+            near = obs[0, pl.ds(row + j, 32, stride=8), :]
+            slot = pltpu.roll(near, (CH - used - quarter) % 128, 1)
+            for g in range(4):
+                part = near if g == 0 else obs[g, pl.ds(row + j, 32, stride=8), :]
+                keep = (lane >= quarter * g) & (lane < quarter * (g + 1))
+                slot = jnp.where(keep, pltpu.roll(part, (quarter * g - used) % 128, 1), slot)
+            groups.append(slot)
+        return jnp.concatenate(groups, axis=0)
+
+    before = jnp.where(spot > 0, direct(jnp.maximum(spot - 1, 0)), spilled(0))
+    after = jnp.where(spot < 7, direct(jnp.minimum(spot + 1, 7)), spilled(4))
+    rows = [before, direct(spot), after]
+    per = rows[0].shape[0]
+    joined = jnp.concatenate(rows, axis=0)
+    embedded = mm(joined[:, :CH].astype(BF), big[0:CH, :]).astype(BF).astype(F32)
+    sums = []
+    for part, shift, top, size in (
+        (0, count - HALO, 0, HALO),
+        (1, 0, HALO, count),
+        (2, 0, HALO + count, HALO),
+    ):
+        slots = rows[part]
+        embeds = embedded[per * part : per * (part + 1)]
+        node_ids = iota((slots.shape[0], size), 1)
+        picks = []
+        for k in range(OBS_EDGES):
+            code = slots[:, CH + k : CH + k + 1] + (DEAD - shift)
+            picks.append((node_ids == code.astype(jnp.int32)).astype(F32))
+        select = jnp.concatenate(picks, axis=0)
+        picked = mm(select.astype(BF), query[top : top + size])
+        message = silu(jnp.concatenate([embeds] * OBS_EDGES, axis=0) + picked)
+        sums.append(mm(select.T.astype(BF), message.astype(BF)).astype(BF))
+    gathered = jnp.concatenate(sums, axis=0)
     hidden = silu(
         mm(init, enc[1]) + mm(gathered, big[a0 : a0 + D, :]) + nbias_ref[0:1, :]
     ).astype(BF)
     first = (
         init.astype(F32) + layer_norm(mm(hidden, big[o0 : o0 + D, :]), gain_ref[0:1, :])
     ).astype(BF)
-    first_ref[...] = first
-    sources = mm(first, proc[0]).astype(BF)
-    src_ref[...] = sources
-    start_ref[...] = sources[:HALO]
-    end_ref[...] = sources[sources.shape[0] - HALO :]
-    tgt_ref[...] = mm(first, proc[1]) + edge_ref[1:2, :]
-    rest_ref[...] = mm(first, proc[2]) + nbias_ref[1:2, :]
-
-
-def processor_kernel(
-    low_ref, src_ref, high_ref, tgt_ref, rest_ref, first_ref, off_ref, pagg_ref, pout_ref, gain_ref, out_ref, ext
-):
-    count = src_ref.shape[0]
-    ext[0:HALO, :] = low_ref[...]
-    ext[HALO : HALO + count, :] = src_ref[...]
-    ext[HALO + count :, :] = high_ref[...]
+    ext[...] = mm(first, proc[0]).astype(BF)
+    first = first[HALO : HALO + count]
     block = count // 2
     span = block + 2 * HALO
     cols = iota((block, span), 1) - iota((block, span), 0) - HALO
+    target = mm(first, proc[1]) + edge_ref[1:2, :]
     sums = []
     for at in range(0, count, block):
         select = jnp.concatenate(
             [(cols == off_ref[at : at + block, k : k + 1]).astype(F32) for k in range(DEG)], axis=0
         ).astype(BF)
         picked = mm(select, ext[at : at + span, :])
-        target = tgt_ref[at : at + block, :]
-        total = silu(picked[:block] + target)
+        base = target[at : at + block]
+        total = silu(picked[:block] + base)
         for k in range(1, DEG):
-            total = total + silu(picked[block * k : block * (k + 1)] + target)
+            total = total + silu(picked[block * k : block * (k + 1)] + base)
         sums.append(total)
-    pooled = jnp.concatenate(sums, axis=0)
-    hidden = silu(rest_ref[...] + mm(pooled.astype(BF), pagg_ref[...])).astype(BF)
+    pooled = jnp.concatenate(sums, axis=0).astype(BF)
+    hidden = silu(
+        mm(first, proc[2]) + nbias_ref[1:2, :] + mm(pooled, big[g0 : g0 + D, :])
+    ).astype(BF)
     out_ref[...] = (
-        first_ref[...].astype(F32) + layer_norm(mm(hidden, pout_ref[...]), gain_ref[1:2, :])
+        first.astype(F32) + layer_norm(mm(hidden, big[u0 : u0 + D, :]), gain_ref[1:2, :])
     ).astype(BF)
 
 
@@ -356,12 +393,16 @@
     )
 
 
-def spread_weights(near, far):
+def spread_weights(near, far, init):
     axes = ("patch", "lat")
+    count = init.shape[0]
+    ring = [(i, (i + 1) % 32) for i in range(32)]
 
     def move(block, masks):
         return lax.ppermute(block, axes, [(i, i ^ masks[i & 1]) for i in range(32)])
 
+    low = lax.ppermute(init[count - HALO :], axes, ring)
+    high = lax.ppermute(init[:HALO], axes, [(j, i) for i, j in ring])
     beside = move(near, (4, 2))
     opposite = move(far, (16, 16))
     aside = move(opposite, (4, 2))
@@ -375,7 +416,7 @@
         pair = jnp.stack([unit, twin])
         other = move(pair, (2, 4))
         pieces += [pair, other, move(pair, (1, 1)), move(other, (1, 1))]
-    return pieces
+    return pieces + [low, init, high]
 
 
 def shards(
@@ -407,50 +448,40 @@
     frames = pl.pallas_call(
         frame_kernel,
         out_shape=[jax.ShapeDtypeStruct((FRAME, D), BF)] * 2,
-        in_specs=[in_smem()] + [in_vmem()] * 4,
+        in_specs=[in_smem()] + [in_any()] * 4,
         out_specs=[in_vmem()] * 2,
         scratch_shapes=[
+            pltpu.VMEM(weights_flat.shape, BF),
+            pltpu.VMEM(obs_values.shape[::-1], BF),
+            pltpu.VMEM(obs_node.shape[::-1], jnp.int32),
+            pltpu.VMEM(obs_count.shape, jnp.int32),
             pltpu.VMEM((128, 128), F32),
             pltpu.VMEM((128, 128), F32),
             pltpu.VMEM((32, D), F32),
             pltpu.VMEM((FRAME, D), F32),
+            pltpu.SemaphoreType.DMA((4,)),
         ],
-        compiler_params=pltpu.CompilerParams(vmem_limit_bytes=8 << 20),
+        compiler_params=pltpu.CompilerParams(vmem_limit_bytes=60 << 20),
         name="frames",
     )(me, weights_flat, obs_values.T, obs_node.T, obs_count)
-    pieces = spread_weights(*frames)
-    wide = jax.ShapeDtypeStruct((count, D), F32)
-    slim = jax.ShapeDtypeStruct((count, D), BF)
-    square = jax.ShapeDtypeStruct((D, D), BF)
-    side = jax.ShapeDtypeStruct((HALO, D), BF)
-    sources, start, end, target, rest, first, w_pagg, w_pout = pl.pallas_call(
-        encoder_kernel,
-        out_shape=[slim, side, side, wide, wide, slim, square, square],
-        in_specs=[in_smem()] + [in_vmem()] * 16 + [in_vmem()] * 4,
-        out_specs=[in_vmem()] * 8,
+    pieces = spread_weights(*frames, mesh_init)
+    return pl.pallas_call(
+        layer_kernel,
+        out_shape=jax.ShapeDtypeStruct((count, D), BF),
+        in_specs=[in_smem()] + [in_vmem()] * 23,
+        out_specs=in_vmem(),
         scratch_shapes=[
             pltpu.VMEM((32 * WROWS, D), BF),
             pltpu.VMEM((32, 3 * TILE, D), BF),
             pltpu.VMEM((4, 256, 128), F32),
             pltpu.VMEM((2, D, D), BF),
             pltpu.VMEM((3, D, D), BF),
+            pltpu.VMEM((count + 2 * HALO, D), BF),
+            pltpu.VMEM((4, 3 * D, 128), F32),
         ],
-        compiler_params=pltpu.CompilerParams(vmem_limit_bytes=34 << 20),
-        name="encoder",
-    )(me, *pieces, mesh_init, edge_bias, node_bias, norm_gain)
-    forward = [(i, (i + 1) % 32) for i in range(32)]
-    backward = [(j, i) for i, j in forward]
-    low = lax.ppermute(end, axes, forward)
-    high = lax.ppermute(start, axes, backward)
-    return pl.pallas_call(
-        processor_kernel,
-        out_shape=slim,
-        in_specs=[in_vmem()] * 10,
-        out_specs=in_vmem(),
-        scratch_shapes=[pltpu.VMEM((count + 2 * HALO, D), BF)],
-        compiler_params=pltpu.CompilerParams(vmem_limit_bytes=20 << 20),
-        name="processor",
-    )(low, sources, high, target, rest, first, mesh_offset, w_pagg, w_pout, norm_gain)
+        compiler_params=pltpu.CompilerParams(vmem_limit_bytes=40 << 20),
+        name="layer",
+    )(me, *pieces, mesh_offset, edge_bias, node_bias, norm_gain)
 
 
 def solution(mesh):

time: 59.9 us -> 61.7 us (1.030)
  the two profiles are of different devices: /device:TPU:15 before, /device:TPU:0 now
where the time goes in v4:
time: 61.7 us; the launch traced here: 61.5 us
  waiting for transfers between devices  28.3 us (46%)
  starting transfers between devices  17.4 us (28%)
  Pallas kernels  12 us (19%)
  local copies, waits for them, and re-layouts  3.48 us (6%)
    ppermute x19, waiting for transfers between devices, move(): return lax.ppermute(block, axes, [(i, i ^ masks[i & 1]) for i in range(32)])  22.4 us
    ppermute x19, starting transfers between devices, move(): return lax.ppermute(block, axes, [(i, i ^ masks[i & 1]) for i in range(32)])  15.9 us
    pallas_call x1, Pallas kernels, shards(): pl.pallas_call(layer_kernel, out_shape=jax.ShapeDtypeStruct((count, D), B...  9.75 us
    ppermute x1, waiting for transfers between devices, spread_weights(): low = lax.ppermute(init[count - HALO:], axes, ring)  5.35 us
    unnamed x21, local copies, waits for them, and re-layouts  3.46 us
    pallas_call x1, Pallas kernels, shards(): pl.pallas_call(frame_kernel, out_shape=[jax.ShapeDtypeStruct((FRAME, D),...  2.23 us
    ppermute x1, starting transfers between devices, spread_weights(): high = lax.ppermute(init[:HALO], axes, [(j, i) for i, j in ring])  1.51 us
  transfers between devices with their start and end apart: 21, of which 11 were waited for; matrix products, arithmetic and copies ran while one was open for 0% of the time, Pallas kernels for 0%

profile of v4, /device:TPU:0, one launch (start us, length us, event | category | flops | bytes accessed | tf_op | source)
XLA Modules:
  0.0 61.5 jit_solution(30266142647396869)
XLA Ops:
  0.0 0.0 copy-start
  0.0 2.2 %frames.1 = (bf16[176,512]{1,0:T(8,128)(2,1)}, bf16[176,512]{1,0:T(8,128)(2,1)}) custom-call(s32[1]{0:T(128)} %bitcast.me_ref, bf16[1,75264]{1,0:T(2,128)(2,1)} %refs_0_.1, bf16[96,128]{1,0:T(8,128)(2,1)} %bitcast.19, s32[3,128]{1,0:T(4,128)} %bitcast.20, s32[1,32]{1,0:T(1,128)} %refs_3_.1), custom_call_target="tpu_custom_call" | custom-call | tf_op jit(solution)/shard_map/frames/pallas_call | solution.py:448
  2.2 4.1 %collective-permute-start.9 = (bf16[176,512]{1,0:T(8,128)(2,1)}, bf16[176,512]{1,0:T(8,128)(2,1)S(1)}, u32[]{:S(2)}, u32[]{:S(2)}) collective-permute-start(bf16[176,512]{1,0:T(8,128)(2,1)} %get-tuple-element.8), channel_id=1, source_target_pairs={{0,16},{1,17},{2,18},{3,19},{4,20},{5,21},{6,22},{7,23},{8,24},{9,... | collective-permute-start | bytes 540680 | tf_op jit(solution)/shard_map/ppermute | solution.py:402
  6.4 0.0 copy-start.8
  6.4 1.6 %collective-permute-start.4 = (bf16[176,512]{1,0:T(8,128)(2,1)}, bf16[176,512]{1,0:T(8,128)(2,1)S(1)}, u32[]{:S(2)}, u32[]{:S(2)}) collective-permute-start(bf16[176,512]{1,0:T(8,128)(2,1)} %get-tuple-element.7), channel_id=1, source_target_pairs={{0,8},{1,9},{2,10},{3,11},{4,12},{5,13},{6,14},{7,15},{8,0},{9,1},... | collective-permute-start | bytes 540680 | tf_op jit(solution)/shard_map/ppermute | solution.py:402
  8.0 1.5 %collective-permute-start = (bf16[176,512]{1,0:T(8,128)(2,1)}, bf16[176,512]{1,0:T(8,128)(2,1)S(1)}, u32[]{:S(2)}, u32[]{:S(2)}) collective-permute-start(bf16[176,512]{1,0:T(8,128)(2,1)} %get-tuple-element.7), channel_id=1, source_target_pairs={{0,4},{1,3},{2,6},{3,1},{4,0},{5,7},{6,2},{7,5},{8,12},{9,11},{10,... | collective-permute-start | bytes 540680 | tf_op jit(solution)/shard_map/ppermute | solution.py:402
  9.4 5.7 %collective-permute-done.9 = bf16[176,512]{1,0:T(8,128)(2,1)S(1)} collective-permute-done((bf16[176,512]{1,0:T(8,128)(2,1)}, bf16[176,512]{1,0:T(8,128)(2,1)S(1)}, u32[]{:S(2)}, u32[]{:S(2)}) %collective-permute-start.9) | collective-permute-done | bytes 180256 | tf_op jit(solution)/shard_map/ppermute | solution.py:402
  15.1 1.5 %collective-permute-start.10 = (bf16[176,512]{1,0:T(8,128)(2,1)S(1)}, bf16[176,512]{1,0:T(8,128)(2,1)S(1)}, u32[]{:S(2)}, u32[]{:S(2)}) collective-permute-start(bf16[176,512]{1,0:T(8,128)(2,1)S(1)} %collective-permute-done.9), channel_id=1, source_target_pairs={{0,4},{1,3},{2,6},{3,1},{4,0},{5,7},{6,2},{7,5},{8,12},{9,11},{10,... | collective-permute-start | bytes 540680 | tf_op jit(solution)/shard_map/ppermute | solution.py:402
  16.6 0.0 copy-done
  16.7 0.7 %collective-permute-start.14 = (bf16[176,512]{1,0:T(8,128)(2,1)S(1)}, bf16[176,512]{1,0:T(8,128)(2,1)S(1)}, u32[]{:S(2)}, u32[]{:S(2)}) collective-permute-start(bf16[176,512]{1,0:T(8,128)(2,1)S(1)} %collective-permute-done.9), channel_id=1, source_target_pairs={{0,8},{1,9},{2,10},{3,11},{4,12},{5,13},{6,14},{7,15},{8,0},{9,1},... | collective-permute-start | bytes 540680 | tf_op jit(solution)/shard_map/ppermute | solution.py:402
  17.4 0.0 collective-permute-done
  17.4 1.4 %collective-permute-start.5 = (bf16[176,512]{1,0:T(8,128)(2,1)S(1)}, bf16[176,512]{1,0:T(8,128)(2,1)S(1)}, u32[]{:S(2)}, u32[]{:S(2)}) collective-permute-start(bf16[176,512]{1,0:T(8,128)(2,1)S(1)} %collective-permute-done), channel_id=1, source_target_pairs={{0,8},{1,9},{2,10},{3,11},{4,12},{5,13},{6,14},{7,15},{8,0},{9,1},... | collective-permute-start | bytes 540680 | tf_op jit(solution)/shard_map/ppermute | solution.py:402
  18.8 0.0 copy-done.8
  18.8 0.1 collective-permute-start.2
  18.9 0.0 collective-permute-done.4
  18.9 1.6 %collective-permute-start.1 = (bf16[2,176,512]{2,1,0:T(8,128)(2,1)S(1)}, bf16[2,176,512]{2,1,0:T(8,128)(2,1)S(1)}, u32[]{:S(2)}, u32[]{:S(2)}) collective-permute-start(bf16[2,176,512]{2,1,0:T(8,128)(2,1)S(1)} %pad_maximum_fusion.refs_0_), channel_id=1, source_target_pairs={{0,2},{1,5},{2,0},{3,7},{4,6},{5,1},{6,4},{7,3},{8,10},{9,13},{10,... | collective-permute-start | bytes 1081352 | tf_op jit(solution)/shard_map/ppermute | solution.py:402
  20.5 0.1 collective-permute-done.10
  20.6 0.7 %collective-permute-start.15 = (bf16[176,512]{1,0:T(8,128)(2,1)S(1)}, bf16[176,512]{1,0:T(8,128)(2,1)S(1)}, u32[]{:S(2)}, u32[]{:S(2)}) collective-permute-start(bf16[176,512]{1,0:T(8,128)(2,1)S(1)} %collective-permute-done.10), channel_id=1, source_target_pairs={{0,8},{1,9},{2,10},{3,11},{4,12},{5,13},{6,14},{7,15},{8,0},{9,1},... | collective-permute-start | bytes 540680 | tf_op jit(solution)/shard_map/ppermute | solution.py:402
  21.4 2.8 %collective-permute-done.14 = bf16[176,512]{1,0:T(8,128)(2,1)S(1)} collective-permute-done((bf16[176,512]{1,0:T(8,128)(2,1)S(1)}, bf16[176,512]{1,0:T(8,128)(2,1)S(1)}, u32[]{:S(2)}, u32[]{:S(2)}) %collective-permute-start.14) | collective-permute-done | bytes 180256 | tf_op jit(solution)/shard_map/ppermute | solution.py:402
  24.2 1.5 %collective-permute-start.20 = (bf16[128,512]{1,0:T(8,128)(2,1)S(1)}, bf16[128,512]{1,0:T(8,128)(2,1)S(1)}, u32[]{:S(2)}, u32[]{:S(2)}) collective-permute-start(bf16[128,512]{1,0:T(8,128)(2,1)S(1)} %get-tuple-element.9), channel_id=1, source_target_pairs={{1,0},{2,1},{3,2},{4,3},{5,4},{6,5},{7,6},{8,7},{9,8},{10,9},{11,1... | collective-permute-start | bytes 393224 | tf_op jit(solution)/shard_map/ppermute | solution.py:405
  25.7 2.0 %collective-permute-done.5 = bf16[176,512]{1,0:T(8,128)(2,1)S(1)} collective-permute-done((bf16[176,512]{1,0:T(8,128)(2,1)S(1)}, bf16[176,512]{1,0:T(8,128)(2,1)S(1)}, u32[]{:S(2)}, u32[]{:S(2)}) %collective-permute-start.5) | collective-permute-done | bytes 180256 | tf_op jit(solution)/shard_map/ppermute | solution.py:402
  27.7 0.0 collective-permute-start.19
  27.7 1.9 %collective-permute-done.15 = bf16[176,512]{1,0:T(8,128)(2,1)S(1)} collective-permute-done((bf16[176,512]{1,0:T(8,128)(2,1)S(1)}, bf16[176,512]{1,0:T(8,128)(2,1)S(1)}, u32[]{:S(2)}, u32[]{:S(2)}) %collective-permute-start.15) | collective-permute-done | bytes 180256 | tf_op jit(solution)/shard_map/ppermute | solution.py:402
  29.6 0.0 collective-permute-start.7
  29.6 0.0 copy-start.9
  29.7 0.0 copy-start.5
  29.7 0.0 copy-start.6
  29.7 0.0 copy-start.7
  29.7 0.6 collective-permute-done.20.refs_18_
  30.3 0.2 collective-permute-start.6
  30.4 5.3 %collective-permute-done.19.refs_16_ = bf16[128,512]{1,0:T(8,128)(2,1)S(1)} collective-permute-done((bf16[128,512]{1,0:T(8,128)(2,1)S(1)}, bf16[128,512]{1,0:T(8,128)(2,1)S(1)}, u32[]{:S(2)}, u32[]{:S(2)}) %collective-permute-start.19) | collective-permute-done | bytes 131104 | tf_op jit(solution)/shard_map/ppermute | solution.py:404
  35.8 0.0 copy-start.3
  35.8 0.7 %copy-done.3 = bf16[128,512]{1,0:T(8,128)(2,1)} copy-done((bf16[128,512]{1,0:T(8,128)(2,1)}, bf16[128,512]{1,0:T(8,128)(2,1)S(1)}, u32[]{:S(2)}) %copy-start.3) | copy-done | bytes 131096
  36.4 0.0 collective-permute-start.12
  36.4 0.0 collective-permute-done.2.refs_2_
  36.4 0.0 collective-permute-start.11
  36.4 0.0 collective-permute-done.1.refs_1_
  36.5 2.0 %collective-permute-start.16 = (bf16[2,176,512]{2,1,0:T(8,128)(2,1)S(1)}, bf16[2,176,512]{2,1,0:T(8,128)(2,1)}, u32[]{:S(2)}, u32[]{:S(2)}) collective-permute-start(bf16[2,176,512]{2,1,0:T(8,128)(2,1)S(1)} %pad_maximum_fusion.3.refs_12_), channel_id=1, source_target_pairs={{0,2},{1,5},{2,0},{3,7},{4,6},{5,1},{6,4},{7,3},{8,10},{9,13},{10,... | collective-permute-start | bytes 1081352 | tf_op jit(solution)/shard_map/ppermute | solution.py:402
  38.5 0.0 collective-permute-done.7.refs_6_
  38.5 0.0 collective-permute-start.17
  38.5 0.6 %collective-permute-done.6.refs_5_ = bf16[2,176,512]{2,1,0:T(8,128)(2,1)S(1)} collective-permute-done((bf16[2,176,512]{2,1,0:T(8,128)(2,1)S(1)}, bf16[2,176,512]{2,1,0:T(8,128)(2,1)S(1)}, u32[]{:S(2)}, u32[]{:S(2)}) %collective-permute-start.6) | collective-permute-done | bytes 360480 | tf_op jit(solution)/shard_map/ppermute | solution.py:402
  39.1 0.0 collective-permute-start.3
  39.1 0.0 collective-permute-done.12.refs_10_
  39.1 0.0 copy-start.1
  39.1 0.8 %copy-done.1 = bf16[2,176,512]{2,1,0:T(8,128)(2,1)} copy-done((bf16[2,176,512]{2,1,0:T(8,128)(2,1)}, bf16[2,176,512]{2,1,0:T(8,128)(2,1)S(1)}, u32[]{:S(2)}) %copy-start.1) | copy-done | bytes 360472
  39.9 0.5 collective-permute-start.8
  40.4 3.6 %collective-permute-done.11.refs_9_ = bf16[2,176,512]{2,1,0:T(8,128)(2,1)} collective-permute-done((bf16[2,176,512]{2,1,0:T(8,128)(2,1)S(1)}, bf16[2,176,512]{2,1,0:T(8,128)(2,1)}, u32[]{:S(2)}, u32[]{:S(2)}) %collective-permute-start.11) | collective-permute-done | bytes 360480 | tf_op jit(solution)/shard_map/ppermute | solution.py:402
  44.0 0.0 collective-permute-start.13
  44.0 3.9 %collective-permute-done.16.refs_13_ = bf16[2,176,512]{2,1,0:T(8,128)(2,1)} collective-permute-done((bf16[2,176,512]{2,1,0:T(8,128)(2,1)S(1)}, bf16[2,176,512]{2,1,0:T(8,128)(2,1)}, u32[]{:S(2)}, u32[]{:S(2)}) %collective-permute-start.16) | collective-permute-done | bytes 360480 | tf_op jit(solution)/shard_map/ppermute | solution.py:402
  47.8 0.0 collective-permute-start.18
  47.8 0.0 copy-done.9
  47.8 0.1 copy.10.refs_19_
  48.0 0.0 collective-permute-done.3.refs_3_
  48.0 0.0 collective-permute-done.17.refs_14_
  48.0 0.0 collective-permute-done.8.refs_7_
  48.0 0.0 collective-permute-done.13.refs_11_
  48.0 1.8 %collective-permute-done.18.refs_15_ = bf16[2,176,512]{2,1,0:T(8,128)(2,1)} collective-permute-done((bf16[2,176,512]{2,1,0:T(8,128)(2,1)}, bf16[2,176,512]{2,1,0:T(8,128)(2,1)}, u32[]{:S(2)}, u32[]{:S(2)}) %collective-permute-start.18) | collective-permute-done | bytes 360480 | tf_op jit(solution)/shard_map/ppermute | solution.py:402
  49.9 0.0 copy-done.5
  49.9 0.0 copy-done.6
  49.9 0.0 copy-done.7
  49.9 0.0 copy-start.2
  49.9 1.0 %copy-done.2 = bf16[2,176,512]{2,1,0:T(8,128)(2,1)S(1)} copy-done((bf16[2,176,512]{2,1,0:T(8,128)(2,1)S(1)}, bf16[2,176,512]{2,1,0:T(8,128)(2,1)}, u32[]{:S(2)}) %copy-start.2) | copy-done | bytes 360472
  50.9 0.9 %copy-done.4 = bf16[128,512]{1,0:T(8,128)(2,1)S(1)} copy-done((bf16[128,512]{1,0:T(8,128)(2,1)S(1)}, bf16[128,512]{1,0:T(8,128)(2,1)}, u32[]{:S(2)}) %copy-start.4) | copy-done | bytes 131096
  51.8 9.7 %layer.1 = bf16[320,512]{1,0:T(8,128)(2,1)} custom-call(s32[1]{0:T(128)} %bitcast.me_ref, bf16[2,176,512]{2,1,0:T(8,128)(2,1)S(1)} %pad_maximum_fusion.refs_0_, bf16[2,176,512]{2,1,0:T(8,128)(2,1)S(1)} %collective-permute-done.1.refs_1_, bf16[2,176,512]{2,1,0:T(8,128)(2,1)S(1)} %collective-permute-done.2.refs_2_, ...), custom_call_target="tpu_custom_call" | custom-call | tf_op jit(solution)/shard_map/layer/pallas_call | solution.py:468
  (6 shorter events, 0.2 us)
Async XLA Ops:
  0.0 16.6 %copy-start = (bf16[320,512]{1,0:T(8,128)(2,1)S(1)}, bf16[320,512]{1,0:T(8,128)(2,1)}, u32[]{:S(2)}) copy-start(bf16[320,512]{1,0:T(8,128)(2,1)} %refs_17_.1) | copy-start | bytes 983044
  2.2 12.9 %collective-permute-start.9 = (bf16[176,512]{1,0:T(8,128)(2,1)}, bf16[176,512]{1,0:T(8,128)(2,1)S(1)}, u32[]{:S(2)}, u32[]{:S(2)}) collective-permute-start(bf16[176,512]{1,0:T(8,128)(2,1)} %get-tuple-element.8), channel_id=1, source_target_pairs={{0,16},{1,17},{2,18},{3,19},{4,20},{5,21},{6,22},{7,23},{8,24},{9,... | collective-permute-start | bytes 540680 | tf_op jit(solution)/shard_map/ppermute | solution.py:402
  6.4 12.4 %copy-start.8 = (bf16[176,512]{1,0:T(8,128)(2,1)S(1)}, bf16[176,512]{1,0:T(8,128)(2,1)}, u32[]{:S(2)}) copy-start(bf16[176,512]{1,0:T(8,128)(2,1)} %get-tuple-element.7) | copy-start | bytes 540676
  6.4 12.5 %collective-permute-start.4 = (bf16[176,512]{1,0:T(8,128)(2,1)}, bf16[176,512]{1,0:T(8,128)(2,1)S(1)}, u32[]{:S(2)}, u32[]{:S(2)}) collective-permute-start(bf16[176,512]{1,0:T(8,128)(2,1)} %get-tuple-element.7), channel_id=1, source_target_pairs={{0,8},{1,9},{2,10},{3,11},{4,12},{5,13},{6,14},{7,15},{8,0},{9,1},... | collective-permute-start | bytes 540680 | tf_op jit(solution)/shard_map/ppermute | solution.py:402
  8.0 9.5 %collective-permute-start = (bf16[176,512]{1,0:T(8,128)(2,1)}, bf16[176,512]{1,0:T(8,128)(2,1)S(1)}, u32[]{:S(2)}, u32[]{:S(2)}) collective-permute-start(bf16[176,512]{1,0:T(8,128)(2,1)} %get-tuple-element.7), channel_id=1, source_target_pairs={{0,4},{1,3},{2,6},{3,1},{4,0},{5,7},{6,2},{7,5},{8,12},{9,11},{10,... | collective-permute-start | bytes 540680 | tf_op jit(solution)/shard_map/ppermute | solution.py:402
  15.1 5.5 %collective-permute-start.10 = (bf16[176,512]{1,0:T(8,128)(2,1)S(1)}, bf16[176,512]{1,0:T(8,128)(2,1)S(1)}, u32[]{:S(2)}, u32[]{:S(2)}) collective-permute-start(bf16[176,512]{1,0:T(8,128)(2,1)S(1)} %collective-permute-done.9), channel_id=1, source_target_pairs={{0,4},{1,3},{2,6},{3,1},{4,0},{5,7},{6,2},{7,5},{8,12},{9,11},{10,... | collective-permute-start | bytes 540680 | tf_op jit(solution)/shard_map/ppermute | solution.py:402
  16.7 7.5 %collective-permute-start.14 = (bf16[176,512]{1,0:T(8,128)(2,1)S(1)}, bf16[176,512]{1,0:T(8,128)(2,1)S(1)}, u32[]{:S(2)}, u32[]{:S(2)}) collective-permute-start(bf16[176,512]{1,0:T(8,128)(2,1)S(1)} %collective-permute-done.9), channel_id=1, source_target_pairs={{0,8},{1,9},{2,10},{3,11},{4,12},{5,13},{6,14},{7,15},{8,0},{9,1},... | collective-permute-start | bytes 540680 | tf_op jit(solution)/shard_map/ppermute | solution.py:402
  17.4 10.3 %collective-permute-start.5 = (bf16[176,512]{1,0:T(8,128)(2,1)S(1)}, bf16[176,512]{1,0:T(8,128)(2,1)S(1)}, u32[]{:S(2)}, u32[]{:S(2)}) collective-permute-start(bf16[176,512]{1,0:T(8,128)(2,1)S(1)} %collective-permute-done), channel_id=1, source_target_pairs={{0,8},{1,9},{2,10},{3,11},{4,12},{5,13},{6,14},{7,15},{8,0},{9,1},... | collective-permute-start | bytes 540680 | tf_op jit(solution)/shard_map/ppermute | solution.py:402
  18.8 17.6 %collective-permute-start.2 = (bf16[2,176,512]{2,1,0:T(8,128)(2,1)S(1)}, bf16[2,176,512]{2,1,0:T(8,128)(2,1)S(1)}, u32[]{:S(2)}, u32[]{:S(2)}) collective-permute-start(bf16[2,176,512]{2,1,0:T(8,128)(2,1)S(1)} %pad_maximum_fusion.refs_0_), channel_id=1, source_target_pairs={{0,1},{1,0},{2,3},{3,2},{4,5},{5,4},{6,7},{7,6},{8,9},{9,8},{10,11... | collective-permute-start | bytes 1081352 | tf_op jit(solution)/shard_map/ppermute | solution.py:402
  18.9 17.6 %collective-permute-start.1 = (bf16[2,176,512]{2,1,0:T(8,128)(2,1)S(1)}, bf16[2,176,512]{2,1,0:T(8,128)(2,1)S(1)}, u32[]{:S(2)}, u32[]{:S(2)}) collective-permute-start(bf16[2,176,512]{2,1,0:T(8,128)(2,1)S(1)} %pad_maximum_fusion.refs_0_), channel_id=1, source_target_pairs={{0,2},{1,5},{2,0},{3,7},{4,6},{5,1},{6,4},{7,3},{8,10},{9,13},{10,... | collective-permute-start | bytes 1081352 | tf_op jit(solution)/shard_map/ppermute | solution.py:402
  20.6 9.0 %collective-permute-start.15 = (bf16[176,512]{1,0:T(8,128)(2,1)S(1)}, bf16[176,512]{1,0:T(8,128)(2,1)S(1)}, u32[]{:S(2)}, u32[]{:S(2)}) collective-permute-start(bf16[176,512]{1,0:T(8,128)(2,1)S(1)} %collective-permute-done.10), channel_id=1, source_target_pairs={{0,8},{1,9},{2,10},{3,11},{4,12},{5,13},{6,14},{7,15},{8,0},{9,1},... | collective-permute-start | bytes 540680 | tf_op jit(solution)/shard_map/ppermute | solution.py:402
  24.2 6.1 %collective-permute-start.20 = (bf16[128,512]{1,0:T(8,128)(2,1)S(1)}, bf16[128,512]{1,0:T(8,128)(2,1)S(1)}, u32[]{:S(2)}, u32[]{:S(2)}) collective-permute-start(bf16[128,512]{1,0:T(8,128)(2,1)S(1)} %get-tuple-element.9), channel_id=1, source_target_pairs={{1,0},{2,1},{3,2},{4,3},{5,4},{6,5},{7,6},{8,7},{9,8},{10,9},{11,1... | collective-permute-start | bytes 393224 | tf_op jit(solution)/shard_map/ppermute | solution.py:405
  27.7 8.1 %collective-permute-start.19 = (bf16[128,512]{1,0:T(8,128)(2,1)S(1)}, bf16[128,512]{1,0:T(8,128)(2,1)S(1)}, u32[]{:S(2)}, u32[]{:S(2)}) collective-permute-start(bf16[128,512]{1,0:T(8,128)(2,1)S(1)} %get-tuple-element.10), channel_id=1, source_target_pairs={{0,1},{1,2},{2,3},{3,4},{4,5},{5,6},{6,7},{7,8},{8,9},{9,10},{10,1... | collective-permute-start | bytes 393224 | tf_op jit(solution)/shard_map/ppermute | solution.py:404
  29.6 8.9 %collective-permute-start.7 = (bf16[2,176,512]{2,1,0:T(8,128)(2,1)S(1)}, bf16[2,176,512]{2,1,0:T(8,128)(2,1)S(1)}, u32[]{:S(2)}, u32[]{:S(2)}) collective-permute-start(bf16[2,176,512]{2,1,0:T(8,128)(2,1)S(1)} %pad_maximum_fusion.1.refs_4_), channel_id=1, source_target_pairs={{0,1},{1,0},{2,3},{3,2},{4,5},{5,4},{6,7},{7,6},{8,9},{9,8},{10,11... | collective-permute-start | bytes 1081352 | tf_op jit(solution)/shard_map/ppermute | solution.py:402
  29.6 18.2 %copy-start.9 = (s32[320,6]{0,1:T(8,128)S(1)}, s32[320,6]{0,1:T(8,128)}, u32[]{:S(2)}) copy-start(s32[320,6]{0,1:T(8,128)} %param.13) | copy-start | bytes 23044
  29.7 20.2 %copy-start.5 = (f32[2,512]{1,0:T(2,128)S(1)}, f32[2,512]{1,0:T(2,128)}, u32[]{:S(2)}) copy-start(f32[2,512]{1,0:T(2,128)} %refs_20_.1) | copy-start | bytes 12292
  29.7 20.2 %copy-start.6 = (f32[2,512]{1,0:T(2,128)S(1)}, f32[2,512]{1,0:T(2,128)}, u32[]{:S(2)}) copy-start(f32[2,512]{1,0:T(2,128)} %refs_21_.1) | copy-start | bytes 12292
  29.7 20.2 %copy-start.7 = (f32[2,512]{1,0:T(2,128)S(1)}, f32[2,512]{1,0:T(2,128)}, u32[]{:S(2)}) copy-start(f32[2,512]{1,0:T(2,128)} %refs_22_.1) | copy-start | bytes 12292
  30.3 8.8 %collective-permute-start.6 = (bf16[2,176,512]{2,1,0:T(8,128)(2,1)S(1)}, bf16[2,176,512]{2,1,0:T(8,128)(2,1)S(1)}, u32[]{:S(2)}, u32[]{:S(2)}) collective-permute-start(bf16[2,176,512]{2,1,0:T(8,128)(2,1)S(1)} %pad_maximum_fusion.1.refs_4_), channel_id=1, source_target_pairs={{0,2},{1,5},{2,0},{3,7},{4,6},{5,1},{6,4},{7,3},{8,10},{9,13},{10,... | collective-permute-start | bytes 1081352 | tf_op jit(solution)/shard_map/ppermute | solution.py:402
  35.8 0.7 %copy-start.3 = (bf16[128,512]{1,0:T(8,128)(2,1)}, bf16[128,512]{1,0:T(8,128)(2,1)S(1)}, u32[]{:S(2)}) copy-start(bf16[128,512]{1,0:T(8,128)(2,1)S(1)} %collective-permute-done.19.refs_16_) | copy-start | bytes 393220
  36.4 2.7 %collective-permute-start.12 = (bf16[2,176,512]{2,1,0:T(8,128)(2,1)S(1)}, bf16[2,176,512]{2,1,0:T(8,128)(2,1)S(1)}, u32[]{:S(2)}, u32[]{:S(2)}) collective-permute-start(bf16[2,176,512]{2,1,0:T(8,128)(2,1)S(1)} %pad_maximum_fusion.2.refs_8_), channel_id=1, source_target_pairs={{0,1},{1,0},{2,3},{3,2},{4,5},{5,4},{6,7},{7,6},{8,9},{9,8},{10,11... | collective-permute-start | bytes 1081352 | tf_op jit(solution)/shard_map/ppermute | solution.py:402
  36.4 7.5 %collective-permute-start.11 = (bf16[2,176,512]{2,1,0:T(8,128)(2,1)S(1)}, bf16[2,176,512]{2,1,0:T(8,128)(2,1)}, u32[]{:S(2)}, u32[]{:S(2)}) collective-permute-start(bf16[2,176,512]{2,1,0:T(8,128)(2,1)S(1)} %pad_maximum_fusion.2.refs_8_), channel_id=1, source_target_pairs={{0,2},{1,5},{2,0},{3,7},{4,6},{5,1},{6,4},{7,3},{8,10},{9,13},{10,... | collective-permute-start | bytes 1081352 | tf_op jit(solution)/shard_map/ppermute | solution.py:402
  36.5 11.4 %collective-permute-start.16 = (bf16[2,176,512]{2,1,0:T(8,128)(2,1)S(1)}, bf16[2,176,512]{2,1,0:T(8,128)(2,1)}, u32[]{:S(2)}, u32[]{:S(2)}) collective-permute-start(bf16[2,176,512]{2,1,0:T(8,128)(2,1)S(1)} %pad_maximum_fusion.3.refs_12_), channel_id=1, source_target_pairs={{0,2},{1,5},{2,0},{3,7},{4,6},{5,1},{6,4},{7,3},{8,10},{9,13},{10,... | collective-permute-start | bytes 1081352 | tf_op jit(solution)/shard_map/ppermute | solution.py:402
  38.5 9.5 %collective-permute-start.17 = (bf16[2,176,512]{2,1,0:T(8,128)(2,1)S(1)}, bf16[2,176,512]{2,1,0:T(8,128)(2,1)}, u32[]{:S(2)}, u32[]{:S(2)}) collective-permute-start(bf16[2,176,512]{2,1,0:T(8,128)(2,1)S(1)} %pad_maximum_fusion.3.refs_12_), channel_id=1, source_target_pairs={{0,1},{1,0},{2,3},{3,2},{4,5},{5,4},{6,7},{7,6},{8,9},{9,8},{10,11... | collective-permute-start | bytes 1081352 | tf_op jit(solution)/shard_map/ppermute | solution.py:402
  39.1 8.9 %collective-permute-start.3 = (bf16[2,176,512]{2,1,0:T(8,128)(2,1)S(1)}, bf16[2,176,512]{2,1,0:T(8,128)(2,1)}, u32[]{:S(2)}, u32[]{:S(2)}) collective-permute-start(bf16[2,176,512]{2,1,0:T(8,128)(2,1)S(1)} %collective-permute-done.1.refs_1_), channel_id=1, source_target_pairs={{0,1},{1,0},{2,3},{3,2},{4,5},{5,4},{6,7},{7,6},{8,9},{9,8},{10,11... | collective-permute-start | bytes 1081352 | tf_op jit(solution)/shard_map/ppermute | solution.py:402
  39.1 0.8 %copy-start.1 = (bf16[2,176,512]{2,1,0:T(8,128)(2,1)}, bf16[2,176,512]{2,1,0:T(8,128)(2,1)S(1)}, u32[]{:S(2)}) copy-start(bf16[2,176,512]{2,1,0:T(8,128)(2,1)S(1)} %collective-permute-done.12.refs_10_) | copy-start | bytes 1081348
  39.9 8.1 %collective-permute-start.8 = (bf16[2,176,512]{2,1,0:T(8,128)(2,1)S(1)}, bf16[2,176,512]{2,1,0:T(8,128)(2,1)}, u32[]{:S(2)}, u32[]{:S(2)}) collective-permute-start(bf16[2,176,512]{2,1,0:T(8,128)(2,1)S(1)} %collective-permute-done.6.refs_5_), channel_id=1, source_target_pairs={{0,1},{1,0},{2,3},{3,2},{4,5},{5,4},{6,7},{7,6},{8,9},{9,8},{10,11... | collective-permute-start | bytes 1081352 | tf_op jit(solution)/shard_map/ppermute | solution.py:402
  44.0 4.0 %collective-permute-start.13 = (bf16[2,176,512]{2,1,0:T(8,128)(2,1)}, bf16[2,176,512]{2,1,0:T(8,128)(2,1)}, u32[]{:S(2)}, u32[]{:S(2)}) collective-permute-start(bf16[2,176,512]{2,1,0:T(8,128)(2,1)} %collective-permute-done.11.refs_9_), channel_id=1, source_target_pairs={{0,1},{1,0},{2,3},{3,2},{4,5},{5,4},{6,7},{7,6},{8,9},{9,8},{10,11... | collective-permute-start | bytes 1081352 | tf_op jit(solution)/shard_map/ppermute | solution.py:402
  47.8 2.0 %collective-permute-start.18 = (bf16[2,176,512]{2,1,0:T(8,128)(2,1)}, bf16[2,176,512]{2,1,0:T(8,128)(2,1)}, u32[]{:S(2)}, u32[]{:S(2)}) collective-permute-start(bf16[2,176,512]{2,1,0:T(8,128)(2,1)} %collective-permute-done.16.refs_13_), channel_id=1, source_target_pairs={{0,1},{1,0},{2,3},{3,2},{4,5},{5,4},{6,7},{7,6},{8,9},{9,8},{10,11... | collective-permute-start | bytes 1081352 | tf_op jit(solution)/shard_map/ppermute | solution.py:402
  49.9 1.0 %copy-start.2 = (bf16[2,176,512]{2,1,0:T(8,128)(2,1)S(1)}, bf16[2,176,512]{2,1,0:T(8,128)(2,1)}, u32[]{:S(2)}) copy-start(bf16[2,176,512]{2,1,0:T(8,128)(2,1)} %copy-done.1) | copy-start | bytes 1081348
  50.8 0.9 %copy-start.4 = (bf16[128,512]{1,0:T(8,128)(2,1)S(1)}, bf16[128,512]{1,0:T(8,128)(2,1)}, u32[]{:S(2)}) copy-start(bf16[128,512]{1,0:T(8,128)(2,1)} %copy-done.3) | copy-start | bytes 393220

commit v5 on v4

--- a/solution.py
+++ b/solution.py
@@ -294,12 +294,21 @@
     p0 = CH + 4 * D
     g0 = CH + 7 * D
     u0 = CH + 8 * D
-    for base, fold, dest in ((e0, 2, enc), (p0, 3, proc)):
-        for j in range(4):
-            lanes = slice(128 * j, 128 * (j + 1))
-            wide[j, 0 : fold * D, :] = big[base : base + fold * D, lanes].astype(F32)
-            for m in range(fold):
-                dest[m, :, lanes] = wide[j, pl.ds(m, D, stride=fold), :].astype(BF)
+
+    def unfold(base, fold, dest, j):
+        lanes = slice(128 * j, 128 * (j + 1))
+        wide[j, 0 : fold * D, :] = big[base : base + fold * D, lanes].astype(F32)
+        for m in range(fold):
+            dest[m, :, lanes] = wide[j, pl.ds(m, D, stride=fold), :].astype(BF)
+
+    out = iota((256, 256), 0)
+    two = (iota((256, 256), 1) == 2 * (out & 127) + (out >> 7)).astype(BF)
+    for j in range(D // 128):
+        got = mm(two, big[e0 + 256 * j : e0 + 256 * (j + 1), :]).astype(BF)
+        enc[0, 128 * j : 128 * (j + 1), :] = got[:128]
+        enc[1, 128 * j : 128 * (j + 1), :] = got[128:]
+        if j == 1:
+            unfold(p0, 3, proc, 0)
     init = jnp.concatenate([low_ref[...], init_ref[...], high_ref[...]], axis=0)
     query = (mm(init, enc[0]) + edge_ref[0:1, :]).astype(BF)
     spot = me & 7
@@ -345,6 +354,7 @@
         picked = mm(select.astype(BF), query[top : top + size])
         message = silu(jnp.concatenate([embeds] * OBS_EDGES, axis=0) + picked)
         sums.append(mm(select.T.astype(BF), message.astype(BF)).astype(BF))
+        unfold(p0, 3, proc, part + 1)
     gathered = jnp.concatenate(sums, axis=0)
     hidden = silu(
         mm(init, enc[1]) + mm(gathered, big[a0 : a0 + D, :]) + nbias_ref[0:1, :]
@@ -357,17 +367,18 @@
     block = count // 2
     span = block + 2 * HALO
     cols = iota((block, span), 1) - iota((block, span), 0) - HALO
-    target = mm(first, proc[1]) + edge_ref[1:2, :]
+    target = 0.5 * (mm(first, proc[1]) + edge_ref[1:2, :])
     sums = []
     for at in range(0, count, block):
         select = jnp.concatenate(
-            [(cols == off_ref[at : at + block, k : k + 1]).astype(F32) for k in range(DEG)], axis=0
+            [jnp.where(cols == off_ref[at : at + block, k : k + 1], 0.5, 0.0) for k in range(DEG)], axis=0
         ).astype(BF)
         picked = mm(select, ext[at : at + span, :])
         base = target[at : at + block]
-        total = silu(picked[:block] + base)
-        for k in range(1, DEG):
-            total = total + silu(picked[block * k : block * (k + 1)] + base)
+        total = jnp.zeros((block, D), F32)
+        for k in range(DEG):
+            half = picked[block * k : block * (k + 1)] + base
+            total = total + (half + half * jnp.tanh(half))
         sums.append(total)
     pooled = jnp.concatenate(sums, axis=0).astype(BF)
     hidden = silu(

time: 61.7 us -> 61.4 us (level)
  no operation moved by 1% of the time
where the time goes in v5:
time: 61.4 us; the launch traced here: 61.2 us
  waiting for transfers between devices  28.3 us (46%)
  starting transfers between devices  17.4 us (28%)
  Pallas kernels  11.7 us (19%)
  local copies, waits for them, and re-layouts  3.48 us (6%)
    ppermute x19, waiting for transfers between devices, move(): return lax.ppermute(block, axes, [(i, i ^ masks[i & 1]) for i in range(32)])  22.4 us
    ppermute x19, starting transfers between devices, move(): return lax.ppermute(block, axes, [(i, i ^ masks[i & 1]) for i in range(32)])  15.9 us
    pallas_call x1, Pallas kernels, shards(): pl.pallas_call(layer_kernel, out_shape=jax.ShapeDtypeStruct((count, D), B...  9.45 us
    ppermute x1, waiting for transfers between devices, spread_weights(): low = lax.ppermute(init[count - HALO:], axes, ring)  5.35 us
    unnamed x21, local copies, waits for them, and re-layouts  3.46 us
    pallas_call x1, Pallas kernels, shards(): pl.pallas_call(frame_kernel, out_shape=[jax.ShapeDtypeStruct((FRAME, D),...  2.23 us
    ppermute x1, starting transfers between devices, spread_weights(): high = lax.ppermute(init[:HALO], axes, [(j, i) for i, j in ring])  1.51 us
  transfers between devices with their start and end apart: 21, of which 11 were waited for; matrix products, arithmetic and copies ran while one was open for 0% of the time, Pallas kernels for 0%

profile of v5, /device:TPU:0, one launch (start us, length us, event | category | flops | bytes accessed | tf_op | source)
XLA Modules:
  0.0 61.2 jit_solution(6663935781981744725)
XLA Ops:
  0.0 0.0 copy-start
  0.0 2.2 %frames.1 = (bf16[176,512]{1,0:T(8,128)(2,1)}, bf16[176,512]{1,0:T(8,128)(2,1)}) custom-call(s32[1]{0:T(128)} %bitcast.me_ref, bf16[1,75264]{1,0:T(2,128)(2,1)} %refs_0_.1, bf16[96,128]{1,0:T(8,128)(2,1)} %bitcast.19, s32[3,128]{1,0:T(4,128)} %bitcast.20, s32[1,32]{1,0:T(1,128)} %refs_3_.1), custom_call_target="tpu_custom_call" | custom-call | tf_op jit(solution)/shard_map/frames/pallas_call | solution.py:459
  2.2 4.1 %collective-permute-start.9 = (bf16[176,512]{1,0:T(8,128)(2,1)}, bf16[176,512]{1,0:T(8,128)(2,1)S(1)}, u32[]{:S(2)}, u32[]{:S(2)}) collective-permute-start(bf16[176,512]{1,0:T(8,128)(2,1)} %get-tuple-element.8), channel_id=1, source_target_pairs={{0,16},{1,17},{2,18},{3,19},{4,20},{5,21},{6,22},{7,23},{8,24},{9,... | collective-permute-start | bytes 540680 | tf_op jit(solution)/shard_map/ppermute | solution.py:413
  6.4 0.0 copy-start.8
  6.4 1.6 %collective-permute-start.4 = (bf16[176,512]{1,0:T(8,128)(2,1)}, bf16[176,512]{1,0:T(8,128)(2,1)S(1)}, u32[]{:S(2)}, u32[]{:S(2)}) collective-permute-start(bf16[176,512]{1,0:T(8,128)(2,1)} %get-tuple-element.7), channel_id=1, source_target_pairs={{0,8},{1,9},{2,10},{3,11},{4,12},{5,13},{6,14},{7,15},{8,0},{9,1},... | collective-permute-start | bytes 540680 | tf_op jit(solution)/shard_map/ppermute | solution.py:413
  8.0 1.5 %collective-permute-start = (bf16[176,512]{1,0:T(8,128)(2,1)}, bf16[176,512]{1,0:T(8,128)(2,1)S(1)}, u32[]{:S(2)}, u32[]{:S(2)}) collective-permute-start(bf16[176,512]{1,0:T(8,128)(2,1)} %get-tuple-element.7), channel_id=1, source_target_pairs={{0,4},{1,3},{2,6},{3,1},{4,0},{5,7},{6,2},{7,5},{8,12},{9,11},{10,... | collective-permute-start | bytes 540680 | tf_op jit(solution)/shard_map/ppermute | solution.py:413
  9.4 5.7 %collective-permute-done.9 = bf16[176,512]{1,0:T(8,128)(2,1)S(1)} collective-permute-done((bf16[176,512]{1,0:T(8,128)(2,1)}, bf16[176,512]{1,0:T(8,128)(2,1)S(1)}, u32[]{:S(2)}, u32[]{:S(2)}) %collective-permute-start.9) | collective-permute-done | bytes 180256 | tf_op jit(solution)/shard_map/ppermute | solution.py:413
  15.1 1.5 %collective-permute-start.10 = (bf16[176,512]{1,0:T(8,128)(2,1)S(1)}, bf16[176,512]{1,0:T(8,128)(2,1)S(1)}, u32[]{:S(2)}, u32[]{:S(2)}) collective-permute-start(bf16[176,512]{1,0:T(8,128)(2,1)S(1)} %collective-permute-done.9), channel_id=1, source_target_pairs={{0,4},{1,3},{2,6},{3,1},{4,0},{5,7},{6,2},{7,5},{8,12},{9,11},{10,... | collective-permute-start | bytes 540680 | tf_op jit(solution)/shard_map/ppermute | solution.py:413
  16.6 0.0 copy-done
  16.7 0.7 %collective-permute-start.14 = (bf16[176,512]{1,0:T(8,128)(2,1)S(1)}, bf16[176,512]{1,0:T(8,128)(2,1)S(1)}, u32[]{:S(2)}, u32[]{:S(2)}) collective-permute-start(bf16[176,512]{1,0:T(8,128)(2,1)S(1)} %collective-permute-done.9), channel_id=1, source_target_pairs={{0,8},{1,9},{2,10},{3,11},{4,12},{5,13},{6,14},{7,15},{8,0},{9,1},... | collective-permute-start | bytes 540680 | tf_op jit(solution)/shard_map/ppermute | solution.py:413
  17.4 0.0 collective-permute-done
  17.4 1.4 %collective-permute-start.5 = (bf16[176,512]{1,0:T(8,128)(2,1)S(1)}, bf16[176,512]{1,0:T(8,128)(2,1)S(1)}, u32[]{:S(2)}, u32[]{:S(2)}) collective-permute-start(bf16[176,512]{1,0:T(8,128)(2,1)S(1)} %collective-permute-done), channel_id=1, source_target_pairs={{0,8},{1,9},{2,10},{3,11},{4,12},{5,13},{6,14},{7,15},{8,0},{9,1},... | collective-permute-start | bytes 540680 | tf_op jit(solution)/shard_map/ppermute | solution.py:413
  18.8 0.0 copy-done.8
  18.8 0.1 collective-permute-start.2
  18.9 0.0 collective-permute-done.4
  18.9 1.6 %collective-permute-start.1 = (bf16[2,176,512]{2,1,0:T(8,128)(2,1)S(1)}, bf16[2,176,512]{2,1,0:T(8,128)(2,1)S(1)}, u32[]{:S(2)}, u32[]{:S(2)}) collective-permute-start(bf16[2,176,512]{2,1,0:T(8,128)(2,1)S(1)} %pad_maximum_fusion.refs_0_), channel_id=1, source_target_pairs={{0,2},{1,5},{2,0},{3,7},{4,6},{5,1},{6,4},{7,3},{8,10},{9,13},{10,... | collective-permute-start | bytes 1081352 | tf_op jit(solution)/shard_map/ppermute | solution.py:413
  20.5 0.1 collective-permute-done.10
  20.6 0.7 %collective-permute-start.15 = (bf16[176,512]{1,0:T(8,128)(2,1)S(1)}, bf16[176,512]{1,0:T(8,128)(2,1)S(1)}, u32[]{:S(2)}, u32[]{:S(2)}) collective-permute-start(bf16[176,512]{1,0:T(8,128)(2,1)S(1)} %collective-permute-done.10), channel_id=1, source_target_pairs={{0,8},{1,9},{2,10},{3,11},{4,12},{5,13},{6,14},{7,15},{8,0},{9,1},... | collective-permute-start | bytes 540680 | tf_op jit(solution)/shard_map/ppermute | solution.py:413
  21.4 2.8 %collective-permute-done.14 = bf16[176,512]{1,0:T(8,128)(2,1)S(1)} collective-permute-done((bf16[176,512]{1,0:T(8,128)(2,1)S(1)}, bf16[176,512]{1,0:T(8,128)(2,1)S(1)}, u32[]{:S(2)}, u32[]{:S(2)}) %collective-permute-start.14) | collective-permute-done | bytes 180256 | tf_op jit(solution)/shard_map/ppermute | solution.py:413
  24.2 1.5 %collective-permute-start.20 = (bf16[128,512]{1,0:T(8,128)(2,1)S(1)}, bf16[128,512]{1,0:T(8,128)(2,1)S(1)}, u32[]{:S(2)}, u32[]{:S(2)}) collective-permute-start(bf16[128,512]{1,0:T(8,128)(2,1)S(1)} %get-tuple-element.9), channel_id=1, source_target_pairs={{1,0},{2,1},{3,2},{4,3},{5,4},{6,5},{7,6},{8,7},{9,8},{10,9},{11,1... | collective-permute-start | bytes 393224 | tf_op jit(solution)/shard_map/ppermute | solution.py:416
  25.7 2.0 %collective-permute-done.5 = bf16[176,512]{1,0:T(8,128)(2,1)S(1)} collective-permute-done((bf16[176,512]{1,0:T(8,128)(2,1)S(1)}, bf16[176,512]{1,0:T(8,128)(2,1)S(1)}, u32[]{:S(2)}, u32[]{:S(2)}) %collective-permute-start.5) | collective-permute-done | bytes 180256 | tf_op jit(solution)/shard_map/ppermute | solution.py:413
  27.7 0.0 collective-permute-start.19
  27.7 1.9 %collective-permute-done.15 = bf16[176,512]{1,0:T(8,128)(2,1)S(1)} collective-permute-done((bf16[176,512]{1,0:T(8,128)(2,1)S(1)}, bf16[176,512]{1,0:T(8,128)(2,1)S(1)}, u32[]{:S(2)}, u32[]{:S(2)}) %collective-permute-start.15) | collective-permute-done | bytes 180256 | tf_op jit(solution)/shard_map/ppermute | solution.py:413
  29.6 0.0 collective-permute-start.7
  29.6 0.0 copy-start.9
  29.7 0.0 copy-start.5
  29.7 0.0 copy-start.6
  29.7 0.0 copy-start.7
  29.7 0.6 collective-permute-done.20.refs_18_
  30.3 0.2 collective-permute-start.6
  30.4 5.3 %collective-permute-done.19.refs_16_ = bf16[128,512]{1,0:T(8,128)(2,1)S(1)} collective-permute-done((bf16[128,512]{1,0:T(8,128)(2,1)S(1)}, bf16[128,512]{1,0:T(8,128)(2,1)S(1)}, u32[]{:S(2)}, u32[]{:S(2)}) %collective-permute-start.19) | collective-permute-done | bytes 131104 | tf_op jit(solution)/shard_map/ppermute | solution.py:415
  35.8 0.0 copy-start.3
  35.8 0.7 %copy-done.3 = bf16[128,512]{1,0:T(8,128)(2,1)} copy-done((bf16[128,512]{1,0:T(8,128)(2,1)}, bf16[128,512]{1,0:T(8,128)(2,1)S(1)}, u32[]{:S(2)}) %copy-start.3) | copy-done | bytes 131096
  36.4 0.0 collective-permute-start.12
  36.4 0.0 collective-permute-done.2.refs_2_
  36.4 0.0 collective-permute-start.11
  36.4 0.0 collective-permute-done.1.refs_1_
  36.5 2.0 %collective-permute-start.16 = (bf16[2,176,512]{2,1,0:T(8,128)(2,1)S(1)}, bf16[2,176,512]{2,1,0:T(8,128)(2,1)}, u32[]{:S(2)}, u32[]{:S(2)}) collective-permute-start(bf16[2,176,512]{2,1,0:T(8,128)(2,1)S(1)} %pad_maximum_fusion.3.refs_12_), channel_id=1, source_target_pairs={{0,2},{1,5},{2,0},{3,7},{4,6},{5,1},{6,4},{7,3},{8,10},{9,13},{10,... | collective-permute-start | bytes 1081352 | tf_op jit(solution)/shard_map/ppermute | solution.py:413
  38.5 0.0 collective-permute-done.7.refs_6_
  38.5 0.0 collective-permute-start.17
  38.5 0.6 %collective-permute-done.6.refs_5_ = bf16[2,176,512]{2,1,0:T(8,128)(2,1)S(1)} collective-permute-done((bf16[2,176,512]{2,1,0:T(8,128)(2,1)S(1)}, bf16[2,176,512]{2,1,0:T(8,128)(2,1)S(1)}, u32[]{:S(2)}, u32[]{:S(2)}) %collective-permute-start.6) | collective-permute-done | bytes 360480 | tf_op jit(solution)/shard_map/ppermute | solution.py:413
  39.1 0.0 collective-permute-start.3
  39.1 0.0 collective-permute-done.12.refs_10_
  39.1 0.0 copy-start.1
  39.1 0.8 %copy-done.1 = bf16[2,176,512]{2,1,0:T(8,128)(2,1)} copy-done((bf16[2,176,512]{2,1,0:T(8,128)(2,1)}, bf16[2,176,512]{2,1,0:T(8,128)(2,1)S(1)}, u32[]{:S(2)}) %copy-start.1) | copy-done | bytes 360472
  39.9 0.5 collective-permute-start.8
  40.4 3.6 %collective-permute-done.11.refs_9_ = bf16[2,176,512]{2,1,0:T(8,128)(2,1)} collective-permute-done((bf16[2,176,512]{2,1,0:T(8,128)(2,1)S(1)}, bf16[2,176,512]{2,1,0:T(8,128)(2,1)}, u32[]{:S(2)}, u32[]{:S(2)}) %collective-permute-start.11) | collective-permute-done | bytes 360480 | tf_op jit(solution)/shard_map/ppermute | solution.py:413
  44.0 0.0 collective-permute-start.13
  44.0 3.9 %collective-permute-done.16.refs_13_ = bf16[2,176,512]{2,1,0:T(8,128)(2,1)} collective-permute-done((bf16[2,176,512]{2,1,0:T(8,128)(2,1)S(1)}, bf16[2,176,512]{2,1,0:T(8,128)(2,1)}, u32[]{:S(2)}, u32[]{:S(2)}) %collective-permute-start.16) | collective-permute-done | bytes 360480 | tf_op jit(solution)/shard_map/ppermute | solution.py:413
  47.8 0.0 collective-permute-start.18
  47.8 0.0 copy-done.9
  47.8 0.1 copy.10.refs_19_
  48.0 0.0 collective-permute-done.3.refs_3_
  48.0 0.0 collective-permute-done.17.refs_14_
  48.0 0.0 collective-permute-done.8.refs_7_
  48.0 0.0 collective-permute-done.13.refs_11_
  48.0 1.8 %collective-permute-done.18.refs_15_ = bf16[2,176,512]{2,1,0:T(8,128)(2,1)} collective-permute-done((bf16[2,176,512]{2,1,0:T(8,128)(2,1)}, bf16[2,176,512]{2,1,0:T(8,128)(2,1)}, u32[]{:S(2)}, u32[]{:S(2)}) %collective-permute-start.18) | collective-permute-done | bytes 360480 | tf_op jit(solution)/shard_map/ppermute | solution.py:413
  49.9 0.0 copy-done.5
  49.9 0.0 copy-done.6
  49.9 0.0 copy-done.7
  49.9 0.0 copy-start.2
  49.9 1.0 %copy-done.2 = bf16[2,176,512]{2,1,0:T(8,128)(2,1)S(1)} copy-done((bf16[2,176,512]{2,1,0:T(8,128)(2,1)S(1)}, bf16[2,176,512]{2,1,0:T(8,128)(2,1)}, u32[]{:S(2)}) %copy-start.2) | copy-done | bytes 360472
  50.9 0.9 %copy-done.4 = bf16[128,512]{1,0:T(8,128)(2,1)S(1)} copy-done((bf16[128,512]{1,0:T(8,128)(2,1)S(1)}, bf16[128,512]{1,0:T(8,128)(2,1)}, u32[]{:S(2)}) %copy-start.4) | copy-done | bytes 131096
  51.8 9.5 %layer.1 = bf16[320,512]{1,0:T(8,128)(2,1)} custom-call(s32[1]{0:T(128)} %bitcast.me_ref, bf16[2,176,512]{2,1,0:T(8,128)(2,1)S(1)} %pad_maximum_fusion.refs_0_, bf16[2,176,512]{2,1,0:T(8,128)(2,1)S(1)} %collective-permute-done.1.refs_1_, bf16[2,176,512]{2,1,0:T(8,128)(2,1)S(1)} %collective-permute-done.2.refs_2_, ...), custom_call_target="tpu_custom_call" | custom-call | tf_op jit(solution)/shard_map/layer/pallas_call | solution.py:479
  (6 shorter events, 0.2 us)
Async XLA Ops:
  0.0 16.6 %copy-start = (bf16[320,512]{1,0:T(8,128)(2,1)S(1)}, bf16[320,512]{1,0:T(8,128)(2,1)}, u32[]{:S(2)}) copy-start(bf16[320,512]{1,0:T(8,128)(2,1)} %refs_17_.1) | copy-start | bytes 983044
  2.2 12.9 %collective-permute-start.9 = (bf16[176,512]{1,0:T(8,128)(2,1)}, bf16[176,512]{1,0:T(8,128)(2,1)S(1)}, u32[]{:S(2)}, u32[]{:S(2)}) collective-permute-start(bf16[176,512]{1,0:T(8,128)(2,1)} %get-tuple-element.8), channel_id=1, source_target_pairs={{0,16},{1,17},{2,18},{3,19},{4,20},{5,21},{6,22},{7,23},{8,24},{9,... | collective-permute-start | bytes 540680 | tf_op jit(solution)/shard_map/ppermute | solution.py:413
  6.4 12.4 %copy-start.8 = (bf16[176,512]{1,0:T(8,128)(2,1)S(1)}, bf16[176,512]{1,0:T(8,128)(2,1)}, u32[]{:S(2)}) copy-start(bf16[176,512]{1,0:T(8,128)(2,1)} %get-tuple-element.7) | copy-start | bytes 540676
  6.4 12.5 %collective-permute-start.4 = (bf16[176,512]{1,0:T(8,128)(2,1)}, bf16[176,512]{1,0:T(8,128)(2,1)S(1)}, u32[]{:S(2)}, u32[]{:S(2)}) collective-permute-start(bf16[176,512]{1,0:T(8,128)(2,1)} %get-tuple-element.7), channel_id=1, source_target_pairs={{0,8},{1,9},{2,10},{3,11},{4,12},{5,13},{6,14},{7,15},{8,0},{9,1},... | collective-permute-start | bytes 540680 | tf_op jit(solution)/shard_map/ppermute | solution.py:413
  8.0 9.5 %collective-permute-start = (bf16[176,512]{1,0:T(8,128)(2,1)}, bf16[176,512]{1,0:T(8,128)(2,1)S(1)}, u32[]{:S(2)}, u32[]{:S(2)}) collective-permute-start(bf16[176,512]{1,0:T(8,128)(2,1)} %get-tuple-element.7), channel_id=1, source_target_pairs={{0,4},{1,3},{2,6},{3,1},{4,0},{5,7},{6,2},{7,5},{8,12},{9,11},{10,... | collective-permute-start | bytes 540680 | tf_op jit(solution)/shard_map/ppermute | solution.py:413
  15.1 5.5 %collective-permute-start.10 = (bf16[176,512]{1,0:T(8,128)(2,1)S(1)}, bf16[176,512]{1,0:T(8,128)(2,1)S(1)}, u32[]{:S(2)}, u32[]{:S(2)}) collective-permute-start(bf16[176,512]{1,0:T(8,128)(2,1)S(1)} %collective-permute-done.9), channel_id=1, source_target_pairs={{0,4},{1,3},{2,6},{3,1},{4,0},{5,7},{6,2},{7,5},{8,12},{9,11},{10,... | collective-permute-start | bytes 540680 | tf_op jit(solution)/shard_map/ppermute | solution.py:413
  16.7 7.5 %collective-permute-start.14 = (bf16[176,512]{1,0:T(8,128)(2,1)S(1)}, bf16[176,512]{1,0:T(8,128)(2,1)S(1)}, u32[]{:S(2)}, u32[]{:S(2)}) collective-permute-start(bf16[176,512]{1,0:T(8,128)(2,1)S(1)} %collective-permute-done.9), channel_id=1, source_target_pairs={{0,8},{1,9},{2,10},{3,11},{4,12},{5,13},{6,14},{7,15},{8,0},{9,1},... | collective-permute-start | bytes 540680 | tf_op jit(solution)/shard_map/ppermute | solution.py:413
  17.4 10.3 %collective-permute-start.5 = (bf16[176,512]{1,0:T(8,128)(2,1)S(1)}, bf16[176,512]{1,0:T(8,128)(2,1)S(1)}, u32[]{:S(2)}, u32[]{:S(2)}) collective-permute-start(bf16[176,512]{1,0:T(8,128)(2,1)S(1)} %collective-permute-done), channel_id=1, source_target_pairs={{0,8},{1,9},{2,10},{3,11},{4,12},{5,13},{6,14},{7,15},{8,0},{9,1},... | collective-permute-start | bytes 540680 | tf_op jit(solution)/shard_map/ppermute | solution.py:413
  18.8 17.6 %collective-permute-start.2 = (bf16[2,176,512]{2,1,0:T(8,128)(2,1)S(1)}, bf16[2,176,512]{2,1,0:T(8,128)(2,1)S(1)}, u32[]{:S(2)}, u32[]{:S(2)}) collective-permute-start(bf16[2,176,512]{2,1,0:T(8,128)(2,1)S(1)} %pad_maximum_fusion.refs_0_), channel_id=1, source_target_pairs={{0,1},{1,0},{2,3},{3,2},{4,5},{5,4},{6,7},{7,6},{8,9},{9,8},{10,11... | collective-permute-start | bytes 1081352 | tf_op jit(solution)/shard_map/ppermute | solution.py:413
  18.9 17.6 %collective-permute-start.1 = (bf16[2,176,512]{2,1,0:T(8,128)(2,1)S(1)}, bf16[2,176,512]{2,1,0:T(8,128)(2,1)S(1)}, u32[]{:S(2)}, u32[]{:S(2)}) collective-permute-start(bf16[2,176,512]{2,1,0:T(8,128)(2,1)S(1)} %pad_maximum_fusion.refs_0_), channel_id=1, source_target_pairs={{0,2},{1,5},{2,0},{3,7},{4,6},{5,1},{6,4},{7,3},{8,10},{9,13},{10,... | collective-permute-start | bytes 1081352 | tf_op jit(solution)/shard_map/ppermute | solution.py:413
  20.6 9.0 %collective-permute-start.15 = (bf16[176,512]{1,0:T(8,128)(2,1)S(1)}, bf16[176,512]{1,0:T(8,128)(2,1)S(1)}, u32[]{:S(2)}, u32[]{:S(2)}) collective-permute-start(bf16[176,512]{1,0:T(8,128)(2,1)S(1)} %collective-permute-done.10), channel_id=1, source_target_pairs={{0,8},{1,9},{2,10},{3,11},{4,12},{5,13},{6,14},{7,15},{8,0},{9,1},... | collective-permute-start | bytes 540680 | tf_op jit(solution)/shard_map/ppermute | solution.py:413
  24.2 6.1 %collective-permute-start.20 = (bf16[128,512]{1,0:T(8,128)(2,1)S(1)}, bf16[128,512]{1,0:T(8,128)(2,1)S(1)}, u32[]{:S(2)}, u32[]{:S(2)}) collective-permute-start(bf16[128,512]{1,0:T(8,128)(2,1)S(1)} %get-tuple-element.9), channel_id=1, source_target_pairs={{1,0},{2,1},{3,2},{4,3},{5,4},{6,5},{7,6},{8,7},{9,8},{10,9},{11,1... | collective-permute-start | bytes 393224 | tf_op jit(solution)/shard_map/ppermute | solution.py:416
  27.7 8.1 %collective-permute-start.19 = (bf16[128,512]{1,0:T(8,128)(2,1)S(1)}, bf16[128,512]{1,0:T(8,128)(2,1)S(1)}, u32[]{:S(2)}, u32[]{:S(2)}) collective-permute-start(bf16[128,512]{1,0:T(8,128)(2,1)S(1)} %get-tuple-element.10), channel_id=1, source_target_pairs={{0,1},{1,2},{2,3},{3,4},{4,5},{5,6},{6,7},{7,8},{8,9},{9,10},{10,1... | collective-permute-start | bytes 393224 | tf_op jit(solution)/shard_map/ppermute | solution.py:415
  29.6 8.9 %collective-permute-start.7 = (bf16[2,176,512]{2,1,0:T(8,128)(2,1)S(1)}, bf16[2,176,512]{2,1,0:T(8,128)(2,1)S(1)}, u32[]{:S(2)}, u32[]{:S(2)}) collective-permute-start(bf16[2,176,512]{2,1,0:T(8,128)(2,1)S(1)} %pad_maximum_fusion.1.refs_4_), channel_id=1, source_target_pairs={{0,1},{1,0},{2,3},{3,2},{4,5},{5,4},{6,7},{7,6},{8,9},{9,8},{10,11... | collective-permute-start | bytes 1081352 | tf_op jit(solution)/shard_map/ppermute | solution.py:413
  29.6 18.2 %copy-start.9 = (s32[320,6]{0,1:T(8,128)S(1)}, s32[320,6]{0,1:T(8,128)}, u32[]{:S(2)}) copy-start(s32[320,6]{0,1:T(8,128)} %param.13) | copy-start | bytes 23044
  29.7 20.2 %copy-start.5 = (f32[2,512]{1,0:T(2,128)S(1)}, f32[2,512]{1,0:T(2,128)}, u32[]{:S(2)}) copy-start(f32[2,512]{1,0:T(2,128)} %refs_20_.1) | copy-start | bytes 12292
  29.7 20.2 %copy-start.6 = (f32[2,512]{1,0:T(2,128)S(1)}, f32[2,512]{1,0:T(2,128)}, u32[]{:S(2)}) copy-start(f32[2,512]{1,0:T(2,128)} %refs_21_.1) | copy-start | bytes 12292
  29.7 20.2 %copy-start.7 = (f32[2,512]{1,0:T(2,128)S(1)}, f32[2,512]{1,0:T(2,128)}, u32[]{:S(2)}) copy-start(f32[2,512]{1,0:T(2,128)} %refs_22_.1) | copy-start | bytes 12292
  30.3 8.8 %collective-permute-start.6 = (bf16[2,176,512]{2,1,0:T(8,128)(2,1)S(1)}, bf16[2,176,512]{2,1,0:T(8,128)(2,1)S(1)}, u32[]{:S(2)}, u32[]{:S(2)}) collective-permute-start(bf16[2,176,512]{2,1,0:T(8,128)(2,1)S(1)} %pad_maximum_fusion.1.refs_4_), channel_id=1, source_target_pairs={{0,2},{1,5},{2,0},{3,7},{4,6},{5,1},{6,4},{7,3},{8,10},{9,13},{10,... | collective-permute-start | bytes 1081352 | tf_op jit(solution)/shard_map/ppermute | solution.py:413
  35.8 0.7 %copy-start.3 = (bf16[128,512]{1,0:T(8,128)(2,1)}, bf16[128,512]{1,0:T(8,128)(2,1)S(1)}, u32[]{:S(2)}) copy-start(bf16[128,512]{1,0:T(8,128)(2,1)S(1)} %collective-permute-done.19.refs_16_) | copy-start | bytes 393220
  36.4 2.7 %collective-permute-start.12 = (bf16[2,176,512]{2,1,0:T(8,128)(2,1)S(1)}, bf16[2,176,512]{2,1,0:T(8,128)(2,1)S(1)}, u32[]{:S(2)}, u32[]{:S(2)}) collective-permute-start(bf16[2,176,512]{2,1,0:T(8,128)(2,1)S(1)} %pad_maximum_fusion.2.refs_8_), channel_id=1, source_target_pairs={{0,1},{1,0},{2,3},{3,2},{4,5},{5,4},{6,7},{7,6},{8,9},{9,8},{10,11... | collective-permute-start | bytes 1081352 | tf_op jit(solution)/shard_map/ppermute | solution.py:413
  36.4 7.5 %collective-permute-start.11 = (bf16[2,176,512]{2,1,0:T(8,128)(2,1)S(1)}, bf16[2,176,512]{2,1,0:T(8,128)(2,1)}, u32[]{:S(2)}, u32[]{:S(2)}) collective-permute-start(bf16[2,176,512]{2,1,0:T(8,128)(2,1)S(1)} %pad_maximum_fusion.2.refs_8_), channel_id=1, source_target_pairs={{0,2},{1,5},{2,0},{3,7},{4,6},{5,1},{6,4},{7,3},{8,10},{9,13},{10,... | collective-permute-start | bytes 1081352 | tf_op jit(solution)/shard_map/ppermute | solution.py:413
  36.5 11.4 %collective-permute-start.16 = (bf16[2,176,512]{2,1,0:T(8,128)(2,1)S(1)}, bf16[2,176,512]{2,1,0:T(8,128)(2,1)}, u32[]{:S(2)}, u32[]{:S(2)}) collective-permute-start(bf16[2,176,512]{2,1,0:T(8,128)(2,1)S(1)} %pad_maximum_fusion.3.refs_12_), channel_id=1, source_target_pairs={{0,2},{1,5},{2,0},{3,7},{4,6},{5,1},{6,4},{7,3},{8,10},{9,13},{10,... | collective-permute-start | bytes 1081352 | tf_op jit(solution)/shard_map/ppermute | solution.py:413
  38.5 9.5 %collective-permute-start.17 = (bf16[2,176,512]{2,1,0:T(8,128)(2,1)S(1)}, bf16[2,176,512]{2,1,0:T(8,128)(2,1)}, u32[]{:S(2)}, u32[]{:S(2)}) collective-permute-start(bf16[2,176,512]{2,1,0:T(8,128)(2,1)S(1)} %pad_maximum_fusion.3.refs_12_), channel_id=1, source_target_pairs={{0,1},{1,0},{2,3},{3,2},{4,5},{5,4},{6,7},{7,6},{8,9},{9,8},{10,11... | collective-permute-start | bytes 1081352 | tf_op jit(solution)/shard_map/ppermute | solution.py:413
  39.1 8.9 %collective-permute-start.3 = (bf16[2,176,512]{2,1,0:T(8,128)(2,1)S(1)}, bf16[2,176,512]{2,1,0:T(8,128)(2,1)}, u32[]{:S(2)}, u32[]{:S(2)}) collective-permute-start(bf16[2,176,512]{2,1,0:T(8,128)(2,1)S(1)} %collective-permute-done.1.refs_1_), channel_id=1, source_target_pairs={{0,1},{1,0},{2,3},{3,2},{4,5},{5,4},{6,7},{7,6},{8,9},{9,8},{10,11... | collective-permute-start | bytes 1081352 | tf_op jit(solution)/shard_map/ppermute | solution.py:413
  39.1 0.8 %copy-start.1 = (bf16[2,176,512]{2,1,0:T(8,128)(2,1)}, bf16[2,176,512]{2,1,0:T(8,128)(2,1)S(1)}, u32[]{:S(2)}) copy-start(bf16[2,176,512]{2,1,0:T(8,128)(2,1)S(1)} %collective-permute-done.12.refs_10_) | copy-start | bytes 1081348
  39.9 8.1 %collective-permute-start.8 = (bf16[2,176,512]{2,1,0:T(8,128)(2,1)S(1)}, bf16[2,176,512]{2,1,0:T(8,128)(2,1)}, u32[]{:S(2)}, u32[]{:S(2)}) collective-permute-start(bf16[2,176,512]{2,1,0:T(8,128)(2,1)S(1)} %collective-permute-done.6.refs_5_), channel_id=1, source_target_pairs={{0,1},{1,0},{2,3},{3,2},{4,5},{5,4},{6,7},{7,6},{8,9},{9,8},{10,11... | collective-permute-start | bytes 1081352 | tf_op jit(solution)/shard_map/ppermute | solution.py:413
  44.0 4.0 %collective-permute-start.13 = (bf16[2,176,512]{2,1,0:T(8,128)(2,1)}, bf16[2,176,512]{2,1,0:T(8,128)(2,1)}, u32[]{:S(2)}, u32[]{:S(2)}) collective-permute-start(bf16[2,176,512]{2,1,0:T(8,128)(2,1)} %collective-permute-done.11.refs_9_), channel_id=1, source_target_pairs={{0,1},{1,0},{2,3},{3,2},{4,5},{5,4},{6,7},{7,6},{8,9},{9,8},{10,11... | collective-permute-start | bytes 1081352 | tf_op jit(solution)/shard_map/ppermute | solution.py:413
  47.8 2.0 %collective-permute-start.18 = (bf16[2,176,512]{2,1,0:T(8,128)(2,1)}, bf16[2,176,512]{2,1,0:T(8,128)(2,1)}, u32[]{:S(2)}, u32[]{:S(2)}) collective-permute-start(bf16[2,176,512]{2,1,0:T(8,128)(2,1)} %collective-permute-done.16.refs_13_), channel_id=1, source_target_pairs={{0,1},{1,0},{2,3},{3,2},{4,5},{5,4},{6,7},{7,6},{8,9},{9,8},{10,11... | collective-permute-start | bytes 1081352 | tf_op jit(solution)/shard_map/ppermute | solution.py:413
  49.9 1.0 %copy-start.2 = (bf16[2,176,512]{2,1,0:T(8,128)(2,1)S(1)}, bf16[2,176,512]{2,1,0:T(8,128)(2,1)}, u32[]{:S(2)}) copy-start(bf16[2,176,512]{2,1,0:T(8,128)(2,1)} %copy-done.1) | copy-start | bytes 1081348
  50.8 0.9 %copy-start.4 = (bf16[128,512]{1,0:T(8,128)(2,1)S(1)}, bf16[128,512]{1,0:T(8,128)(2,1)}, u32[]{:S(2)}) copy-start(bf16[128,512]{1,0:T(8,128)(2,1)} %copy-done.3) | copy-start | bytes 393220
